TPU v7x, 128 devices: a whole 4x4x4 slice. The times are simulated.
128 devices in a mesh: clip: 8 (over x, core), row: 16 (over y, z).
Axes of the slice: x: 4, y: 4, z: 4, core: 2. Of those that a mesh axis runs over, the one named last changes fastest.
Arguments:
- features: bfloat16 [8, 16, 256, 48, 128], P('clip', None, 'row'), may hold values from -6 to 6
- target: bfloat16 [8, 16, 256, 3, 48], P('clip', None, 'row'), may hold values from -6 to 6
- conv_weight: bfloat16 [3, 3, 3, 128], replicated, may hold values from -0.4375 to 0.4375
- disc_first: bfloat16 [4, 4, 3, 64], replicated, may hold values from -0.875 to 0.875
- disc_second: bfloat16 [4, 4, 64, 128], replicated, may hold values from -0.1875 to 0.1875
- disc_third: bfloat16 [4, 4, 128, 256], replicated, may hold values from -0.125 to 0.125
- disc_fourth: bfloat16 [4, 4, 256, 512], replicated, may hold values from -0.09375 to 0.09375
- disc_head: bfloat16 [4, 4, 512, 1], replicated, may hold values from -0.0625 to 0.0625
Outputs:
- feature_grad: bfloat16 [8, 16, 256, 48, 128], P('clip', None, 'row')
- gan_grad: bfloat16 [8, 16, 256, 3, 48], P('clip', None, 'row')
- weight_grad: float32 [3, 3, 3, 128], replicated
- adaptive: float32 [], replicated
All inputs are finite; a program needn't handle non-finite values.
Results may differ from a plain program's by a relative error of at most 0.015.
Values may be sent and summed in bfloat16 or wider, within the bound.
A program may use at most 64 MiB of HBM per device.

v0:
```python
import jax
import jax.numpy as jnp
from jax import lax
from jax.sharding import PartitionSpec as P

loss_scale = 64.0
epsilon = 0.0001


def padded_2(cells, sides, width):
    for axis, dim in sides:
        count = lax.axis_size(axis)
        ends = count - 1
        head = lax.slice_in_dim(cells, 0, width, axis=dim)
        tail = lax.slice_in_dim(cells, cells.shape[dim] - width, cells.shape[dim], axis=dim)
        cells = jnp.concatenate(
            [
                lax.ppermute(tail, axis, [(i, (i + 1) % count) for i in range(ends)]),
                cells,
                lax.ppermute(head, axis, [((i + 1) % count, i) for i in range(ends)]),
            ],
            axis=dim,
        )
    return cells


def forward_conv(padded, conv_weight):
    return lax.conv_general_dilated(
        padded,
        conv_weight,
        (1, 1),
        "VALID",
        dimension_numbers=("NHWC", "HWOI", "NHCW"),
        preferred_element_type=jnp.float32,
    )


def weight_terms(padded, grads):
    return lax.conv_general_dilated(
        padded,
        grads,
        (1, 1),
        "VALID",
        dimension_numbers=("CHWN", "IHOW", "HWCN"),
        preferred_element_type=jnp.float32,
    )


def input_grad(grad_rows, conv_weight):
    flipped = conv_weight[::-1, ::-1]
    result = lax.conv_general_dilated(
        grad_rows,
        flipped,
        (1, 1),
        ((0, 0), (1, 1)),
        dimension_numbers=("NHCW", "HWIO", "NHWC"),
        preferred_element_type=jnp.float32,
    )
    return result.astype(jnp.bfloat16)


def down_conv(values, weight, stride, layout_spec):
    return lax.conv_general_dilated(
        values,
        weight,
        (stride, stride),
        ((1, 1), (1, 1)),
        dimension_numbers=layout_spec,
        preferred_element_type=jnp.float32,
    )


def back_conv(cotangent, weight, stride, layout_spec):
    return lax.conv_general_dilated(
        cotangent,
        weight[::-1, ::-1],
        (1, 1),
        ((2, 2), (2, 2)),
        lhs_dilation=(stride, stride),
        dimension_numbers=layout_spec,
        preferred_element_type=jnp.float32,
    )


def silu_slope(values):
    logistic = jax.nn.sigmoid(values)
    return logistic * (1.0 + values * (1.0 - logistic))


def disc_gradient(images, layer_one, layer_two, layer_three, layer_four, layer_head):
    plain = ("NHWC", "HWIO", "NHWC")
    pre_one = down_conv(images, layer_one, 2, ("NHCW", "HWIO", "NHWC"))
    act_one = jax.nn.silu(pre_one).astype(jnp.bfloat16)
    pre_two = down_conv(act_one, layer_two, 2, plain)
    act_two = jax.nn.silu(pre_two).astype(jnp.bfloat16)
    pre_three = down_conv(act_two, layer_three, 2, plain)
    act_three = jax.nn.silu(pre_three).astype(jnp.bfloat16)
    pre_four = down_conv(act_three, layer_four, 1, plain)
    act_four = jax.nn.silu(pre_four).astype(jnp.bfloat16)
    back_spec = ("NHWC", "HWOI", "NHWC")
    cot_head = jnp.full(
        (act_four.shape[0], act_four.shape[1] - 1, act_four.shape[2] - 1, 1),
        -loss_scale,
        jnp.bfloat16,
    )
    cot_four = (back_conv(cot_head, layer_head, 1, back_spec) * silu_slope(pre_four)).astype(
        jnp.bfloat16
    )
    cot_three = (back_conv(cot_four, layer_four, 1, back_spec) * silu_slope(pre_three)).astype(
        jnp.bfloat16
    )
    cot_two = (back_conv(cot_three, layer_three, 2, back_spec) * silu_slope(pre_two)).astype(
        jnp.bfloat16
    )
    cot_one = (back_conv(cot_two, layer_two, 2, back_spec) * silu_slope(pre_one)).astype(
        jnp.bfloat16
    )
    return back_conv(cot_one, layer_one, 2, ("NHWC", "HWOI", "NHCW")).astype(jnp.bfloat16)


def per_device(
    features, target, conv_weight, disc_first, disc_second, disc_third, disc_fourth, disc_head
):
    row_count = lax.axis_size("row")
    clip_count = lax.axis_size("clip")
    pixels = clip_count * features.shape[1] * features.shape[2] * row_count * features.shape[3]
    row_block = padded_2(features, (("row", 2),), 1)
    padded = jnp.pad(row_block[0], ((0, 0), (0, 0), (1, 1), (0, 0)))
    wanted = target[0]
    rebuilt = forward_conv(padded, conv_weight)
    rec_grad = loss_scale * (rebuilt - wanted.astype(jnp.float32))
    rec_part = weight_terms(padded, rec_grad.astype(jnp.bfloat16))
    images = rebuilt.astype(jnp.bfloat16)
    frame_total = images.shape[0]
    group_frames = frame_total // row_count
    grouped = images.reshape((row_count, group_frames) + images.shape[1:])
    framed = disc_gradient(
        lax.all_to_all(grouped, "row", split_axis=0, concat_axis=2, tiled=True)[0],
        disc_first,
        disc_second,
        disc_third,
        disc_fourth,
        disc_head,
    )[None]
    returned = lax.all_to_all(framed, "row", split_axis=2, concat_axis=0, tiled=True)
    gan_grad = returned.reshape((frame_total,) + returned.shape[2:])
    gan_part = weight_terms(padded, gan_grad)
    rec_weight, gan_weight = lax.psum((rec_part, gan_part), ("clip", "row"))
    adaptive = jnp.sqrt(jnp.sum(rec_weight * rec_weight)) / (
        jnp.sqrt(jnp.sum(gan_weight * gan_weight)) + epsilon
    )
    weight_grad = (rec_weight + adaptive * gan_weight) / pixels
    combined = (rec_grad + adaptive * gan_grad.astype(jnp.float32)).astype(jnp.bfloat16)
    grad_rows = padded_2(combined[None], (("row", 2),), 1)[0]
    feature_grad = input_grad(grad_rows, conv_weight)[None]
    image_back = gan_grad[None]
    return (feature_grad, image_back, weight_grad, adaptive)


def solution(mesh):
    return jax.shard_map(
        per_device,
        mesh=mesh,
        in_specs=(
            P("clip", None, "row", None, None),
            P("clip", None, "row", None, None),
            P(),
            P(),
            P(),
            P(),
            P(),
            P(),
        ),
        out_specs=(
            P("clip", None, "row", None, None),
            P("clip", None, "row", None, None),
            P(),
            P(),
        ),
        check_vma=False,
    )
```

profile of v0, /device:TPU:1, one launch (start us, length us, event | category | flops | bytes accessed | tf_op | source)
XLA Modules:
  0.0 262.6 jit_solution(3006759044168204883)
XLA Ops:
  0.7 4.0 %copy.137 = bf16[1,16,16,48,128]{4,1,3,2,0:T(8,128)(2,1)S(1)} copy(bf16[1,16,16,48,128]{4,3,2,1,0:T(8,128)(2,1)} %param.8) | data formatting | bytes 6291456 | tf_op args[0]
  4.7 4.4 %collective-permute-start = (bf16[1,16,1,48,128]{4,1,3,2,0:T(8,128)(2,1)S(1)}, bf16[1,16,1,48,128]{4,1,3,2,0:T(8,128)(2,1)S(1)}, u32[]{:S(2)}, u32[]{:S(2)}) collective-permute-start(bf16[1,16,1,48,128]{4,1,3,2,0:T(8,128)(2,1)S(1)} %get-tuple-element.30), channel_id=1, source_target_pairs={{0,1},{1,2},{2,3},{3,4},{4,5},{5,6},{6,7},{7,8},{8,9},{9,10},{10,1... | collective-permute-start | bytes 589832 | tf_op jit(solution)/shard_map/ppermute | solution.py:18
  9.1 1.5 collective-permute-start.1
  10.6 2.0 collective-permute-done
  12.7 4.2 %collective-permute-done.1 = bf16[1,16,1,48,128]{4,1,3,2,0:T(8,128)(2,1)S(1)} collective-permute-done((bf16[1,16,1,48,128]{4,1,3,2,0:T(8,128)(2,1)S(1)}, bf16[1,16,1,48,128]{4,1,3,2,0:T(8,128)(2,1)S(1)}, u32[]{:S(2)}, u32[]{:S(2)}) %collective-permute-start.1) | collective-permute-done | bytes 196640 | tf_op jit(solution)/shard_map/ppermute | solution.py:20
  16.9 36.7 %fusion.80 = f32[16,16,3,48]{0,2,3,1:T(4,128)S(1)} fusion(bf16[3,3,3,128]{3,2,1,0:T(4,128)(2,1)S(1)} %copy-done.16, bf16[1,16,1,48,128]{4,1,3,2,0:T(8,128)(2,1)S(1)} %collective-permute-done.1, bf16[1,16,16,48,128]{4,1,3,2,0:T(8,128)(2,1)S(1)} %copy.137, bf16[1,16,1,48,128]{4,1,3,2,0:T(8,128)(2,1)S(1)} %collective-permute-done), kind=kOutput, calls=%fused_computation.103 | convolution fusion | flops 94371840 | bytes 3693312 | tf_op jit(solution)/shard_map/conv_general_dilated | solution.py:28
  53.9 1.1 copy.142
  55.0 1.8 reshape.63
  56.9 8.2 %all-to-all-start = ((bf16[16,2,1152]{2,1,0:T(2,128)(2,1)}), bf16[16,2,1152]{2,1,0:T(2,128)(2,1)S(1)}, u32[]{:S(2)}, u32[]{:S(2)}) async-start(bf16[16,2,1152]{2,1,0:T(2,128)(2,1)} %reshape.63), calls=%async_computation | async-start | bytes 147456 | tf_op jit(solution)/shard_map/all_to_all | solution.py:138
  65.1 2.4 copy.140
  67.4 4.1 %all-to-all-done = bf16[16,2,1152]{2,1,0:T(2,128)(2,1)S(1)} async-done(((bf16[16,2,1152]{2,1,0:T(2,128)(2,1)}), bf16[16,2,1152]{2,1,0:T(2,128)(2,1)S(1)}, u32[]{:S(2)}, u32[]{:S(2)}) %all-to-all-start) | async-done | bytes 73760 | tf_op jit(solution)/shard_map/all_to_all | solution.py:138
  72.0 3.7 %copy.146 = bf16[256,3,1,8,8]{3,1,4,0,2:T(4,128)(2,1)} copy(bf16[256,3,1,8,8]{0,4,3,1,2:T(8,128)(2,1)S(1)} %pad_bitcast_fusion) | data formatting | bytes 196608 | tf_op jit(solution)/shard_map/conv_general_dilated | solution.py:63
  75.6 1.6 slice.26
  77.3 6.5 %add_multiply_fusion = (f32[128,8,4,64]{3,1,2,0:T(8,128)}, f32[128,8,4,64]{3,1,2,0:T(8,128)S(1)}) fusion(pred[8,4]{0,1:T(4,128)(4,1)S(1)} %copy-done.7, bf16[4,4,3,64]{3,1,2,0:T(4,128)(2,1)S(1)} %copy-done.14, bf16[256,3,1,7,3]{3,1,4,0,2:T(4,128)(2,1)S(1)} %slice.26, bf16[256,3,1,8,8]{3,1,4,0,2:T(4,128)(2,1)} %copy.146), kind=kOutput, calls=%fused_computation.13 | convolution fusion | flops 27570176 | bytes 2233888 | tf_op jit(solution)/shard_map/conv_general_dilated | solution.py:63
  83.8 0.6 select_bitcast_fusion
  84.8 0.8 multiply_convert_fusion.2
  85.6 1.4 fusion.43
  87.2 5.0 %fusion.54 = f32[1,31,5,512]{3,0,2,1:T(1,128)} fusion(bf16[4,4,256,512]{3,2,1,0:T(8,128)(2,1)S(1)} %copy-done.8, bf16[1,32,6,256]{3,1,2,0:T(8,128)(2,1)S(1)} %multiply_convert_fusion.3), kind=kOutput, calls=%fused_computation.71 | convolution fusion | flops 575668224 | bytes 4610048 | tf_op jit(solution)/shard_map/conv_general_dilated | solution.py:63
  92.2 8.7 %fusion.30 = f32[1,32,6,256]{3,0,2,1:T(1,128)S(1)} fusion(bf16[4,4,256,512]{3,2,1,0:T(8,128)(2,1)} %param.14, f32[1,31,5,512]{3,0,2,1:T(1,128)} %fusion.54, bf16[4,4,512,1]{2,1,3,0:T(4,128)(2,1)S(1)} %copy-done.13), kind=kOutput, calls=%fused_computation.40 | convolution fusion | flops 578074112 | bytes 4724736 | tf_op jit(solution)/shard_map/conv_general_dilated | solution.py:74
  100.9 0.7 fusion.53
  101.8 0.8 slice.30
  102.6 3.7 %copy.158 = f32[128,8,4,64]{0,3,2,1:T(8,128)} copy(f32[128,8,4,64]{3,1,2,0:T(8,128)} %get-tuple-element.36) | data formatting | bytes 2097152 | tf_op jit(solution)/shard_map/mul | solution.py:87
  106.3 1.2 slice.31
  107.4 1.6 copy.175
  109.1 3.8 %fusion.28 = bf16[1,64,12,128]{3,0,2,1:T(2,128)(2,1)S(1)} fusion(bf16[4,4,128,256]{3,2,1,0:T(8,128)(2,1)S(1)} %copy-done, f32[64,1,12,128]{3,0,2,1:T(8,128)} %slice.30, bf16[1,32,6,256]{3,1,2,0:T(8,128)(2,1)S(1)} %copy-done.5), kind=kOutput, calls=%fused_computation.37 | convolution fusion | flops 181862400 | bytes 1736704 | tf_op jit(solution)/shard_map/conv_general_dilated | solution.py:74
  112.9 8.9 %multiply_convert_fusion.1 = bf16[1,128,24,64]{3,0,2,1:T(2,128)(2,1)} fusion(f32[1,128,24,64]{3,0,2,1:T(1,128)S(1)} %bitcast.76, bf16[1,64,12,128]{3,0,2,1:T(2,128)(2,1)S(1)} %fusion.28, bf16[4,4,64,128]{3,2,1,0:T(8,128)(2,1)S(1)} %copy-done.10), kind=kOutput, calls=%fused_computation.34 | convolution fusion | flops 191823872 | bytes 1638400 | tf_op jit(solution)/shard_map/conv_general_dilated | solution.py:74
  121.8 3.9 %copy.160 = bf16[1,128,24,64]{1,3,2,0:T(8,128)(2,1)S(1)} copy(bf16[1,128,24,64]{3,0,2,1:T(2,128)(2,1)} %multiply_convert_fusion.1) | data formatting | bytes 786432 | tf_op jit(solution)/shard_map/convert_element_type | solution.py:115
  125.7 2.5 copy.162
  128.3 1.2 slice.32
  129.5 20.3 %fusion.21 = bf16[256,8,8,3]{1,3,2,0:T(4,128)(2,1)} fusion(bf16[128,1,7,2,64]{4,2,3,0,1:T(8,128)(2,1)S(1)} %slice.32, bf16[128,1,8,4,64]{4,2,3,0,1:T(8,128)(2,1)} %copy.162, bf16[4,4,3,64]{3,1,2,0:T(4,128)(2,1)S(1)} %copy-done.15), kind=kOutput, calls=%fused_computation.27 | convolution fusion | flops 27426816 | bytes 858112 | tf_op jit(solution)/shard_map/conv_general_dilated | solution.py:74
  149.8 3.2 %copy.164 = bf16[256,8,8,3]{0,2,3,1:T(8,128)(2,1)S(1)} copy(bf16[256,8,8,3]{1,3,2,0:T(4,128)(2,1)} %fusion.21) | data formatting | bytes 196608 | tf_op jit(solution)/shard_map/conv_general_dilated | solution.py:74
  153.1 0.9 copy.166
  154.0 1.9 reshape.65
  155.9 3.5 %all-to-all-start.1 = ((bf16[16,2,1152]{2,1,0:T(2,128)(2,1)}), bf16[16,2,1152]{2,1,0:T(2,128)(2,1)S(1)}, u32[]{:S(2)}, u32[]{:S(2)}) async-start(bf16[16,2,1152]{2,1,0:T(2,128)(2,1)} %reshape.65), calls=%async_computation.1 | async-start | bytes 147456 | tf_op jit(solution)/shard_map/all_to_all | solution.py:145
  159.4 5.9 %fusion.37 = f32[3,3,3,128]{3,2,1,0:T(4,128)S(1)} fusion(f32[16,16,3,48]{0,2,3,1:T(4,128)S(1)} %fusion.80, bf16[1,16,16,3,48]{1,3,4,2,0:T(4,128)(2,1)S(1)} %copy-done.2, bf16[1,16,1,48,128]{4,1,3,2,0:T(8,128)(2,1)} %copy-done.12, bf16[1,16,16,48,128]{4,1,3,2,0:T(8,128)(2,1)} %copy-done.1, bf16[1,16,1,48,128]{4,1,3,2,0:T(8,128)(2,1)} %copy-done.11), kind=kOutput, calls=%fused_computation.49 | convolution fusion | flops 94519296 | bytes 3773952 | tf_op jit(solution)/shard_map/conv_general_dilated | solution.py:39
  165.9 1.0 reshape.66
  166.9 1.7 copy.167
  168.5 2.3 copy.168
  170.9 5.6 %fusion.79 = f32[3,3,3,128]{3,2,1,0:T(4,128)S(1)} fusion(bf16[16,16,3,48]{0,2,3,1:T(4,128)(2,1)} %copy.168, bf16[1,16,1,48,128]{4,1,3,2,0:T(8,128)(2,1)} %copy-done.12, bf16[1,16,16,48,128]{4,1,3,2,0:T(8,128)(2,1)} %copy-done.1, bf16[1,16,1,48,128]{4,1,3,2,0:T(8,128)(2,1)} %copy-done.11), kind=kOutput, calls=%fused_computation.102 | convolution fusion | flops 94371840 | bytes 3626496 | tf_op jit(solution)/shard_map/conv_general_dilated | solution.py:39
  176.5 67.5 %all-reduce = (f32[3,3,3,128]{3,2,1,0:T(4,128)S(1)}, f32[3,3,3,128]{3,2,1,0:T(4,128)S(1)}) all-reduce(f32[3,3,3,128]{3,2,1,0:T(4,128)S(1)} %fusion.37, f32[3,3,3,128]{3,2,1,0:T(4,128)S(1)} %fusion.79), channel_id=1, replica_groups=mesh['clip'=8,'row'=16] {'clip','row'}, use_global_device_ids=true, to_apply=%region_0.1 | all-reduce | flops 6912 | bytes 55296 | tf_op jit(solution)/shard_map/psum | solution.py:148
  246.0 1.9 fusion.39
  248.0 2.6 %collective-permute-start.2 = (bf16[1,16,1,3,48]{1,3,4,2,0:T(4,128)(2,1)S(1)}, bf16[1,16,1,3,48]{1,3,4,2,0:T(4,128)(2,1)S(1)}, u32[]{:S(2)}, u32[]{:S(2)}) collective-permute-start(bf16[1,16,1,3,48]{1,3,4,2,0:T(4,128)(2,1)S(1)} %get-tuple-element.32), channel_id=1, source_target_pairs={{0,1},{1,2},{2,3},{3,4},{4,5},{5,6},{6,7},{7,8},{8,9},{9,10},{10,1... | collective-permute-start | bytes 13832 | tf_op jit(solution)/shard_map/ppermute | solution.py:18
  250.6 1.3 collective-permute-start.3
  251.9 0.6 add_multiply_fusion.2
  252.6 0.7 copy.172
  253.3 2.2 collective-permute-done.3
  255.5 3.0 %convert_bitcast_fusion = bf16[1,16,16,48,128]{4,1,3,2,0:T(8,128)(2,1)S(1)} fusion(bf16[3,3,3,128]{3,2,1,0:T(4,128)(2,1)S(1)} %copy-done.17, bf16[1,16,1,3,48]{1,3,4,2,0:T(4,128)(2,1)S(1)} %collective-permute-done.3, bf16[1,16,16,3,48]{1,3,4,2,0:T(4,128)(2,1)S(1)} %fusion.39, bf16[1,16,1,3,48]{1,3,4,2,0:T(4,128)(2,1)S(1)} %collective-permute-done.2), kind=kOutput, calls=%fused_computation.8 | convolution fusion | flops 85576704 | bytes 3235584 | tf_op jit(solution)/shard_map/conv_general_dilated | solution.py:51
  258.5 2.5 copy.171
  (55 shorter events, 2.8 us)
Async XLA Ops:
  0.6 85.0 %copy-start = (bf16[4,4,128,256]{3,2,1,0:T(8,128)(2,1)S(1)}, bf16[4,4,128,256]{3,2,1,0:T(8,128)(2,1)}, u32[]{:S(2)}) copy-start(bf16[4,4,128,256]{3,2,1,0:T(8,128)(2,1)} %param.13) | copy-start | bytes 3145732
  0.6 16.2 %copy-start.16 = (bf16[3,3,3,128]{3,2,1,0:T(4,128)(2,1)S(1)}, bf16[3,3,3,128]{3,2,1,0:T(4,128)(2,1)}, u32[]{:S(2)}) copy-start(bf16[3,3,3,128]{3,2,1,0:T(4,128)(2,1)} %param.10) | copy-start | bytes 20740
  4.7 48.8 %copy-start.1 = (bf16[1,16,16,48,128]{4,1,3,2,0:T(8,128)(2,1)}, bf16[1,16,16,48,128]{4,1,3,2,0:T(8,128)(2,1)S(1)}, u32[]{:S(2)}) copy-start(bf16[1,16,16,48,128]{4,1,3,2,0:T(8,128)(2,1)S(1)} %copy.137) | copy-start | bytes 9437188
  4.7 7.9 %collective-permute-start = (bf16[1,16,1,48,128]{4,1,3,2,0:T(8,128)(2,1)S(1)}, bf16[1,16,1,48,128]{4,1,3,2,0:T(8,128)(2,1)S(1)}, u32[]{:S(2)}, u32[]{:S(2)}) collective-permute-start(bf16[1,16,1,48,128]{4,1,3,2,0:T(8,128)(2,1)S(1)} %get-tuple-element.30), channel_id=1, source_target_pairs={{0,1},{1,2},{2,3},{3,4},{4,5},{5,6},{6,7},{7,8},{8,9},{9,10},{10,1... | collective-permute-start | bytes 589832 | tf_op jit(solution)/shard_map/ppermute | solution.py:18
  9.1 7.8 %collective-permute-start.1 = (bf16[1,16,1,48,128]{4,1,3,2,0:T(8,128)(2,1)S(1)}, bf16[1,16,1,48,128]{4,1,3,2,0:T(8,128)(2,1)S(1)}, u32[]{:S(2)}, u32[]{:S(2)}) collective-permute-start(bf16[1,16,1,48,128]{4,1,3,2,0:T(8,128)(2,1)S(1)} %get-tuple-element.31), channel_id=1, source_target_pairs={{1,0},{2,1},{3,2},{4,3},{5,4},{6,5},{7,6},{8,7},{9,8},{10,9},{11,1... | collective-permute-start | bytes 589832 | tf_op jit(solution)/shard_map/ppermute | solution.py:20
  12.7 40.9 %copy-start.11 = (bf16[1,16,1,48,128]{4,1,3,2,0:T(8,128)(2,1)}, bf16[1,16,1,48,128]{4,1,3,2,0:T(8,128)(2,1)S(1)}, u32[]{:S(2)}) copy-start(bf16[1,16,1,48,128]{4,1,3,2,0:T(8,128)(2,1)S(1)} %collective-permute-done) | copy-start | bytes 589828
  16.9 36.7 %copy-start.12 = (bf16[1,16,1,48,128]{4,1,3,2,0:T(8,128)(2,1)}, bf16[1,16,1,48,128]{4,1,3,2,0:T(8,128)(2,1)S(1)}, u32[]{:S(2)}) copy-start(bf16[1,16,1,48,128]{4,1,3,2,0:T(8,128)(2,1)S(1)} %collective-permute-done.1) | copy-start | bytes 589828
  56.9 14.7 %all-to-all-start = ((bf16[16,2,1152]{2,1,0:T(2,128)(2,1)}), bf16[16,2,1152]{2,1,0:T(2,128)(2,1)S(1)}, u32[]{:S(2)}, u32[]{:S(2)}) async-start(bf16[16,2,1152]{2,1,0:T(2,128)(2,1)} %reshape.63), calls=%async_computation | async-start | bytes 147456 | tf_op jit(solution)/shard_map/all_to_all | solution.py:138
  65.0 12.2 %copy-start.7 = (pred[8,4]{0,1:T(4,128)(4,1)S(1)}, pred[8,4]{0,1:T(4,128)(4,1)}, u32[]{:S(2)}) copy-start(pred[8,4]{0,1:T(4,128)(4,1)} %constant.38) | copy-start | bytes 100
  65.1 12.2 %copy-start.14 = (bf16[4,4,3,64]{3,1,2,0:T(4,128)(2,1)S(1)}, bf16[4,4,3,64]{3,1,2,0:T(4,128)(2,1)}, u32[]{:S(2)}) copy-start(bf16[4,4,3,64]{3,1,2,0:T(4,128)(2,1)} %param.11) | copy-start | bytes 18436
  83.8 0.9 copy-start.9
  84.8 2.4 copy-start.8
  87.2 5.0 %copy-start.13 = (bf16[4,4,512,1]{2,1,3,0:T(4,128)(2,1)S(1)}, bf16[4,4,512,1]{2,1,3,0:T(4,128)(2,1)}, u32[]{:S(2)}) copy-start(bf16[4,4,512,1]{2,1,3,0:T(4,128)(2,1)} %param.15) | copy-start | bytes 49156
  102.6 6.5 %copy-start.5 = (bf16[1,32,6,256]{3,1,2,0:T(8,128)(2,1)S(1)}, bf16[1,32,6,256]{3,1,2,0:T(8,128)(2,1)}, u32[]{:S(2)}) copy-start(bf16[1,32,6,256]{3,1,2,0:T(8,128)(2,1)} %fusion.53) | copy-start | bytes 294916
  109.1 3.8 %copy-start.4 = (f32[128,1,24,64]{3,2,0,1:T(8,128)S(1)}, f32[128,1,24,64]{3,2,0,1:T(8,128)}, u32[]{:S(2)}) copy-start(f32[128,1,24,64]{3,2,0,1:T(8,128)} %copy.175) | copy-start | bytes 2359300
  109.1 3.8 %copy-start.10 = (bf16[4,4,64,128]{3,2,1,0:T(8,128)(2,1)S(1)}, bf16[4,4,64,128]{3,2,1,0:T(8,128)(2,1)}, u32[]{:S(2)}) copy-start(bf16[4,4,64,128]{3,2,1,0:T(8,128)(2,1)} %param.12) | copy-start | bytes 786436
  121.8 7.7 %copy-start.15 = (bf16[4,4,3,64]{3,1,2,0:T(4,128)(2,1)S(1)}, bf16[4,4,3,64]{3,1,2,0:T(4,128)(2,1)}, u32[]{:S(2)}) copy-start(bf16[4,4,3,64]{3,1,2,0:T(4,128)(2,1)} %param.11) | copy-start | bytes 18436
  129.5 23.5 %copy-start.6 = (pred[8,8]{1,0:T(8,128)(4,1)S(1)}, pred[8,8]{1,0:T(8,128)(4,1)}, u32[]{:S(2)}) copy-start(pred[8,8]{1,0:T(8,128)(4,1)} %constant.37) | copy-start | bytes 196
  149.8 9.6 %copy-start.2 = (bf16[1,16,16,3,48]{1,3,4,2,0:T(4,128)(2,1)S(1)}, bf16[1,16,16,3,48]{1,3,4,2,0:T(4,128)(2,1)}, u32[]{:S(2)}) copy-start(bf16[1,16,16,3,48]{1,3,4,2,0:T(4,128)(2,1)} %copy.140) | copy-start | bytes 221188
  155.9 10.0 %all-to-all-start.1 = ((bf16[16,2,1152]{2,1,0:T(2,128)(2,1)}), bf16[16,2,1152]{2,1,0:T(2,128)(2,1)S(1)}, u32[]{:S(2)}, u32[]{:S(2)}) async-start(bf16[16,2,1152]{2,1,0:T(2,128)(2,1)} %reshape.65), calls=%async_computation.1 | async-start | bytes 147456 | tf_op jit(solution)/shard_map/all_to_all | solution.py:145
  176.4 79.0 %copy-start.17 = (bf16[3,3,3,128]{3,2,1,0:T(4,128)(2,1)S(1)}, bf16[3,3,3,128]{3,2,1,0:T(4,128)(2,1)}, u32[]{:S(2)}) copy-start(bf16[3,3,3,128]{3,2,1,0:T(4,128)(2,1)} %param.10) | copy-start | bytes 20740
  246.0 6.5 %copy-start.3 = (bf16[1,1,256,3,48]{4,2,3,1,0:T(8,128)(2,1)S(1)}, bf16[1,1,256,3,48]{4,2,3,1,0:T(8,128)(2,1)}, u32[]{:S(2)}) copy-start(bf16[1,1,256,3,48]{4,2,3,1,0:T(8,128)(2,1)} %copy.167) | copy-start | bytes 221188
  248.0 5.3 %collective-permute-start.2 = (bf16[1,16,1,3,48]{1,3,4,2,0:T(4,128)(2,1)S(1)}, bf16[1,16,1,3,48]{1,3,4,2,0:T(4,128)(2,1)S(1)}, u32[]{:S(2)}, u32[]{:S(2)}) collective-permute-start(bf16[1,16,1,3,48]{1,3,4,2,0:T(4,128)(2,1)S(1)} %get-tuple-element.32), channel_id=1, source_target_pairs={{0,1},{1,2},{2,3},{3,4},{4,5},{5,6},{6,7},{7,8},{8,9},{9,10},{10,1... | collective-permute-start | bytes 13832 | tf_op jit(solution)/shard_map/ppermute | solution.py:18
  250.6 4.8 %collective-permute-start.3 = (bf16[1,16,1,3,48]{1,3,4,2,0:T(4,128)(2,1)S(1)}, bf16[1,16,1,3,48]{1,3,4,2,0:T(4,128)(2,1)S(1)}, u32[]{:S(2)}, u32[]{:S(2)}) collective-permute-start(bf16[1,16,1,3,48]{1,3,4,2,0:T(4,128)(2,1)S(1)} %get-tuple-element.33), channel_id=1, source_target_pairs={{1,0},{2,1},{3,2},{4,3},{5,4},{6,5},{7,6},{8,7},{9,8},{10,9},{11,1... | collective-permute-start | bytes 13832 | tf_op jit(solution)/shard_map/ppermute | solution.py:20
where the time goes:
time: 268 us; the launch traced here: 263 us
  matrix products  107 us (40%)
  blocking collectives  67.5 us (25%)
  local copies, waits for them, and re-layouts  44.8 us (17%)
  starting transfers between devices  21.5 us (8%)
  waiting for transfers between devices  13.2 us (5%)
  other arithmetic  4.95 us (2%)
  between operations  4.03 us (2%)
    psum x1, blocking collectives, per_device(): rec_weight, gan_weight = lax.psum((rec_part, gan_part), ('clip', 'row'))  67.5 us
    conv_general_dilated x4, matrix products, back_conv(): lax.conv_general_dilated(cotangent, weight[::-1, ::-1], (1, 1), ((2, 2),...  41.7 us
    conv_general_dilated x1, matrix products, forward_conv(): lax.conv_general_dilated(padded, conv_weight, (1, 1), 'VALID', dimension_...  36.7 us
    unnamed x46, local copies, waits for them, and re-layouts  16.5 us
    conv_general_dilated x4, matrix products, down_conv(): lax.conv_general_dilated(values, weight, (stride, stride), ((1, 1), (1, 1...  13.7 us
    conv_general_dilated x2, matrix products, weight_terms(): lax.conv_general_dilated(padded, grads, (1, 1), 'VALID', dimension_number...  11.5 us
    all_to_all x1, starting transfers between devices, per_device(): lax.all_to_all(grouped, 'row', split_axis=0, concat_axis=2, tiled=True)[0]  8.17 us
    ppermute x2, starting transfers between devices, padded_2(): lax.ppermute(tail, axis, [(i, (i + 1) % count) for i in range(ends)])  7.01 us
  transfers between devices with their start and end apart: 6, of which 5 were waited for; matrix products, arithmetic and copies ran while one was open for 4% of the time, Pallas kernels for 0%

commit v1 on v0

v1 whole, which is shorter than its diff:
```python
import functools

import jax
import jax.numpy as jnp
from jax import lax
from jax.experimental import pallas as pl
from jax.experimental.pallas import tpu as pltpu
from jax.sharding import PartitionSpec as P

MESH = pl.DeviceIdType.MESH
F32 = jnp.float32
BF16 = jnp.bfloat16
SCALE = 64.0
EPS = 0.0001
FR = 16
W = 48
NT = (((1,), (1,)), ((), ()))
TN = (((0,), (0,)), ((), ()))
VM = pltpu.VMEM


def vspec():
    return pl.BlockSpec(memory_space=pltpu.VMEM)


def dot(a, b, dims=(((1,), (0,)), ((), ()))):
    return lax.dot_general(a, b, dims, preferred_element_type=F32)


def iota(shape, dim):
    return lax.broadcasted_iota(jnp.int32, shape, dim)


def rnd(v):
    return v.astype(BF16).astype(F32)


def down1(v):
    return jnp.where(iota(v.shape, 0) >= 1, pltpu.roll(v, 1, 0), 0.0)


def up1(v):
    n = v.shape[0]
    return jnp.where(iota(v.shape, 0) < n - 1, pltpu.roll(v, n - 1, 0), 0.0)


def lroll(v, s):
    s = s % v.shape[1]
    return v if s == 0 else pltpu.roll(v, s, 1)


def forward_body(w_ref, f_ref, r_ref, e_ref, wm, frames):
    i = pl.program_id(0)

    @pl.when(i == 0)
    def _():
        wm[...] = jnp.zeros_like(wm)
        for ab in range(9):
            wm[ab * 8 : ab * 8 + 3, :] = w_ref[ab // 3, ab % 3].astype(F32)

    wmb = wm[...].astype(BF16)
    col = iota((8, 768), 1) % W
    pad = jnp.zeros((8, 128), F32)
    for k in range(frames):
        feats = f_ref[k].reshape(768, 128)
        part = dot(wmb, feats, NT)
        total = None
        for ab in range(9):
            a, b = ab // 3, ab % 3
            g = part[ab * 8 : ab * 8 + 8, :]
            if b == 0:
                g = jnp.where(col <= W - 2, g, 0.0)
            elif b == 2:
                g = jnp.where(col >= 1, g, 0.0)
            g = lroll(jnp.concatenate([g, pad], 1), (2 - a) * W + 1 - b)
            total = g if total is None else total + g
        f = i * frames + k
        for t in range(7):
            tile = total[0:3, t * 128 : t * 128 + 128]
            r_ref[k, 3 * t : 3 * t + 3, :] = tile
            if t in (0, 6):
                for o in range(3):
                    e_ref[0 if t == 0 else 1, o, pl.ds(f, 1), :] = tile[o : o + 1, :]
        r_ref[k, 21:24, :] = jnp.zeros((3, 128), F32)


def forward_partials(conv_weight, features):
    frames = 4
    return pl.pallas_call(
        functools.partial(forward_body, frames=frames),
        grid=(FR // frames,),
        out_shape=(
            jax.ShapeDtypeStruct((FR, 24, 128), F32),
            jax.ShapeDtypeStruct((2, 3, FR, 128), F32),
        ),
        in_specs=[
            pl.BlockSpec((3, 3, 3, 128), lambda i: (0, 0, 0, 0)),
            pl.BlockSpec((frames, 16, W, 128), lambda i: (i, 0, 0, 0)),
        ],
        out_specs=(
            pl.BlockSpec((frames, 24, 128), lambda i: (i, 0, 0)),
            pl.BlockSpec((2, 3, FR, 128), lambda i: (0, 0, 0, 0)),
        ),
        scratch_shapes=[VM((80, 128), F32)],
        name="forward_partials",
    )(conv_weight, features)


def exchange_body(m_ref, e_ref, recv, nb, send, got, esend, egot, own):
    r = lax.axis_index("row")
    barrier = pltpu.get_barrier_semaphore()
    for d in range(1, FR):
        pl.semaphore_signal(
            barrier, inc=1, device_id={"row": lax.rem(r + d, FR)}, device_id_type=MESH
        )
    local = pltpu.make_async_copy(m_ref.at[r], recv.at[r], own)
    local.start()
    pl.semaphore_wait(barrier, FR - 1)
    copies = []
    for d in range(1, FR):
        peer = lax.rem(r + d, FR)
        copies.append(
            pltpu.make_async_remote_copy(
                src_ref=m_ref.at[peer],
                dst_ref=recv.at[r],
                send_sem=send.at[d],
                recv_sem=got.at[d],
                device_id={"row": peer},
                device_id_type=MESH,
            )
        )
    for d, k in ((FR - 1, 0), (1, 1)):
        copies.append(
            pltpu.make_async_remote_copy(
                src_ref=e_ref.at[k],
                dst_ref=nb.at[1 - k],
                send_sem=esend.at[k],
                recv_sem=egot.at[k],
                device_id={"row": lax.rem(r + d, FR)},
                device_id_type=MESH,
            )
        )
    for c in copies:
        c.start()
    local.wait()
    for c in copies:
        c.wait()


def exchange(messages, edges, collective_id):
    return pl.pallas_call(
        exchange_body,
        out_shape=(
            jax.ShapeDtypeStruct((FR, 24, 128), F32),
            jax.ShapeDtypeStruct((2, 3, FR, 128), F32),
        ),
        in_specs=[vspec(), vspec()],
        out_specs=(vspec(), vspec()),
        scratch_shapes=[
            pltpu.SemaphoreType.DMA((FR,)),
            pltpu.SemaphoreType.DMA((FR,)),
            pltpu.SemaphoreType.DMA((2,)),
            pltpu.SemaphoreType.DMA((2,)),
            pltpu.SemaphoreType.DMA,
        ],
        compiler_params=pltpu.CompilerParams(collective_id=collective_id, has_side_effects=True),
        name=f"exchange_{collective_id}",
    )(messages, edges)


def place(tiles, lane, src, dst):
    t, off = src // 128, src % 128
    v = lroll(tiles[t], dst - off)
    if off + W > 128:
        v = jnp.where(lane - dst < 128 - off, v, lroll(tiles[t + 1], dst - off))
    return jnp.where((lane >= dst) & (lane < dst + W), v, 0.0)


def spread(tiles, lane, v, src, dst):
    t, off = dst // 128, dst % 128
    v = lroll(jnp.where((lane >= src) & (lane < src + W), v, 0.0), off - src)
    if off + W > 128:
        tiles[t] = tiles[t] + jnp.where(lane >= off, v, 0.0)
        tiles[t + 1] = tiles[t + 1] + jnp.where(lane < off + W - 128, v, 0.0)
    else:
        tiles[t] = tiles[t] + v


def build_band(w1_ref, t1):
    t1[...] = jnp.zeros_like(t1)
    row = iota((16, 128), 0)
    lane = iota((16, 128), 1)
    for ao in range(12):
        w = w1_ref[ao // 3, ao % 3].astype(F32)
        left = jnp.concatenate([w, jnp.zeros((12, 64), F32)], 0)
        patch = jnp.concatenate([left, pltpu.roll(left, 2, 0)], 1)
        for s in (13, 1, 5, 9):
            rolled = pltpu.roll(patch, s, 0)
            parts = [(0, rolled)]
            if s == 13:
                parts = [(0, jnp.where(row >= 13, rolled, 0.0)), (1, jnp.where(row < 13, rolled, 0.0))]
            for v in range(13):
                start = 4 * v - 3
                if start % 16 != s:
                    continue
                for over, tile in parts:
                    g = start // 16 + over
                    if g < 0 or g > 2:
                        continue
                    if v == 0:
                        tile = jnp.where(lane >= 64, tile, 0.0)
                    if v == 12:
                        tile = jnp.where(lane < 64, tile, 0.0)
                    r0 = ao * 64 + g * 16
                    t1[r0 : r0 + 16, v * 128 : v * 128 + 128] = tile.astype(BF16)


def silu_pair(v):
    s = jax.nn.sigmoid(v)
    return v * s, s * (1.0 + v * (1.0 - s))


def rows16(v, k):
    return v[k * 16 : k * 16 + 16]


def disc_body(
    recv_ref, w1_ref, w2_ref, w3_ref, w4_ref, head_ref, out_ref,
    t1, pp, a1, s1, a2, s2, a3, s3, c4, c3, c2, c1,
):
    lane = iota((16, 128), 1)
    build_band(w1_ref, t1)
    x = []
    for o in range(3):
        tiles = [recv_ref[pl.ds(3 * t + o, 16, stride=24), :] for t in range(7)]
        first, last = tiles[0], tiles[6]
        tiles[0] = first + jnp.where((lane >= W) & (lane < 2 * W), down1(last), 0.0)
        tiles[6] = last + jnp.where(lane < W, up1(first), 0.0)
        x.append([rnd(v) for v in tiles])
    halves = {}
    for m in range(16):
        s = 1 - m % 2
        for o in range(3):
            q = s * 3 + o
            halves[m, q] = place(x[o], lane, W * (m + 1), (q % 2) * 64)
    for i in range(9):
        piece = {}
        for q in range(6):
            m = 2 * i - 1 if q < 3 else 2 * i
            if m == -1:
                piece[q] = down1(halves[15, q])
            elif m == 16:
                piece[q] = up1(halves[0, q])
            else:
                piece[q] = halves[m, q]
        for j in range(3):
            pp[i, :, j * 128 : j * 128 + 128] = (piece[2 * j] + piece[2 * j + 1]).astype(BF16)
    lhs = jnp.concatenate([pp[0:8].reshape(128, 384), pp[1:9].reshape(128, 384)], 1)
    for v in range(13):
        pre = dot(lhs, t1[:, v * 128 : v * 128 + 128])
        act, slope = silu_pair(pre)
        s1[:, v] = slope.reshape(8, 16, 128)
        a1[1:9, v] = act.astype(BF16).reshape(8, 16, 128)
        a1[0, v] = down1(rows16(act, 7)).astype(BF16)
        a1[9, v] = up1(rows16(act, 0)).astype(BF16)
    zero = jnp.zeros((16, 128), BF16)
    for m in range(6):
        a2[m, 0, 0] = zero
        a2[m, 1, 6] = zero
        c2[m, 0] = zero
        c2[m, 13] = zero
    for m in range(4):
        lhs = jnp.concatenate(
            [a1[2 * m + a, k : k + 12].reshape(192, 128) for a in range(4) for k in range(2)], 1
        )
        pre = dot(lhs, w2_ref[...].reshape(1024, 128))
        act, slope = silu_pair(pre)
        s2[m] = slope.reshape(12, 16, 128)
        for c in range(12):
            v = rows16(act, c)
            e, p = (c + 1) % 2, (c + 1) // 2
            a2[m + 1, e, p] = v.astype(BF16)
            if m == 3:
                a2[0, e, p] = down1(v).astype(BF16)
            if m == 0:
                a2[5, e, p] = up1(v).astype(BF16)
    zero = jnp.zeros((16, 256), BF16)
    for k in range(5):
        a3[k, 0] = zero
        a3[k, 7] = zero
    for k in range(4):
        c3[k, 0] = zero
        c3[k, 7] = zero
    acc = None
    for a in range(4):
        lhs = jnp.concatenate(
            [
                jnp.concatenate(
                    [a2[2 * m + a, b % 2, b // 2 : b // 2 + 6].reshape(96, 128) for m in range(2)], 0
                )
                for b in range(4)
            ],
            1,
        )
        term = dot(lhs, w3_ref[a * 4 : a * 4 + 4].reshape(512, 256))
        acc = term if acc is None else acc + term
    act, slope = silu_pair(acc)
    s3[...] = slope.reshape(2, 6, 16, 256)
    for c in range(6):
        v0, v1 = rows16(act, c), rows16(act, 6 + c)
        a3[0, c + 1] = down1(v1).astype(BF16)
        a3[1, c + 1] = v0.astype(BF16)
        a3[2, c + 1] = v1.astype(BF16)
        a3[3, c + 1] = up1(v0).astype(BF16)
        a3[4, c + 1] = up1(v1).astype(BF16)
    acc = None
    for a in range(4):
        lhs = jnp.concatenate(
            [
                jnp.concatenate([a3[m + a, b : b + 5].reshape(80, 256) for m in range(2)], 0)
                for b in range(4)
            ],
            1,
        )
        term = dot(lhs, w4_ref[a * 4 : a * 4 + 4].reshape(1024, 512))
        acc = term if acc is None else acc + term
    _, slope = silu_pair(acc)
    rr = iota((160, 16), 0)
    tap = iota((160, 16), 1)
    y4 = 2 * (rr % 16) + rr // 80
    x4 = (rr % 80) // 16
    py = y4 + 1 - tap // 4
    px = x4 + 1 - tap % 4
    ok = (py >= 0) & (py <= 29) & (px >= 0) & (px <= 3) & (y4 <= 30)
    mask = jnp.where(ok, -SCALE, 0.0).astype(BF16)
    head = jnp.concatenate([head_ref[a].astype(F32) for a in range(4)], 0).astype(BF16)
    cot = dot(mask, head) * slope
    zero = jnp.zeros((16, 512), BF16)
    for k in range(5):
        for c in (0, 1, 7, 8):
            c4[k, c] = zero
    for c in range(5):
        v0, v1 = rows16(cot, c), rows16(cot, 5 + c)
        c4[0, c + 2] = down1(v0).astype(BF16)
        c4[1, c + 2] = down1(v1).astype(BF16)
        c4[2, c + 2] = v0.astype(BF16)
        c4[3, c + 2] = v1.astype(BF16)
        c4[4, c + 2] = up1(v0).astype(BF16)
    acc = None
    for a in range(4):
        for b in range(4):
            lhs = jnp.concatenate(
                [c4[m + 3 - a, 3 - b : 9 - b].reshape(96, 512) for m in range(2)], 0
            )
            term = dot(lhs, w4_ref[a * 4 + b], NT)
            acc = term if acc is None else acc + term
    cot = acc * s3[...].reshape(192, 256)
    for c in range(6):
        v0, v1 = rows16(cot, c), rows16(cot, 6 + c)
        c3[0, c + 1] = down1(v1).astype(BF16)
        c3[1, c + 1] = v0.astype(BF16)
        c3[2, c + 1] = v1.astype(BF16)
        c3[3, c + 1] = up1(v0).astype(BF16)
    for first in (0, 1):
        rows = (1, 3) if first == 0 else (0, 2)
        for e in range(2):
            p0 = 1 - e
            acc = None
            for a in (first, first + 2):
                for b in (e, e + 2):
                    lo = p0 + 1 - b // 2
                    lhs = jnp.concatenate(
                        [c3[(m + 1 - a) // 2 + 1, lo : lo + 6].reshape(96, 256) for m in rows], 0
                    )
                    term = dot(lhs, w3_ref[a * 4 + b], NT)
                    acc = term if acc is None else acc + term
            for n, m in enumerate(rows):
                for p in range(6):
                    c = 2 * (p0 + p) + e - 1
                    v = rows16(acc, n * 6 + p) * s2[m, c]
                    c2[m + 1, c + 1] = v.astype(BF16)
                    if m == 3:
                        c2[0, c + 1] = down1(v).astype(BF16)
                    if m == 0:
                        c2[5, c + 1] = up1(v).astype(BF16)
    for first in (0, 1):
        rhs = jnp.concatenate(
            [w2_ref[a, h * 128 : h * 128 + 128] for a in (first, first + 2) for h in range(2)], 1
        )
        for i in range(4):
            m = 2 * i + 1 - first
            lhs = jnp.concatenate(
                [
                    c2[(m + 1 - a) // 2 + 1, 1 - h : 14 - h].reshape(208, 128)
                    for a in (first, first + 2)
                    for h in range(2)
                ],
                1,
            )
            cot = dot(lhs, rhs, NT) * s1[m].reshape(208, 128)
            for v in range(13):
                c1[m * 16 : m * 16 + 16, v * 128 : v * 128 + 128] = rows16(cot, v).astype(BF16)
    grad = dot(c1[...], t1[...], NT)
    halves = {}
    for j in range(3):
        ps = []
        for i in range(9):
            v = None
            if i <= 7:
                v = grad[i * 16 : i * 16 + 16, j * 128 : j * 128 + 128]
            if i >= 1:
                u = grad[(i - 1) * 16 : i * 16, 384 + j * 128 : 512 + j * 128]
                v = u if v is None else v + u
            ps.append(v)
        for h in range(2):
            q = 2 * j + h
            for i in range(9):
                m = 2 * i - 1 if q < 3 else 2 * i
                if 0 <= m <= 15:
                    v = ps[i]
                    if m == 15:
                        v = v + up1(ps[0])
                    if m == 0:
                        v = v + down1(ps[8])
                    halves[m, q] = rnd(v)
    for o in range(3):
        tiles = [jnp.zeros((16, 128), F32) for _ in range(7)]
        for m in range(16):
            q = (1 - m % 2) * 3 + o
            spread(tiles, lane, halves[m, q], (q % 2) * 64, W * (m + 1))
        first, last = tiles[0], tiles[6]
        tiles[0] = first + jnp.where(lane < W, down1(last), 0.0)
        tiles[6] = last + jnp.where((lane >= W) & (lane < 2 * W), up1(first), 0.0)
        for t in range(7):
            out_ref[pl.ds(3 * t + o, 16, stride=24), :] = tiles[t]
    for k in range(21, 24):
        out_ref[pl.ds(k, 16, stride=24), :] = jnp.zeros((16, 128), F32)


def disc(recv, w1, w2, w3, w4, head):
    return pl.pallas_call(
        disc_body,
        out_shape=jax.ShapeDtypeStruct((FR * 24, 128), F32),
        in_specs=[vspec()] * 6,
        out_specs=vspec(),
        scratch_shapes=[
            VM((768, 1664), BF16),
            VM((9, 16, 384), BF16),
            VM((10, 13, 16, 128), BF16),
            VM((8, 13, 16, 128), F32),
            VM((6, 2, 7, 16, 128), BF16),
            VM((4, 12, 16, 128), F32),
            VM((5, 8, 16, 256), BF16),
            VM((2, 6, 16, 256), F32),
            VM((5, 9, 16, 512), BF16),
            VM((4, 8, 16, 256), BF16),
            VM((6, 14, 16, 128), BF16),
            VM((128, 1664), BF16),
        ],
        name="disc",
    )(recv, w1, w2, w3, w4, head)


def rec_body(r_ref, nb_ref, t_ref, out_ref, e_ref, wide):
    r = lax.axis_index("row")
    lane = iota((16, 128), 1)
    wide[:, 0:W] = t_ref[...].astype(F32)
    for o in range(3):
        want = [jnp.zeros((16, 128), F32) for _ in range(7)]
        for y in range(16):
            v = wide[pl.ds(o * 16 + y, 16, stride=48), :]
            spread(want, lane, v, 0, W * (y + 1))
        for t in range(7):
            v = r_ref[pl.ds(3 * t + o, 16, stride=24), :]
            if t == 0:
                v = v + jnp.where((lane >= W) & (lane < 2 * W) & (r > 0), nb_ref[0, o], 0.0)
            if t == 6:
                v = v + jnp.where((lane < W) & (r < FR - 1), nb_ref[1, o], 0.0)
            v = SCALE * (v - want[t])
            if t == 0:
                v = jnp.where(lane >= W, v, 0.0)
            if t == 6:
                v = jnp.where(lane < W, v, 0.0)
            out_ref[t, o] = v
            if t in (0, 6):
                e_ref[t // 6, o] = v


def rec_gradient(r, nb, target):
    return pl.pallas_call(
        rec_body,
        out_shape=(
            jax.ShapeDtypeStruct((7, 3, FR, 128), F32),
            jax.ShapeDtypeStruct((2, 3, FR, 128), F32),
        ),
        in_specs=[vspec()] * 3,
        out_specs=(vspec(), vspec()),
        scratch_shapes=[VM((768, 128), F32)],
        name="rec_gradient",
    )(r, nb, target)


def weights_body(rec_ref, ne_ref, gan_ref, f_ref, acc_ref, g_ref, back_ref, gg, wide, frames):
    i = pl.program_id(0)
    lane = iota((16, 128), 1)

    @pl.when(i == 0)
    def _():
        r = lax.axis_index("row")
        acc_ref[...] = jnp.zeros_like(acc_ref)
        zero = jnp.zeros((16, 128), F32)
        for o in range(3):
            tiles = []
            for t in range(7):
                v = rec_ref[t, o]
                if t == 0:
                    v = v + jnp.where((lane < W) & (r > 0), ne_ref[0, o], 0.0)
                if t == 6:
                    v = v + jnp.where((lane >= W) & (lane < 2 * W) & (r < FR - 1), ne_ref[1, o], 0.0)
                gg[pl.ds(t * 8 + o, 16, stride=56), :] = v
                v = gan_ref[pl.ds(3 * t + o, 16, stride=24), :]
                gg[pl.ds(t * 8 + 4 + o, 16, stride=56), :] = v
                tiles.append(v)
            for y in range(16):
                wide[pl.ds(o * 16 + y, 16, stride=48), :] = place(tiles, lane, W * (y + 1), 0)
        for t in range(7):
            gg[pl.ds(t * 8 + 3, 16, stride=56), :] = zero
            gg[pl.ds(t * 8 + 7, 16, stride=56), :] = zero
        back_ref[...] = wide[:, 0:W].astype(BF16)

    col = iota((8, 768), 1) % W
    for k in range(frames):
        f = i * frames + k
        g = jnp.concatenate([gg[pl.ds(f * 56 + t * 8, 8), :] for t in range(7)], 1)
        rows = []
        for ab in range(9):
            a, b = ab // 3, ab % 3
            v = lroll(g, -((2 - a) * W + 1 - b))[:, 0:768]
            if b == 0:
                v = jnp.where(col <= W - 2, v, 0.0)
            elif b == 2:
                v = jnp.where(col >= 1, v, 0.0)
            rows.append(v)
        rows.append(jnp.zeros((8, 768), F32))
        gt = jnp.concatenate(rows, 0).astype(BF16)
        g_ref[k] = gt
        acc_ref[...] += dot(gt, f_ref[k].reshape(768, 128))


def weight_gradients(rec, ne, gan, features):
    frames = 4
    full = lambda shape: pl.BlockSpec(shape, lambda i: (0,) * len(shape))
    return pl.pallas_call(
        functools.partial(weights_body, frames=frames),
        grid=(FR // frames,),
        out_shape=(
            jax.ShapeDtypeStruct((80, 128), F32),
            jax.ShapeDtypeStruct((FR, 80, 768), BF16),
            jax.ShapeDtypeStruct((768, W), BF16),
        ),
        in_specs=[
            full((7, 3, FR, 128)),
            full((2, 3, FR, 128)),
            full((FR * 24, 128)),
            pl.BlockSpec((frames, 16, W, 128), lambda i: (i, 0, 0, 0)),
        ],
        out_specs=(
            full((80, 128)),
            pl.BlockSpec((frames, 80, 768), lambda i: (i, 0, 0)),
            full((768, W)),
        ),
        scratch_shapes=[VM((FR * 56, 128), F32), VM((768, 128), F32)],
        name="weight_gradients",
    )(rec, ne, gan, features)


def total_body(x_ref, out_ref, pair, bx, by, bz, psend, pgot, send, got, fsend, fgot):
    clip = lax.axis_index("clip")
    row = lax.axis_index("row")
    core, x = lax.rem(clip, 2), clip // 2
    y, z = row // 4, lax.rem(row, 4)

    def at(xx, yy, zz, cc):
        return (xx * 2 + cc, yy * 4 + zz)

    partner = at(x, y, z, 1 - core)
    peers = []
    for d in range(1, 4):
        peers.append(at(lax.rem(x + d, 4), y, z, core))
    for d in range(1, 4):
        peers.append(at(x, lax.rem(y + d, 4), z, core))
    for d in range(1, 4):
        peers.append(at(x, y, lax.rem(z + d, 4), core))
    barrier = pltpu.get_barrier_semaphore()
    for p in [partner] + peers:
        pl.semaphore_signal(barrier, inc=1, device_id=p, device_id_type=MESH)
    pl.semaphore_wait(barrier, 10)

    mine = pl.ds(pl.multiple_of(core * 40, 8), 40)
    other = pl.ds(pl.multiple_of((1 - core) * 40, 8), 40)
    copy = pltpu.make_async_remote_copy(
        src_ref=x_ref.at[other], dst_ref=pair, send_sem=psend, recv_sem=pgot,
        device_id=partner, device_id_type=MESH,
    )
    copy.start()
    copy.wait()
    value = x_ref[mine, :] + pair[...]
    for axis, (buf, me) in enumerate(((bx, x), (by, y), (bz, z))):
        buf[me] = value
        copies = []
        for d in range(3):
            k = axis * 3 + d
            copies.append(
                pltpu.make_async_remote_copy(
                    src_ref=buf.at[me], dst_ref=buf.at[me], send_sem=send.at[k],
                    recv_sem=got.at[k], device_id=peers[k], device_id_type=MESH,
                )
            )
        for c in copies:
            c.start()
        for c in copies:
            c.wait()
        value = (buf[0] + buf[1]) + (buf[2] + buf[3])
    out_ref[mine, :] = value
    copy = pltpu.make_async_remote_copy(
        src_ref=out_ref.at[mine], dst_ref=out_ref.at[mine], send_sem=fsend, recv_sem=fgot,
        device_id=partner, device_id_type=MESH,
    )
    copy.start()
    copy.wait()


def total(acc):
    half = (40, 128)
    return pl.pallas_call(
        total_body,
        out_shape=jax.ShapeDtypeStruct((80, 128), F32),
        in_specs=[vspec()],
        out_specs=vspec(),
        scratch_shapes=[
            VM(half, F32),
            VM((4,) + half, F32),
            VM((4,) + half, F32),
            VM((4,) + half, F32),
            pltpu.SemaphoreType.DMA,
            pltpu.SemaphoreType.DMA,
            pltpu.SemaphoreType.DMA((9,)),
            pltpu.SemaphoreType.DMA((9,)),
            pltpu.SemaphoreType.DMA,
            pltpu.SemaphoreType.DMA,
        ],
        compiler_params=pltpu.CompilerParams(collective_id=2, has_side_effects=True),
        name="total",
    )(acc)


def final_body(s_ref, w_ref, g_ref, out_ref, wg_ref, ad_ref, wf, frames, pixels):
    i = pl.program_id(0)

    @pl.when(i == 0)
    def _():
        s = s_ref[...]
        kind = iota((80, 128), 0) % 8
        sq = s * s
        rec = jnp.sum(jnp.where(kind < 3, sq, 0.0), keepdims=True)
        gan = jnp.sum(jnp.where((kind >= 4) & (kind < 7), sq, 0.0), keepdims=True)
        adaptive = jnp.sqrt(rec) / (jnp.sqrt(gan) + EPS)
        ad_ref[...] = jnp.broadcast_to(adaptive, (8, 128))
        wf[...] = jnp.zeros_like(wf)
        for ab in range(9):
            k = ab * 8
            wf[k : k + 3, :] = w_ref[ab // 3, ab % 3].astype(F32)
            wf[k + 4 : k + 7, :] = adaptive * w_ref[ab // 3, ab % 3].astype(F32)
            wg_ref[ab // 3, ab % 3] = (s[k : k + 3] + adaptive * s[k + 4 : k + 7]) / pixels

    wfb = wf[...].astype(BF16)
    for k in range(frames):
        out_ref[k] = dot(g_ref[k], wfb, TN).astype(BF16).reshape(16, W, 128)


def final(sums, conv_weight, g, pixels):
    frames = 4
    full = lambda shape: pl.BlockSpec(shape, lambda i: (0,) * len(shape))
    return pl.pallas_call(
        functools.partial(final_body, frames=frames, pixels=pixels),
        grid=(FR // frames,),
        out_shape=(
            jax.ShapeDtypeStruct((FR, 16, W, 128), BF16),
            jax.ShapeDtypeStruct((3, 3, 3, 128), F32),
            jax.ShapeDtypeStruct((8, 128), F32),
        ),
        in_specs=[
            full((80, 128)),
            full((3, 3, 3, 128)),
            pl.BlockSpec((frames, 80, 768), lambda i: (i, 0, 0)),
        ],
        out_specs=(
            pl.BlockSpec((frames, 16, W, 128), lambda i: (i, 0, 0, 0)),
            full((3, 3, 3, 128)),
            full((8, 128)),
        ),
        scratch_shapes=[VM((80, 128), F32)],
        name="final",
    )(sums, conv_weight, g)


def per_device(
    features, target, conv_weight, disc_first, disc_second, disc_third, disc_fourth, disc_head
):
    feats = features[0]
    wanted = jnp.transpose(target[0], (0, 2, 1, 3)).reshape(768, W)
    w1 = jnp.transpose(disc_first, (0, 2, 1, 3))
    w2 = disc_second.reshape(4, 256, 128)
    w3 = disc_third.reshape(16, 128, 256)
    w4 = disc_fourth.reshape(16, 256, 512)
    head = disc_head.reshape(4, 4, 512)
    pixels = float(8 * FR * 256 * W)
    parts, edges = forward_partials(conv_weight, feats)
    recv, nb = exchange(parts, edges, 0)
    rec, rec_edges = rec_gradient(parts.reshape(FR * 24, 128), nb, wanted)
    messages = disc(recv.reshape(FR * 24, 128), w1, w2, w3, w4, head)
    gan, ne = exchange(messages.reshape(FR, 24, 128), rec_edges, 1)
    acc, g, back = weight_gradients(rec, ne, gan.reshape(FR * 24, 128), feats)
    sums = total(acc)
    feature_grad, weight_grad, adaptive = final(sums, conv_weight, g, pixels)
    image_back = jnp.transpose(back.reshape(FR, 3, 16, W), (0, 2, 1, 3))
    return (feature_grad[None], image_back[None], weight_grad, adaptive[0, 0])


def solution(mesh):
    return jax.shard_map(
        per_device,
        mesh=mesh,
        in_specs=(
            P("clip", None, "row", None, None),
            P("clip", None, "row", None, None),
            P(),
            P(),
            P(),
            P(),
            P(),
            P(),
        ),
        out_specs=(
            P("clip", None, "row", None, None),
            P("clip", None, "row", None, None),
            P(),
            P(),
        ),
        check_vma=False,
    )
```

time: 268 us -> 73.6 us (0.27); the launches traced: 263 us -> 73.1 us
  matrix products: 107 us -> 0 us
  Pallas kernels: 0 us -> 71.3 us
  blocking collectives: 67.5 us -> 0 us
  local copies, waits for them, and re-layouts: 44.8 us -> 1.18 us
  starting transfers between devices: 21.5 us -> 0 us
  waiting for transfers between devices: 13.2 us -> 0 us
  other arithmetic: 4.95 us -> 0 us
  between operations: 4.03 us -> 0.66 us
    conv_general_dilated x12 -> x0, matrix products: 107 us -> none  [the longest x4 41.7 us: back_conv(): lax.conv_general_dilated(cotangent, weight[::-1, ::-1], (1, 1), ((2, 2),...]
    pallas_call x0 -> x8, Pallas kernels: none -> 71.3 us  [the longest x2 22.9 us: exchange(): pl.pallas_call(exchange_body, out_shape=(jax.ShapeDtypeStruct((FR, 24, 12...]
    psum x1 -> x0, blocking collectives: 67.5 us -> none  [per_device(): rec_weight, gan_weight = lax.psum((rec_part, gan_part), ('clip', 'row'))]
    unnamed x46 -> x0, local copies, waits for them, and re-layouts: 16.5 us -> none
    conv_general_dilated x6 -> x0, local copies, waits for them, and re-layouts: 12.3 us -> none  [the longest x3 6.92 us: back_conv(): lax.conv_general_dilated(cotangent, weight[::-1, ::-1], (1, 1), ((2, 2),...]
    all_to_all x2 -> x0, starting transfers between devices: 11.7 us -> none  [the longest x1 8.17 us: per_device(): lax.all_to_all(grouped, 'row', split_axis=0, concat_axis=2, tiled=True)[0]]
    ppermute x4 -> x0, starting transfers between devices: 9.81 us -> none  [the longest x2 7.01 us: padded_2(): lax.ppermute(tail, axis, [(i, (i + 1) % count) for i in range(ends)])]
    ppermute x4 -> x0, waiting for transfers between devices: 8.46 us -> none  [the longest x2 6.41 us: padded_2(): lax.ppermute(head, axis, [((i + 1) % count, i) for i in range(ends)])]
  transfers between devices with their start and end apart: 6 -> 0, of which waited for: 5 -> 0; matrix products, arithmetic and copies ran while one was open for 4% -> 0% of each run, Pallas kernels for 0% -> 0%
where the time goes in v1:
time: 73.6 us; the launch traced here: 73.1 us
  Pallas kernels  71.3 us (97%)
  local copies, waits for them, and re-layouts  1.18 us (2%)
    pallas_call x2, Pallas kernels, exchange(): pl.pallas_call(exchange_body, out_shape=(jax.ShapeDtypeStruct((FR, 24, 12...  22.9 us
    pallas_call x1, Pallas kernels, total(): pl.pallas_call(total_body, out_shape=jax.ShapeDtypeStruct((80, 128), F32)...  20.5 us
    pallas_call x1, Pallas kernels, disc(): pl.pallas_call(disc_body, out_shape=jax.ShapeDtypeStruct((FR * 24, 128),...  11.6 us
    pallas_call x1, Pallas kernels, weight_gradients(): pl.pallas_call(functools.partial(weights_body, frames=frames), grid=(FR /...  4.93 us
    pallas_call x1, Pallas kernels, final(): pl.pallas_call(functools.partial(final_body, frames=frames, pixels=pixels...  4.85 us
    pallas_call x1, Pallas kernels, forward_partials(): pl.pallas_call(functools.partial(forward_body, frames=frames), grid=(FR /...  4.55 us
    pallas_call x1, Pallas kernels, rec_gradient(): pl.pallas_call(rec_body, out_shape=(jax.ShapeDtypeStruct((7, 3, FR, 128),...  1.95 us

profile of v1, /device:TPU:1, one launch (start us, length us, event | category | flops | bytes accessed | tf_op | source)
XLA Modules:
  0.0 73.1 jit_solution(7970855487623628274)
XLA Ops:
  0.6 4.6 %forward_partials.1 = (f32[16,24,128]{2,1,0:T(8,128)}, f32[2,3,16,128]{3,2,1,0:T(8,128)}) custom-call(bf16[3,3,3,128]{3,2,1,0:T(4,128)(2,1)} %w_ref.3, bf16[16,16,48,128]{3,2,1,0:T(8,128)(2,1)} %bitcast.22), custom_call_target="tpu_custom_call" | custom-call | tf_op jit(solution)/shard_map/forward_partials/pallas_call | solution.py:89
  5.2 12.7 %exchange_0.1 = (f32[16,24,128]{2,1,0:T(8,128)}, f32[2,3,16,128]{3,2,1,0:T(8,128)}) custom-call(f32[16,24,128]{2,1,0:T(8,128)} %get-tuple-element.18.m_ref, f32[2,3,16,128]{3,2,1,0:T(8,128)} %get-tuple-element.19.e_ref), custom_call_target="tpu_custom_call" | custom-call | tf_op jit(solution)/shard_map/exchange_0/pallas_call | solution.py:151
  17.9 1.9 %rec_gradient.1 = (f32[7,3,16,128]{3,2,1,0:T(8,128)}, f32[2,3,16,128]{3,2,1,0:T(8,128)}) custom-call(f32[384,128]{1,0:T(8,128)} %bitcast.27, f32[2,3,16,128]{3,2,1,0:T(8,128)} %get-tuple-element.20.nb_ref, bf16[768,48]{1,0:T(8,128)(2,1)} %bitcast.30), custom_call_target="tpu_custom_call" | custom-call | tf_op jit(solution)/shard_map/rec_gradient/pallas_call | solution.py:490
  19.9 11.6 %disc.1 = f32[384,128]{1,0:T(8,128)} custom-call(f32[384,128]{1,0:T(8,128)} %bitcast.29, bf16[4,3,4,64]{3,2,1,0:T(4,128)(2,1)} %bitcast.33, bf16[4,256,128]{2,1,0:T(8,128)(2,1)} %bitcast.28, bf16[16,128,256]{2,1,0:T(8,128)(2,1)} %bitcast.25, bf16[16,256,512]{2,1,0:T(8,128)(2,1)} %bitcast.24, bf16[4,4,512]{2,1,0:T(4,128)(2,1)} %bitcast.32), custom_call_target="tpu_custom_call" | custom-call | tf_op jit(solution)/shard_map/disc/pallas_call | solution.py:441
  31.5 10.2 %exchange_1.1 = (f32[16,24,128]{2,1,0:T(8,128)}, f32[2,3,16,128]{3,2,1,0:T(8,128)}) custom-call(f32[16,24,128]{2,1,0:T(8,128)} %bitcast.26, f32[2,3,16,128]{3,2,1,0:T(8,128)} %get-tuple-element.23.e_ref), custom_call_target="tpu_custom_call" | custom-call | tf_op jit(solution)/shard_map/exchange_1/pallas_call | solution.py:151
  41.7 4.9 %weight_gradients.1 = (f32[80,128]{1,0:T(8,128)}, bf16[16,80,768]{2,1,0:T(8,128)(2,1)}, bf16[768,48]{1,0:T(8,128)(2,1)}) custom-call(f32[7,3,16,128]{3,2,1,0:T(8,128)} %get-tuple-element.21.rec_ref, f32[2,3,16,128]{3,2,1,0:T(8,128)} %get-tuple-element.24.ne_ref, f32[384,128]{1,0:T(8,128)} %bitcast.31, bf16[16,16,48,128]{3,2,1,0:T(8,128)(2,1)} %bitcast.23), custom_call_target="tpu_custom_call" | custom-call | tf_op jit(solution)/shard_map/weight_gradients/pallas_call | solution.py:553
  46.6 20.5 %total.1.s_ref = f32[80,128]{1,0:T(8,128)} custom-call(f32[80,128]{1,0:T(8,128)} %get-tuple-element.26.x_ref), custom_call_target="tpu_custom_call" | custom-call | tf_op jit(solution)/shard_map/total/pallas_call | solution.py:635
  67.1 4.8 %final.1 = (bf16[16,16,48,128]{3,2,1,0:T(8,128)(2,1)}, f32[3,3,3,128]{3,2,1,0:T(4,128)}, f32[8,128]{1,0:T(8,128)}) custom-call(f32[80,128]{1,0:T(8,128)} %total.1.s_ref, bf16[3,3,3,128]{3,2,1,0:T(4,128)(2,1)} %w_ref.3, bf16[16,80,768]{2,1,0:T(8,128)(2,1)} %get-tuple-element.27.g_ref), custom_call_target="tpu_custom_call" | custom-call | tf_op jit(solution)/shard_map/final/pallas_call | solution.py:684
  71.9 1.2 %slice.3 = f32[1,1]{1,0:T(1,128)} slice(f32[8,128]{1,0:T(8,128)} %get-tuple-element.31), slice={[0:1], [0:1]} | slice | bytes 8 | tf_op jit(solution)/shard_map/slice | solution.py:727

commit v2 on v1

v2 whole, which is shorter than its diff:
```python
import functools

import jax
import jax.numpy as jnp
from jax import lax
from jax.experimental import pallas as pl
from jax.experimental.pallas import tpu as pltpu
from jax.sharding import PartitionSpec as P

MESH = pl.DeviceIdType.MESH
F32 = jnp.float32
BF16 = jnp.bfloat16
SCALE = 64.0
EPS = 0.0001
FR = 16
W = 48
NT = (((1,), (1,)), ((), ()))
TN = (((0,), (0,)), ((), ()))
VM = pltpu.VMEM


def vspec():
    return pl.BlockSpec(memory_space=pltpu.VMEM)


def dot(a, b, dims=(((1,), (0,)), ((), ()))):
    return lax.dot_general(a, b, dims, preferred_element_type=F32)


def iota(shape, dim):
    return lax.broadcasted_iota(jnp.int32, shape, dim)


def rnd(v):
    return v.astype(BF16).astype(F32)


def down1(v):
    return jnp.where(iota(v.shape, 0) >= 1, pltpu.roll(v, 1, 0), 0.0)


def up1(v):
    n = v.shape[0]
    return jnp.where(iota(v.shape, 0) < n - 1, pltpu.roll(v, n - 1, 0), 0.0)


def lroll(v, s):
    s = s % v.shape[1]
    return v if s == 0 else pltpu.roll(v, s, 1)


def place(tiles, lane, src, dst):
    t, off = src // 128, src % 128
    v = lroll(tiles[t], dst - off)
    if off + W > 128:
        v = jnp.where(lane - dst < 128 - off, v, lroll(tiles[t + 1], dst - off))
    return jnp.where((lane >= dst) & (lane < dst + W), v, 0.0)


def spread(tiles, lane, v, src, dst):
    t, off = dst // 128, dst % 128
    v = lroll(jnp.where((lane >= src) & (lane < src + W), v, 0.0), off - src)
    if off + W > 128:
        tiles[t] = tiles[t] + jnp.where(lane >= off, v, 0.0)
        tiles[t + 1] = tiles[t + 1] + jnp.where(lane < off + W - 128, v, 0.0)
    else:
        tiles[t] = tiles[t] + v


def build_band(w1_ref, t1):
    t1[...] = jnp.zeros_like(t1)
    row = iota((16, 128), 0)
    lane = iota((16, 128), 1)
    for ao in range(12):
        w = w1_ref[ao // 3, ao % 3].astype(F32)
        left = jnp.concatenate([w, jnp.zeros((12, 64), F32)], 0)
        patch = jnp.concatenate([left, pltpu.roll(left, 2, 0)], 1)
        for s in (13, 1, 5, 9):
            rolled = pltpu.roll(patch, s, 0)
            parts = [(0, rolled)]
            if s == 13:
                parts = [(0, jnp.where(row >= 13, rolled, 0.0)), (1, jnp.where(row < 13, rolled, 0.0))]
            for v in range(13):
                start = 4 * v - 3
                if start % 16 != s:
                    continue
                for over, tile in parts:
                    g = start // 16 + over
                    if g < 0 or g > 2:
                        continue
                    if v == 0:
                        tile = jnp.where(lane >= 64, tile, 0.0)
                    if v == 12:
                        tile = jnp.where(lane < 64, tile, 0.0)
                    r0 = ao * 64 + g * 16
                    t1[r0 : r0 + 16, v * 128 : v * 128 + 128] = tile.astype(BF16)


def silu_pair(v):
    s = jax.nn.sigmoid(v)
    return v * s, s * (1.0 + v * (1.0 - s))


def rows16(v, k):
    return v[k * 16 : k * 16 + 16]


def disc_stage(
    recv_ref, w2_ref, w3_ref, w4_ref, head_ref, out_ref, wait2, wait3, wait4,
    t1, pp, a1, s1, a2, s2, a3, s3, c4, c3, c2, c1,
):
    lane = iota((16, 128), 1)
    x = []
    for o in range(3):
        tiles = [recv_ref[pl.ds(3 * t + o, 16, stride=24), :] for t in range(7)]
        first, last = tiles[0], tiles[6]
        tiles[0] = first + jnp.where((lane >= W) & (lane < 2 * W), down1(last), 0.0)
        tiles[6] = last + jnp.where(lane < W, up1(first), 0.0)
        x.append([rnd(v) for v in tiles])
    halves = {}
    for m in range(16):
        s = 1 - m % 2
        for o in range(3):
            q = s * 3 + o
            halves[m, q] = place(x[o], lane, W * (m + 1), (q % 2) * 64)
    for i in range(9):
        piece = {}
        for q in range(6):
            m = 2 * i - 1 if q < 3 else 2 * i
            if m == -1:
                piece[q] = down1(halves[15, q])
            elif m == 16:
                piece[q] = up1(halves[0, q])
            else:
                piece[q] = halves[m, q]
        for j in range(3):
            pp[i, :, j * 128 : j * 128 + 128] = (piece[2 * j] + piece[2 * j + 1]).astype(BF16)
    lhs = jnp.concatenate([pp[0:8].reshape(128, 384), pp[1:9].reshape(128, 384)], 1)
    for v in range(13):
        pre = dot(lhs, t1[:, v * 128 : v * 128 + 128])
        act, slope = silu_pair(pre)
        s1[:, v] = slope.reshape(8, 16, 128)
        a1[1:9, v] = act.astype(BF16).reshape(8, 16, 128)
        a1[0, v] = down1(rows16(act, 7)).astype(BF16)
        a1[9, v] = up1(rows16(act, 0)).astype(BF16)
    wait2()
    zero = jnp.zeros((16, 128), BF16)
    for m in range(6):
        a2[m, 0, 0] = zero
        a2[m, 1, 6] = zero
        c2[m, 0] = zero
        c2[m, 13] = zero
    for m in range(4):
        lhs = jnp.concatenate(
            [a1[2 * m + a, k : k + 12].reshape(192, 128) for a in range(4) for k in range(2)], 1
        )
        pre = dot(lhs, w2_ref[...].reshape(1024, 128))
        act, slope = silu_pair(pre)
        s2[m] = slope.reshape(12, 16, 128)
        for c in range(12):
            v = rows16(act, c)
            e, p = (c + 1) % 2, (c + 1) // 2
            a2[m + 1, e, p] = v.astype(BF16)
            if m == 3:
                a2[0, e, p] = down1(v).astype(BF16)
            if m == 0:
                a2[5, e, p] = up1(v).astype(BF16)
    wait3()
    zero = jnp.zeros((16, 256), BF16)
    for k in range(5):
        a3[k, 0] = zero
        a3[k, 7] = zero
    for k in range(4):
        c3[k, 0] = zero
        c3[k, 7] = zero
    acc = None
    for a in range(4):
        lhs = jnp.concatenate(
            [
                jnp.concatenate(
                    [a2[2 * m + a, b % 2, b // 2 : b // 2 + 6].reshape(96, 128) for m in range(2)], 0
                )
                for b in range(4)
            ],
            1,
        )
        term = dot(lhs, w3_ref[a * 4 : a * 4 + 4].reshape(512, 256))
        acc = term if acc is None else acc + term
    act, slope = silu_pair(acc)
    s3[...] = slope.reshape(2, 6, 16, 256)
    for c in range(6):
        v0, v1 = rows16(act, c), rows16(act, 6 + c)
        a3[0, c + 1] = down1(v1).astype(BF16)
        a3[1, c + 1] = v0.astype(BF16)
        a3[2, c + 1] = v1.astype(BF16)
        a3[3, c + 1] = up1(v0).astype(BF16)
        a3[4, c + 1] = up1(v1).astype(BF16)
    wait4()
    acc = None
    for a in range(4):
        lhs = jnp.concatenate(
            [
                jnp.concatenate([a3[m + a, b : b + 5].reshape(80, 256) for m in range(2)], 0)
                for b in range(4)
            ],
            1,
        )
        term = dot(lhs, w4_ref[a * 4 : a * 4 + 4].reshape(1024, 512))
        acc = term if acc is None else acc + term
    _, slope = silu_pair(acc)
    rr = iota((160, 16), 0)
    tap = iota((160, 16), 1)
    y4 = 2 * (rr % 16) + rr // 80
    x4 = (rr % 80) // 16
    py = y4 + 1 - tap // 4
    px = x4 + 1 - tap % 4
    ok = (py >= 0) & (py <= 29) & (px >= 0) & (px <= 3) & (y4 <= 30)
    mask = jnp.where(ok, -SCALE, 0.0).astype(BF16)
    head = jnp.concatenate([head_ref[a].astype(F32) for a in range(4)], 0).astype(BF16)
    cot = dot(mask, head) * slope
    zero = jnp.zeros((16, 512), BF16)
    for k in range(5):
        for c in (0, 1, 7, 8):
            c4[k, c] = zero
    for c in range(5):
        v0, v1 = rows16(cot, c), rows16(cot, 5 + c)
        c4[0, c + 2] = down1(v0).astype(BF16)
        c4[1, c + 2] = down1(v1).astype(BF16)
        c4[2, c + 2] = v0.astype(BF16)
        c4[3, c + 2] = v1.astype(BF16)
        c4[4, c + 2] = up1(v0).astype(BF16)
    acc = None
    for a in range(4):
        for b in range(4):
            lhs = jnp.concatenate(
                [c4[m + 3 - a, 3 - b : 9 - b].reshape(96, 512) for m in range(2)], 0
            )
            term = dot(lhs, w4_ref[a * 4 + b], NT)
            acc = term if acc is None else acc + term
    cot = acc * s3[...].reshape(192, 256)
    for c in range(6):
        v0, v1 = rows16(cot, c), rows16(cot, 6 + c)
        c3[0, c + 1] = down1(v1).astype(BF16)
        c3[1, c + 1] = v0.astype(BF16)
        c3[2, c + 1] = v1.astype(BF16)
        c3[3, c + 1] = up1(v0).astype(BF16)
    for first in (0, 1):
        rows = (1, 3) if first == 0 else (0, 2)
        for e in range(2):
            p0 = 1 - e
            acc = None
            for a in (first, first + 2):
                for b in (e, e + 2):
                    lo = p0 + 1 - b // 2
                    lhs = jnp.concatenate(
                        [c3[(m + 1 - a) // 2 + 1, lo : lo + 6].reshape(96, 256) for m in rows], 0
                    )
                    term = dot(lhs, w3_ref[a * 4 + b], NT)
                    acc = term if acc is None else acc + term
            for n, m in enumerate(rows):
                for p in range(6):
                    c = 2 * (p0 + p) + e - 1
                    v = rows16(acc, n * 6 + p) * s2[m, c]
                    c2[m + 1, c + 1] = v.astype(BF16)
                    if m == 3:
                        c2[0, c + 1] = down1(v).astype(BF16)
                    if m == 0:
                        c2[5, c + 1] = up1(v).astype(BF16)
    for first in (0, 1):
        rhs = jnp.concatenate(
            [w2_ref[a, h * 128 : h * 128 + 128] for a in (first, first + 2) for h in range(2)], 1
        )
        for i in range(4):
            m = 2 * i + 1 - first
            lhs = jnp.concatenate(
                [
                    c2[(m + 1 - a) // 2 + 1, 1 - h : 14 - h].reshape(208, 128)
                    for a in (first, first + 2)
                    for h in range(2)
                ],
                1,
            )
            cot = dot(lhs, rhs, NT) * s1[m].reshape(208, 128)
            for v in range(13):
                c1[m * 16 : m * 16 + 16, v * 128 : v * 128 + 128] = rows16(cot, v).astype(BF16)
    grad = dot(c1[...], t1[...], NT)
    halves = {}
    for j in range(3):
        ps = []
        for i in range(9):
            v = None
            if i <= 7:
                v = grad[i * 16 : i * 16 + 16, j * 128 : j * 128 + 128]
            if i >= 1:
                u = grad[(i - 1) * 16 : i * 16, 384 + j * 128 : 512 + j * 128]
                v = u if v is None else v + u
            ps.append(v)
        for h in range(2):
            q = 2 * j + h
            for i in range(9):
                m = 2 * i - 1 if q < 3 else 2 * i
                if 0 <= m <= 15:
                    v = ps[i]
                    if m == 15:
                        v = v + up1(ps[0])
                    if m == 0:
                        v = v + down1(ps[8])
                    halves[m, q] = rnd(v)
    for o in range(3):
        tiles = [jnp.zeros((16, 128), F32) for _ in range(7)]
        for m in range(16):
            q = (1 - m % 2) * 3 + o
            spread(tiles, lane, halves[m, q], (q % 2) * 64, W * (m + 1))
        first, last = tiles[0], tiles[6]
        tiles[0] = first + jnp.where(lane < W, down1(last), 0.0)
        tiles[6] = last + jnp.where((lane >= W) & (lane < 2 * W), up1(first), 0.0)
        for t in range(7):
            out_ref[pl.ds(3 * t + o, 16, stride=24), :] = tiles[t]
    for k in range(21, 24):
        out_ref[pl.ds(k, 16, stride=24), :] = jnp.zeros((16, 128), F32)

def edge_mask(v, b, col):
    if b == 0:
        return jnp.where(col <= W - 2, v, 0.0)
    if b == 2:
        return jnp.where(col >= 1, v, 0.0)
    return v


def shifted(g, col):
    rows = []
    for ab in range(9):
        a, b = ab // 3, ab % 3
        rows.append(edge_mask(lroll(g, -((2 - a) * W + 1 - b))[:, 0:768], b, col))
    rows.append(jnp.zeros((56, 768), F32))
    return jnp.concatenate(rows, 0).astype(BF16)


def compact(dst, acc):
    dst[...] = jnp.zeros_like(dst)
    for ab in range(9):
        k = ab * 8
        dst[ab * 3 : ab * 3 + 3, :] = acc[k : k + 3, 0:128] + acc[k + 4 : k + 7, 128:256]


class Gather:
    def __init__(self, axis, count, buf, send, got):
        me = lax.axis_index(axis)
        self.buf, self.me, self.count = buf, me, count
        self.copies = [
            pltpu.make_async_remote_copy(
                src_ref=buf.at[me],
                dst_ref=buf.at[me],
                send_sem=send.at[d],
                recv_sem=got.at[d],
                device_id={axis: lax.rem(me + d, count)},
                device_id_type=MESH,
            )
            for d in range(1, count)
        ]

    def start(self, value):
        self.buf[self.me] = value
        for c in self.copies:
            c.start()

    def finish(self):
        for c in self.copies:
            c.wait()
        parts = [self.buf[k] for k in range(self.count)]
        while len(parts) > 1:
            parts = [a + b for a, b in zip(parts[::2], parts[1::2])]
        return parts[0]


def row_exchange(src, dst, send, got, own):
    r = lax.axis_index("row")
    local = pltpu.make_async_copy(src.at[r], dst.at[r], own)
    copies = [local]
    for d in range(1, FR):
        peer = lax.rem(r + d, FR)
        copies.append(
            pltpu.make_async_remote_copy(
                src_ref=src.at[peer],
                dst_ref=dst.at[r],
                send_sem=send.at[d],
                recv_sem=got.at[d],
                device_id={"row": peer},
                device_id_type=MESH,
            )
        )
    return copies


def edge_exchange(src, dst, send, got):
    r = lax.axis_index("row")
    return [
        pltpu.make_async_remote_copy(
            src_ref=src.at[k],
            dst_ref=dst.at[1 - k],
            send_sem=send.at[k],
            recv_sem=got.at[k],
            device_id={"row": lax.rem(r + d, FR)},
            device_id_type=MESH,
        )
        for d, k in ((FR - 1, 0), (1, 1))
    ]


def start_all(copies):
    for c in copies:
        c.start()


def wait_all(copies):
    for c in copies:
        c.wait()


def core_body(
    clips,
    w_ref, f_hbm, t_ref, w1_ref, w2_hbm, w3_hbm, w4_hbm, head_ref,
    sums_ref, gt_hbm, back_ref,
    fs, w2s, w3s, w4s, wm, parts, edges, recv, nb, wide, want, rec, redges, ne, msg, gan,
    gg, gts, xsum, clip_buf, row_buf,
    t1, pp, a1, s1, a2, s2, a3, s3, c4, c3, c2, c1,
    fsem, wsem, gsem, own, send0, got0, send1, got1, esend0, egot0, esend1, egot1,
    csend, cgot, rsend, rgot,
):
    r = lax.axis_index("row")
    clip = lax.axis_index("clip")
    barrier = pltpu.get_barrier_semaphore()
    for d in range(1, FR):
        pl.semaphore_signal(
            barrier, inc=1, device_id={"row": lax.rem(r + d, FR)}, device_id_type=MESH
        )
    for d in range(1, clips):
        pl.semaphore_signal(
            barrier, inc=1, device_id={"clip": lax.rem(clip + d, clips)}, device_id_type=MESH
        )
    loads = [pltpu.make_async_copy(f_hbm.at[f], fs.at[f], fsem.at[f]) for f in range(FR)]
    for p in range(8):
        loads[p].start()
        loads[p + 8].start()
    weights = [
        pltpu.make_async_copy(a, b, wsem.at[k])
        for k, (a, b) in enumerate(((w2_hbm, w2s), (w3_hbm, w3s), (w4_hbm, w4s)))
    ]
    start_all(weights)

    wm[...] = jnp.zeros_like(wm)
    for ab in range(9):
        v = w_ref[ab // 3, ab % 3].astype(F32)
        wm[ab * 8 : ab * 8 + 3, 0:128] = v
        wm[ab * 8 + 4 : ab * 8 + 7, 128:256] = v
    wmb = wm[...].astype(BF16)
    col = iota((8, 768), 1) % W
    lane = iota((16, 128), 1)
    pad = jnp.zeros((8, 128), F32)
    for k in range(21, 24):
        parts[:, k, :] = jnp.zeros((FR, 128), F32)

    def pair_features(p):
        return jnp.concatenate([fs[p].reshape(768, 128), fs[p + 8].reshape(768, 128)], 1)

    for p in range(8):
        loads[p].wait()
        loads[p + 8].wait()
        out = dot(wmb, pair_features(p), NT)
        total = None
        for ab in range(9):
            a, b = ab // 3, ab % 3
            g = edge_mask(out[ab * 8 : ab * 8 + 8, :], b, col)
            g = lroll(jnp.concatenate([g, pad], 1), (2 - a) * W + 1 - b)
            total = g if total is None else total + g
        for h in range(2):
            f = p + 8 * h
            for t in range(7):
                tile = total[4 * h : 4 * h + 3, t * 128 : t * 128 + 128]
                parts[f, 3 * t : 3 * t + 3, :] = tile
                if t in (0, 6):
                    for o in range(3):
                        edges[t // 6, o, f : f + 1, :] = tile[o : o + 1, :]
    pl.semaphore_wait(barrier, FR + clips - 2)
    first = row_exchange(parts, recv, send0, got0, own.at[0])
    ends = edge_exchange(edges, nb, esend0, egot0)
    start_all(ends)
    start_all(first)

    build_band(w1_ref, t1)
    wide[:, 0:W] = t_ref[...].astype(F32)
    for o in range(3):
        tiles = [jnp.zeros((16, 128), F32) for _ in range(7)]
        for y in range(16):
            spread(tiles, lane, wide[pl.ds(o * 16 + y, 16, stride=48), :], 0, W * (y + 1))
        for t in range(7):
            want[t, o] = tiles[t]
    flat = parts.reshape(FR * 24, 128)
    wait_all(ends)
    for o in range(3):
        for t in range(7):
            v = flat[pl.ds(3 * t + o, 16, stride=24), :]
            if t == 0:
                v = v + jnp.where((lane >= W) & (lane < 2 * W) & (r > 0), nb[0, o], 0.0)
            if t == 6:
                v = v + jnp.where((lane < W) & (r < FR - 1), nb[1, o], 0.0)
            v = SCALE * (v - want[t, o])
            if t == 0:
                v = jnp.where(lane >= W, v, 0.0)
            if t == 6:
                v = jnp.where(lane < W, v, 0.0)
            rec[t, o] = v
            if t in (0, 6):
                redges[t // 6, o] = v
    rends = edge_exchange(redges, ne, esend1, egot1)
    start_all(rends)
    wait_all(first)

    disc_stage(
        recv.reshape(FR * 24, 128), w2s, w3s, w4s, head_ref, msg.reshape(FR * 24, 128),
        weights[0].wait, weights[1].wait, weights[2].wait,
        t1, pp, a1, s1, a2, s2, a3, s3, c4, c3, c2, c1,
    )
    second = row_exchange(msg, gan, send1, got1, own.at[1])
    start_all(second)

    gg[...] = jnp.zeros_like(gg)
    wait_all(rends)

    def put(k, t, o, v):
        gg[k, pl.ds(t * 8 + o, 8, stride=56), :] = v[0:8]
        gg[k, pl.ds(t * 8 + 4 + o, 8, stride=56), :] = v[8:16]

    for o in range(3):
        for t in range(7):
            v = rec[t, o]
            if t == 0:
                v = v + jnp.where((lane < W) & (r > 0), ne[0, o], 0.0)
            if t == 6:
                v = v + jnp.where((lane >= W) & (lane < 2 * W) & (r < FR - 1), ne[1, o], 0.0)
            put(0, t, o, v)

    def weight_part(k, p, acc):
        g = jnp.concatenate([gg[k, p * 56 + t * 8 : p * 56 + t * 8 + 8, :] for t in range(7)], 1)
        gt = shifted(g, col)
        gts[p, :, k * 128 : k * 128 + 128] = gt.T
        term = dot(gt[0:80], pair_features(p))
        return term if acc is None else acc + term

    acc = None
    for p in range(8):
        acc = weight_part(0, p, acc)
    compact(xsum, acc)
    rec_clip = Gather("clip", clips, clip_buf.at[0], csend.at[0], cgot.at[0])
    rec_row = Gather("row", FR, row_buf.at[0], rsend.at[0], rgot.at[0])
    gan_clip = Gather("clip", clips, clip_buf.at[1], csend.at[1], cgot.at[1])
    gan_row = Gather("row", FR, row_buf.at[1], rsend.at[1], rgot.at[1])
    rec_clip.start(xsum[...])

    wait_all(second)
    flat = gan.reshape(FR * 24, 128)
    for o in range(3):
        for t in range(7):
            put(1, t, o, flat[pl.ds(3 * t + o, 16, stride=24), :])
    acc = None
    for p in range(8):
        acc = weight_part(1, p, acc)
    compact(xsum, acc)
    gan_clip.start(xsum[...])
    stores = [pltpu.make_async_copy(gts.at[p], gt_hbm.at[p], gsem.at[p]) for p in range(8)]
    start_all(stores)
    rec_row.start(rec_clip.finish())
    for o in range(3):
        tiles = [flat[pl.ds(3 * t + o, 16, stride=24), :] for t in range(7)]
        for y in range(16):
            wide[pl.ds(o * 16 + y, 16, stride=48), :] = place(tiles, lane, W * (y + 1), 0)
    back_ref[...] = wide[:, 0:W].astype(BF16)
    gan_row.start(gan_clip.finish())
    sums_ref[0:32] = rec_row.finish()
    sums_ref[32:64] = gan_row.finish()
    wait_all(stores)


def core(clips, conv_weight, features, target, w1, w2, w3, w4, head):
    anyspec = lambda: pl.BlockSpec(memory_space=pl.ANY)
    dma = pltpu.SemaphoreType.DMA
    return pl.pallas_call(
        functools.partial(core_body, clips),
        out_shape=(
            jax.ShapeDtypeStruct((64, 128), F32),
            jax.ShapeDtypeStruct((8, 768, 256), BF16),
            jax.ShapeDtypeStruct((768, W), BF16),
        ),
        in_specs=[vspec(), anyspec(), vspec(), vspec(), anyspec(), anyspec(), anyspec(), vspec()],
        out_specs=(vspec(), anyspec(), vspec()),
        scratch_shapes=[
            VM((FR, 16, W, 128), BF16),
            VM((4, 256, 128), BF16),
            VM((16, 128, 256), BF16),
            VM((16, 256, 512), BF16),
            VM((80, 256), F32),
            VM((FR, 24, 128), F32),
            VM((2, 3, FR, 128), F32),
            VM((FR, 24, 128), F32),
            VM((2, 3, FR, 128), F32),
            VM((768, 128), F32),
            VM((7, 3, FR, 128), F32),
            VM((7, 3, FR, 128), F32),
            VM((2, 3, FR, 128), F32),
            VM((2, 3, FR, 128), F32),
            VM((FR, 24, 128), F32),
            VM((FR, 24, 128), F32),
            VM((2, 448, 128), F32),
            VM((8, 768, 256), BF16),
            VM((32, 128), F32),
            VM((2, clips, 32, 128), F32),
            VM((2, FR, 32, 128), F32),
            VM((768, 1664), BF16),
            VM((9, 16, 384), BF16),
            VM((10, 13, 16, 128), BF16),
            VM((8, 13, 16, 128), F32),
            VM((6, 2, 7, 16, 128), BF16),
            VM((4, 12, 16, 128), F32),
            VM((5, 8, 16, 256), BF16),
            VM((2, 6, 16, 256), F32),
            VM((5, 9, 16, 512), BF16),
            VM((4, 8, 16, 256), BF16),
            VM((6, 14, 16, 128), BF16),
            VM((128, 1664), BF16),
            dma((FR,)),
            dma((3,)),
            dma((8,)),
            dma((2,)),
            dma((FR,)),
            dma((FR,)),
            dma((FR,)),
            dma((FR,)),
            dma((2,)),
            dma((2,)),
            dma((2,)),
            dma((2,)),
            dma((2, clips)),
            dma((2, clips)),
            dma((2, FR)),
            dma((2, FR)),
        ],
        compiler_params=pltpu.CompilerParams(collective_id=0, has_side_effects=True),
        name="core",
    )(conv_weight, features, target, w1, w2, w3, w4, head)


def final_body(s_ref, w_ref, g_ref, b_ref, out_ref, wg_ref, ad_ref, back_ref, wf, step, pixels):
    i = pl.program_id(0)

    @pl.when(i == 0)
    def _():
        rec, gan = s_ref[0:32], s_ref[32:64]
        adaptive = jnp.sqrt(jnp.sum(rec * rec, keepdims=True)) / (
            jnp.sqrt(jnp.sum(gan * gan, keepdims=True)) + EPS
        )
        ad_ref[...] = adaptive
        wf[...] = jnp.zeros_like(wf)
        for ab in range(9):
            w = w_ref[ab // 3, ab % 3].astype(F32)
            k = ab * 8
            wf[k : k + 3, 0:128] = w
            wf[k + 4 : k + 7, 128:256] = w
            wf[128 + k : 131 + k, 0:128] = adaptive * w
            wf[132 + k : 135 + k, 128:256] = adaptive * w
        mixed = (rec + adaptive * gan) / pixels
        for ab in range(9):
            wg_ref[ab // 3, ab % 3] = mixed[ab * 3 : ab * 3 + 3]
        back_ref[...] = b_ref[...]

    wfb = wf[...].astype(BF16)
    for k in range(step):
        out = dot(g_ref[k], wfb).astype(BF16)
        out_ref[0, k] = out[:, 0:128].reshape(16, W, 128)
        out_ref[1, k] = out[:, 128:256].reshape(16, W, 128)


def final(sums, conv_weight, g, back, pixels):
    step = 2
    full = lambda shape: pl.BlockSpec(shape, lambda i: (0,) * len(shape))
    return pl.pallas_call(
        functools.partial(final_body, step=step, pixels=pixels),
        grid=(8 // step,),
        out_shape=(
            jax.ShapeDtypeStruct((2, 8, 16, W, 128), BF16),
            jax.ShapeDtypeStruct((3, 3, 3, 128), F32),
            jax.ShapeDtypeStruct((1, 1), F32),
            jax.ShapeDtypeStruct((768, W), BF16),
        ),
        in_specs=[
            full((64, 128)),
            full((3, 3, 3, 128)),
            pl.BlockSpec((step, 768, 256), lambda i: (i, 0, 0)),
            full((768, W)),
        ],
        out_specs=(
            pl.BlockSpec((2, step, 16, W, 128), lambda i: (0, i, 0, 0, 0)),
            full((3, 3, 3, 128)),
            full((1, 1)),
            full((768, W)),
        ),
        scratch_shapes=[VM((256, 256), F32)],
        name="final",
    )(sums, conv_weight, g, back)


def per_device(
    features, target, conv_weight, disc_first, disc_second, disc_third, disc_fourth, disc_head
):
    clips = lax.axis_size("clip")
    wanted = jnp.transpose(target[0], (0, 2, 1, 3)).reshape(768, W)
    w1 = jnp.transpose(disc_first, (0, 2, 1, 3))
    w2 = disc_second.reshape(4, 256, 128)
    w3 = disc_third.reshape(16, 128, 256)
    w4 = disc_fourth.reshape(16, 256, 512)
    head = disc_head.reshape(4, 4, 512)
    pixels = float(clips * FR * 256 * W)
    sums, g, back = core(clips, conv_weight, features[0], wanted, w1, w2, w3, w4, head)
    feature_grad, weight_grad, adaptive, back = final(sums, conv_weight, g, back, pixels)
    feature_grad = feature_grad.reshape(1, FR, 16, W, 128)
    image_back = jnp.transpose(back.reshape(1, FR, 3, 16, W), (0, 1, 3, 2, 4))
    return (feature_grad, image_back, weight_grad, adaptive[0, 0])


def solution(mesh):
    return jax.shard_map(
        per_device,
        mesh=mesh,
        in_specs=(
            P("clip", None, "row", None, None),
            P("clip", None, "row", None, None),
            P(),
            P(),
            P(),
            P(),
            P(),
            P(),
        ),
        out_specs=(
            P("clip", None, "row", None, None),
            P("clip", None, "row", None, None),
            P(),
            P(),
        ),
        check_vma=False,
    )
```

time: 73.6 us -> 50.4 us (0.68)
  Pallas kernels: 71.3 us -> 49.1 us
  local copies, waits for them, and re-layouts: 1.18 us -> 0 us
    pallas_call x8 -> x2, Pallas kernels: 71.3 us -> 49.1 us  [the longest x1 43.9 us: core(): pl.pallas_call(functools.partial(core_body, clips), out_shape=(jax.ShapeD...]
    slice x1 -> x0, local copies, waits for them, and re-layouts: 1.18 us -> none  [per_device(): return (feature_grad[None], image_back[None], weight_grad, adaptive[0, 0])]
where the time goes in v2:
time: 50.4 us; the launch traced here: 49.7 us
  Pallas kernels  49.1 us (97%)
  between operations  0.64 us (1%)
    pallas_call x1, Pallas kernels, core(): pl.pallas_call(functools.partial(core_body, clips), out_shape=(jax.ShapeD...  43.9 us
    pallas_call x1, Pallas kernels, final(): pl.pallas_call(functools.partial(final_body, step=step, pixels=pixels), g...  5.16 us

profile of v2, /device:TPU:1, one launch (start us, length us, event | category | flops | bytes accessed | tf_op | source)
XLA Modules:
  0.0 49.7 jit_solution(942382472819217925)
XLA Ops:
  0.6 43.9 %core.1 = (f32[64,128]{1,0:T(8,128)}, bf16[8,768,256]{2,1,0:T(8,128)(2,1)}, bf16[768,48]{1,0:T(8,128)(2,1)}) custom-call(bf16[3,3,3,128]{3,2,1,0:T(4,128)(2,1)} %w_ref.3, bf16[16,16,48,128]{3,2,1,0:T(8,128)(2,1)} %bitcast.17, bf16[768,48]{1,0:T(8,128)(2,1)} %bitcast.20, bf16[4,3,4,64]{3,2,1,0:T(4,128)(2,1)} %bitcast.22, bf16[4,256,128]{2,1,0:T(8,128)(2,1)} %bitcast.19, ...), custom_call_target="tpu_custom_call" | custom-call | tf_op jit(solution)/shard_map/core/pallas_call | solution.py:587
  44.6 5.2 %final.1 = (bf16[2,8,16,48,128]{4,3,2,1,0:T(8,128)(2,1)}, f32[3,3,3,128]{3,2,1,0:T(4,128)}, f32[1,1]{1,0:T(1,128)}, bf16[768,48]{1,0:T(8,128)(2,1)}) custom-call(f32[64,128]{1,0:T(8,128)} %get-tuple-element.11.s_ref, bf16[3,3,3,128]{3,2,1,0:T(4,128)(2,1)} %w_ref.3, bf16[8,768,256]{2,1,0:T(8,128)(2,1)} %get-tuple-element.12.g_ref, ...), custom_call_target="tpu_custom_call" | custom-call | tf_op jit(solution)/shard_map/final/pallas_call | solution.py:685

commit v3 on v2

--- a/solution.py
+++ b/solution.py
@@ -231,12 +231,18 @@
         c4[4, c + 2] = up1(v0).astype(BF16)
     acc = None
     for a in range(4):
-        for b in range(4):
-            lhs = jnp.concatenate(
-                [c4[m + 3 - a, 3 - b : 9 - b].reshape(96, 512) for m in range(2)], 0
-            )
-            term = dot(lhs, w4_ref[a * 4 + b], NT)
-            acc = term if acc is None else acc + term
+        lhs = jnp.concatenate(
+            [
+                jnp.concatenate(
+                    [c4[m + 3 - a, 3 - b : 9 - b].reshape(96, 512) for m in range(2)], 0
+                )
+                for b in range(4)
+            ],
+            1,
+        )
+        rhs = jnp.concatenate([w4_ref[a * 4 + b] for b in range(4)], 1)
+        term = dot(lhs, rhs, NT)
+        acc = term if acc is None else acc + term
     cot = acc * s3[...].reshape(192, 256)
     for c in range(6):
         v0, v1 = rows16(cot, c), rows16(cot, 6 + c)
@@ -248,15 +254,21 @@
         rows = (1, 3) if first == 0 else (0, 2)
         for e in range(2):
             p0 = 1 - e
-            acc = None
-            for a in (first, first + 2):
-                for b in (e, e + 2):
-                    lo = p0 + 1 - b // 2
-                    lhs = jnp.concatenate(
-                        [c3[(m + 1 - a) // 2 + 1, lo : lo + 6].reshape(96, 256) for m in rows], 0
+            taps = [(a, b) for a in (first, first + 2) for b in (e, e + 2)]
+            lhs = jnp.concatenate(
+                [
+                    jnp.concatenate(
+                        [
+                            c3[(m + 1 - a) // 2 + 1, p0 + 1 - b // 2 : p0 + 7 - b // 2].reshape(96, 256)
+                            for m in rows
+                        ],
+                        0,
                     )
-                    term = dot(lhs, w3_ref[a * 4 + b], NT)
-                    acc = term if acc is None else acc + term
+                    for a, b in taps
+                ],
+                1,
+            )
+            acc = dot(lhs, jnp.concatenate([w3_ref[a * 4 + b] for a, b in taps], 1), NT)
             for n, m in enumerate(rows):
                 for p in range(6):
                     c = 2 * (p0 + p) + e - 1
@@ -332,7 +344,7 @@
     for ab in range(9):
         a, b = ab // 3, ab % 3
         rows.append(edge_mask(lroll(g, -((2 - a) * W + 1 - b))[:, 0:768], b, col))
-    rows.append(jnp.zeros((56, 768), F32))
+    rows.append(jnp.zeros((8, 768), F32))
     return jnp.concatenate(rows, 0).astype(BF16)
 
 
@@ -419,12 +431,12 @@
 
 def core_body(
     clips,
-    w_ref, f_hbm, t_ref, w1_ref, w2_hbm, w3_hbm, w4_hbm, head_ref,
-    sums_ref, gt_hbm, back_ref,
-    fs, w2s, w3s, w4s, wm, parts, edges, recv, nb, wide, want, rec, redges, ne, msg, gan,
-    gg, gts, xsum, clip_buf, row_buf,
+    w_hbm, f_hbm, t_hbm, w1_hbm, w2_hbm, w3_hbm, w4_hbm, head_hbm,
+    sums_ref, a_ref, b_ref, back_ref,
+    fs, w_ref, t_ref, w1_ref, w2s, w3s, w4s, head_ref, wm, parts, edges, recv, nb, wide, want, rec, redges, ne, msg, gan,
+    gg, xsum, clip_buf, row_buf,
     t1, pp, a1, s1, a2, s2, a3, s3, c4, c3, c2, c1,
-    fsem, wsem, gsem, own, send0, got0, send1, got1, esend0, egot0, esend1, egot1,
+    fsem, wsem, own, send0, got0, send1, got1, esend0, egot0, esend1, egot1,
     csend, cgot, rsend, rgot,
 ):
     r = lax.axis_index("row")
@@ -439,14 +451,21 @@
             barrier, inc=1, device_id={"clip": lax.rem(clip + d, clips)}, device_id_type=MESH
         )
     loads = [pltpu.make_async_copy(f_hbm.at[f], fs.at[f], fsem.at[f]) for f in range(FR)]
+    weights = [
+        pltpu.make_async_copy(a, b, wsem.at[k])
+        for k, (a, b) in enumerate(
+            (
+                (w2_hbm, w2s), (w3_hbm, w3s), (w4_hbm, w4s), (head_hbm, head_ref),
+                (w1_hbm, w1_ref), (t_hbm, t_ref), (w_hbm, w_ref),
+            )
+        )
+    ]
+    weights[6].start()
     for p in range(8):
         loads[p].start()
         loads[p + 8].start()
-    weights = [
-        pltpu.make_async_copy(a, b, wsem.at[k])
-        for k, (a, b) in enumerate(((w2_hbm, w2s), (w3_hbm, w3s), (w4_hbm, w4s)))
-    ]
-    start_all(weights)
+    start_all(weights[3:6])
+    weights[6].wait()
 
     wm[...] = jnp.zeros_like(wm)
     for ab in range(9):
@@ -466,6 +485,8 @@
     for p in range(8):
         loads[p].wait()
         loads[p + 8].wait()
+        if p == 5:
+            start_all(weights[0:3])
         out = dot(wmb, pair_features(p), NT)
         total = None
         for ab in range(9):
@@ -487,7 +508,9 @@
     start_all(ends)
     start_all(first)
 
+    weights[4].wait()
     build_band(w1_ref, t1)
+    weights[5].wait()
     wide[:, 0:W] = t_ref[...].astype(F32)
     for o in range(3):
         tiles = [jnp.zeros((16, 128), F32) for _ in range(7)]
@@ -515,6 +538,7 @@
     rends = edge_exchange(redges, ne, esend1, egot1)
     start_all(rends)
     wait_all(first)
+    weights[3].wait()
 
     disc_stage(
         recv.reshape(FR * 24, 128), w2s, w3s, w4s, head_ref, msg.reshape(FR * 24, 128),
@@ -540,16 +564,18 @@
                 v = v + jnp.where((lane >= W) & (lane < 2 * W) & (r < FR - 1), ne[1, o], 0.0)
             put(0, t, o, v)
 
-    def weight_part(k, p, acc):
+    def weight_part(k, p, acc, part_ref):
         g = jnp.concatenate([gg[k, p * 56 + t * 8 : p * 56 + t * 8 + 8, :] for t in range(7)], 1)
         gt = shifted(g, col)
-        gts[p, :, k * 128 : k * 128 + 128] = gt.T
-        term = dot(gt[0:80], pair_features(p))
+        out = dot(gt, wmb, TN)
+        part_ref[p] = out[:, 0:128]
+        part_ref[p + 8] = out[:, 128:256]
+        term = dot(gt, pair_features(p))
         return term if acc is None else acc + term
 
     acc = None
     for p in range(8):
-        acc = weight_part(0, p, acc)
+        acc = weight_part(0, p, acc, a_ref)
     compact(xsum, acc)
     rec_clip = Gather("clip", clips, clip_buf.at[0], csend.at[0], cgot.at[0])
     rec_row = Gather("row", FR, row_buf.at[0], rsend.at[0], rgot.at[0])
@@ -564,11 +590,9 @@
             put(1, t, o, flat[pl.ds(3 * t + o, 16, stride=24), :])
     acc = None
     for p in range(8):
-        acc = weight_part(1, p, acc)
+        acc = weight_part(1, p, acc, b_ref)
     compact(xsum, acc)
     gan_clip.start(xsum[...])
-    stores = [pltpu.make_async_copy(gts.at[p], gt_hbm.at[p], gsem.at[p]) for p in range(8)]
-    start_all(stores)
     rec_row.start(rec_clip.finish())
     for o in range(3):
         tiles = [flat[pl.ds(3 * t + o, 16, stride=24), :] for t in range(7)]
@@ -578,26 +602,30 @@
     gan_row.start(gan_clip.finish())
     sums_ref[0:32] = rec_row.finish()
     sums_ref[32:64] = gan_row.finish()
-    wait_all(stores)
 
 
 def core(clips, conv_weight, features, target, w1, w2, w3, w4, head):
-    anyspec = lambda: pl.BlockSpec(memory_space=pl.ANY)
+    hbm = lambda: pl.BlockSpec(memory_space=pltpu.HBM)
     dma = pltpu.SemaphoreType.DMA
     return pl.pallas_call(
         functools.partial(core_body, clips),
         out_shape=(
-            jax.ShapeDtypeStruct((64, 128), F32),
-            jax.ShapeDtypeStruct((8, 768, 256), BF16),
-            jax.ShapeDtypeStruct((768, W), BF16),
+            VM((64, 128), F32),
+            VM((FR, 768, 128), F32),
+            VM((FR, 768, 128), F32),
+            VM((768, W), BF16),
         ),
-        in_specs=[vspec(), anyspec(), vspec(), vspec(), anyspec(), anyspec(), anyspec(), vspec()],
-        out_specs=(vspec(), anyspec(), vspec()),
+        in_specs=[hbm()] * 8,
+        out_specs=(vspec(), vspec(), vspec(), vspec()),
         scratch_shapes=[
             VM((FR, 16, W, 128), BF16),
+            VM((3, 3, 3, 128), BF16),
+            VM((768, W), BF16),
+            VM((4, 3, 4, 64), BF16),
             VM((4, 256, 128), BF16),
             VM((16, 128, 256), BF16),
             VM((16, 256, 512), BF16),
+            VM((4, 4, 512), BF16),
             VM((80, 256), F32),
             VM((FR, 24, 128), F32),
             VM((2, 3, FR, 128), F32),
@@ -611,7 +639,6 @@
             VM((FR, 24, 128), F32),
             VM((FR, 24, 128), F32),
             VM((2, 448, 128), F32),
-            VM((8, 768, 256), BF16),
             VM((32, 128), F32),
             VM((2, clips, 32, 128), F32),
             VM((2, FR, 32, 128), F32),
@@ -628,8 +655,7 @@
             VM((6, 14, 16, 128), BF16),
             VM((128, 1664), BF16),
             dma((FR,)),
-            dma((3,)),
-            dma((8,)),
+            dma((7,)),
             dma((2,)),
             dma((FR,)),
             dma((FR,)),
@@ -644,68 +670,54 @@
             dma((2, FR)),
             dma((2, FR)),
         ],
-        compiler_params=pltpu.CompilerParams(collective_id=0, has_side_effects=True),
+        compiler_params=pltpu.CompilerParams(
+            collective_id=0, has_side_effects=True, vmem_limit_bytes=36 << 20
+        ),
         name="core",
-    )(conv_weight, features, target, w1, w2, w3, w4, head)
-
-
-def final_body(s_ref, w_ref, g_ref, b_ref, out_ref, wg_ref, ad_ref, back_ref, wf, step, pixels):
-    i = pl.program_id(0)
-
-    @pl.when(i == 0)
-    def _():
-        rec, gan = s_ref[0:32], s_ref[32:64]
-        adaptive = jnp.sqrt(jnp.sum(rec * rec, keepdims=True)) / (
-            jnp.sqrt(jnp.sum(gan * gan, keepdims=True)) + EPS
-        )
-        ad_ref[...] = adaptive
-        wf[...] = jnp.zeros_like(wf)
-        for ab in range(9):
-            w = w_ref[ab // 3, ab % 3].astype(F32)
-            k = ab * 8
-            wf[k : k + 3, 0:128] = w
-            wf[k + 4 : k + 7, 128:256] = w
-            wf[128 + k : 131 + k, 0:128] = adaptive * w
-            wf[132 + k : 135 + k, 128:256] = adaptive * w
-        mixed = (rec + adaptive * gan) / pixels
-        for ab in range(9):
-            wg_ref[ab // 3, ab % 3] = mixed[ab * 3 : ab * 3 + 3]
-        back_ref[...] = b_ref[...]
-
-    wfb = wf[...].astype(BF16)
-    for k in range(step):
-        out = dot(g_ref[k], wfb).astype(BF16)
-        out_ref[0, k] = out[:, 0:128].reshape(16, W, 128)
-        out_ref[1, k] = out[:, 128:256].reshape(16, W, 128)
-
-
-def final(sums, conv_weight, g, back, pixels):
-    step = 2
-    full = lambda shape: pl.BlockSpec(shape, lambda i: (0,) * len(shape))
+    )(
+        *(
+            pltpu.with_memory_space_constraint(v, pltpu.HBM)
+            for v in (conv_weight, features, target, w1, w2, w3, w4, head)
+        )
+    )
+
+
+def final_body(pixels, s_ref, a_ref, b_ref, g_ref, out_hbm, wg_ref, ad_ref, back_ref, buf, sem):
+    rec, gan = s_ref[0:32], s_ref[32:64]
+    adaptive = jnp.sqrt(jnp.sum(rec * rec, keepdims=True)) / (
+        jnp.sqrt(jnp.sum(gan * gan, keepdims=True)) + EPS
+    )
+    scale = jnp.broadcast_to(adaptive, (8, 128))[None]
+    stores = []
+    for f in range(FR):
+        v = a_ref[f].reshape(96, 8, 128) + scale * b_ref[f].reshape(96, 8, 128)
+        buf[f] = v.reshape(16, W, 128).astype(BF16)
+        copy = pltpu.make_async_copy(buf.at[f], out_hbm.at[f], sem.at[f])
+        copy.start()
+        stores.append(copy)
+    ad_ref[...] = adaptive
+    mixed = (rec + adaptive * gan) / pixels
+    for ab in range(9):
+        wg_ref[ab // 3, ab % 3] = mixed[ab * 3 : ab * 3 + 3]
+    back_ref[...] = g_ref[...]
+    wait_all(stores)
+
+
+def final(sums, a, b, back, pixels):
     return pl.pallas_call(
-        functools.partial(final_body, step=step, pixels=pixels),
-        grid=(8 // step,),
+        functools.partial(final_body, pixels),
         out_shape=(
-            jax.ShapeDtypeStruct((2, 8, 16, W, 128), BF16),
+            jax.ShapeDtypeStruct((FR, 16, W, 128), BF16),
             jax.ShapeDtypeStruct((3, 3, 3, 128), F32),
             jax.ShapeDtypeStruct((1, 1), F32),
             jax.ShapeDtypeStruct((768, W), BF16),
         ),
-        in_specs=[
-            full((64, 128)),
-            full((3, 3, 3, 128)),
-            pl.BlockSpec((step, 768, 256), lambda i: (i, 0, 0)),
-            full((768, W)),
-        ],
-        out_specs=(
-            pl.BlockSpec((2, step, 16, W, 128), lambda i: (0, i, 0, 0, 0)),
-            full((3, 3, 3, 128)),
-            full((1, 1)),
-            full((768, W)),
-        ),
-        scratch_shapes=[VM((256, 256), F32)],
+        in_specs=[vspec()] * 4,
+        out_specs=(pl.BlockSpec(memory_space=pltpu.HBM), vspec(), vspec(), vspec()),
+        scratch_shapes=[VM((FR, 16, W, 128), BF16), pltpu.SemaphoreType.DMA((FR,))],
+        compiler_params=pltpu.CompilerParams(vmem_limit_bytes=24 << 20),
         name="final",
-    )(sums, conv_weight, g, back)
+    )(sums, a, b, back)
 
 
 def per_device(
@@ -719,11 +731,10 @@
     w4 = disc_fourth.reshape(16, 256, 512)
     head = disc_head.reshape(4, 4, 512)
     pixels = float(clips * FR * 256 * W)
-    sums, g, back = core(clips, conv_weight, features[0], wanted, w1, w2, w3, w4, head)
-    feature_grad, weight_grad, adaptive, back = final(sums, conv_weight, g, back, pixels)
-    feature_grad = feature_grad.reshape(1, FR, 16, W, 128)
+    sums, a, b, back = core(clips, conv_weight, features[0], wanted, w1, w2, w3, w4, head)
+    feature_grad, weight_grad, adaptive, back = final(sums, a, b, back, pixels)
     image_back = jnp.transpose(back.reshape(1, FR, 3, 16, W), (0, 1, 3, 2, 4))
-    return (feature_grad, image_back, weight_grad, adaptive[0, 0])
+    return (feature_grad[None], image_back, weight_grad, adaptive[0, 0])
 
 
 def solution(mesh):

time: 50.4 us -> 47.6 us (0.944)
  Pallas kernels: 49.1 us -> 46.4 us
    pallas_call x2, Pallas kernels: 49.1 us -> 46.4 us  [the longest x1 43.7 us: core(): pl.pallas_call(functools.partial(core_body, clips), out_shape=(VM((64, 12...]
where the time goes in v3:
time: 47.6 us; the launch traced here: 47.1 us
  Pallas kernels  46.4 us (97%)
  between operations  0.64 us (1%)
    pallas_call x1, Pallas kernels, core(): pl.pallas_call(functools.partial(core_body, clips), out_shape=(VM((64, 12...  43.7 us
    pallas_call x1, Pallas kernels, final(): pl.pallas_call(functools.partial(final_body, pixels), out_shape=(jax.Shap...  2.69 us

profile of v3, /device:TPU:1, one launch (start us, length us, event | category | flops | bytes accessed | tf_op | source)
XLA Modules:
  0.0 47.1 jit_solution(9860282797182614293)
XLA Ops:
  0.6 43.7 %core.1 = (f32[64,128]{1,0:T(8,128)S(1)}, f32[16,768,128]{2,1,0:T(8,128)S(1)}, f32[16,768,128]{2,1,0:T(8,128)S(1)}, bf16[768,48]{1,0:T(8,128)(2,1)S(1)}) custom-call(bf16[3,3,3,128]{3,2,1,0:T(4,128)(2,1)} %w_hbm.1, bf16[16,16,48,128]{3,2,1,0:T(8,128)(2,1)} %bitcast.17, bf16[768,48]{1,0:T(8,128)(2,1)} %bitcast.20, bf16[4,3,4,64]{3,2,1,0:T(4,128)(2,1)} %bitcast.22, ...), custom_call_target="tpu_custom_call" | custom-call | tf_op jit(solution)/shard_map/core/pallas_call | solution.py:610
  44.4 2.7 %final.1 = (bf16[16,16,48,128]{3,2,1,0:T(8,128)(2,1)}, f32[3,3,3,128]{3,2,1,0:T(4,128)}, f32[1,1]{1,0:T(1,128)}, bf16[768,48]{1,0:T(8,128)(2,1)}) custom-call(f32[64,128]{1,0:T(8,128)S(1)} %get-tuple-element.12.s_ref, f32[16,768,128]{2,1,0:T(8,128)S(1)} %get-tuple-element.13.a_ref, f32[16,768,128]{2,1,0:T(8,128)S(1)} %get-tuple-element.14.b_ref, ...), custom_call_target="tpu_custom_call" | custom-call | tf_op jit(solution)/shard_map/final/pallas_call | solution.py:707

commit v4 on v3

--- a/solution.py
+++ b/solution.py
@@ -105,8 +105,21 @@
     return v[k * 16 : k * 16 + 16]
 
 
+def head_term(head_ref, hg):
+    rr = iota((160, 16), 0)
+    tap = iota((160, 16), 1)
+    y4 = 2 * (rr % 16) + rr // 80
+    x4 = (rr % 80) // 16
+    py = y4 + 1 - tap // 4
+    px = x4 + 1 - tap % 4
+    ok = (py >= 0) & (py <= 29) & (px >= 0) & (px <= 3) & (y4 <= 30)
+    mask = jnp.where(ok, -SCALE, 0.0).astype(BF16)
+    head = jnp.concatenate([head_ref[a].astype(F32) for a in range(4)], 0).astype(BF16)
+    hg[...] = dot(mask, head)
+
+
 def disc_stage(
-    recv_ref, w2_ref, w3_ref, w4_ref, head_ref, out_ref, wait2, wait3, wait4,
+    recv_ref, w2_ref, w3_ref, w4_ref, w4t, t1t, hg, out_ref,
     t1, pp, a1, s1, a2, s2, a3, s3, c4, c3, c2, c1,
 ):
     lane = iota((16, 128), 1)
@@ -136,14 +149,15 @@
         for j in range(3):
             pp[i, :, j * 128 : j * 128 + 128] = (piece[2 * j] + piece[2 * j + 1]).astype(BF16)
     lhs = jnp.concatenate([pp[0:8].reshape(128, 384), pp[1:9].reshape(128, 384)], 1)
-    for v in range(13):
-        pre = dot(lhs, t1[:, v * 128 : v * 128 + 128])
-        act, slope = silu_pair(pre)
-        s1[:, v] = slope.reshape(8, 16, 128)
-        a1[1:9, v] = act.astype(BF16).reshape(8, 16, 128)
-        a1[0, v] = down1(rows16(act, 7)).astype(BF16)
-        a1[9, v] = up1(rows16(act, 0)).astype(BF16)
-    wait2()
+    for v0 in range(0, 13, 2):
+        n = min(2, 13 - v0)
+        pre = dot(lhs, t1[:, v0 * 128 : (v0 + n) * 128])
+        for v in range(v0, v0 + n):
+            act, slope = silu_pair(pre[:, (v - v0) * 128 : (v - v0 + 1) * 128])
+            s1[:, v] = slope.reshape(8, 16, 128)
+            a1[1:9, v] = act.astype(BF16).reshape(8, 16, 128)
+            a1[0, v] = down1(rows16(act, 7)).astype(BF16)
+            a1[9, v] = up1(rows16(act, 0)).astype(BF16)
     zero = jnp.zeros((16, 128), BF16)
     for m in range(6):
         a2[m, 0, 0] = zero
@@ -165,7 +179,6 @@
                 a2[0, e, p] = down1(v).astype(BF16)
             if m == 0:
                 a2[5, e, p] = up1(v).astype(BF16)
-    wait3()
     zero = jnp.zeros((16, 256), BF16)
     for k in range(5):
         a3[k, 0] = zero
@@ -195,7 +208,6 @@
         a3[2, c + 1] = v1.astype(BF16)
         a3[3, c + 1] = up1(v0).astype(BF16)
         a3[4, c + 1] = up1(v1).astype(BF16)
-    wait4()
     acc = None
     for a in range(4):
         lhs = jnp.concatenate(
@@ -208,16 +220,7 @@
         term = dot(lhs, w4_ref[a * 4 : a * 4 + 4].reshape(1024, 512))
         acc = term if acc is None else acc + term
     _, slope = silu_pair(acc)
-    rr = iota((160, 16), 0)
-    tap = iota((160, 16), 1)
-    y4 = 2 * (rr % 16) + rr // 80
-    x4 = (rr % 80) // 16
-    py = y4 + 1 - tap // 4
-    px = x4 + 1 - tap % 4
-    ok = (py >= 0) & (py <= 29) & (px >= 0) & (px <= 3) & (y4 <= 30)
-    mask = jnp.where(ok, -SCALE, 0.0).astype(BF16)
-    head = jnp.concatenate([head_ref[a].astype(F32) for a in range(4)], 0).astype(BF16)
-    cot = dot(mask, head) * slope
+    cot = hg[...] * slope
     zero = jnp.zeros((16, 512), BF16)
     for k in range(5):
         for c in (0, 1, 7, 8):
@@ -240,8 +243,7 @@
             ],
             1,
         )
-        rhs = jnp.concatenate([w4_ref[a * 4 + b] for b in range(4)], 1)
-        term = dot(lhs, rhs, NT)
+        term = dot(lhs, w4t[a * 4 : a * 4 + 4].reshape(2048, 256))
         acc = term if acc is None else acc + term
     cot = acc * s3[...].reshape(192, 256)
     for c in range(6):
@@ -295,7 +297,7 @@
             cot = dot(lhs, rhs, NT) * s1[m].reshape(208, 128)
             for v in range(13):
                 c1[m * 16 : m * 16 + 16, v * 128 : v * 128 + 128] = rows16(cot, v).astype(BF16)
-    grad = dot(c1[...], t1[...], NT)
+    grad = dot(c1[...], t1t[...])
     halves = {}
     for j in range(3):
         ps = []
@@ -355,16 +357,20 @@
         dst[ab * 3 : ab * 3 + 3, :] = acc[k : k + 3, 0:128] + acc[k + 4 : k + 7, 128:256]
 
 
+def drain(ref, sem):
+    pltpu.make_async_copy(ref, ref, sem).wait()
+
+
 class Gather:
     def __init__(self, axis, count, buf, send, got):
         me = lax.axis_index(axis)
-        self.buf, self.me, self.count = buf, me, count
+        self.buf, self.me, self.count, self.sems = buf, me, count, (send, got)
         self.copies = [
             pltpu.make_async_remote_copy(
                 src_ref=buf.at[me],
                 dst_ref=buf.at[me],
-                send_sem=send.at[d],
-                recv_sem=got.at[d],
+                send_sem=send,
+                recv_sem=got,
                 device_id={axis: lax.rem(me + d, count)},
                 device_id_type=MESH,
             )
@@ -377,46 +383,64 @@
             c.start()
 
     def finish(self):
-        for c in self.copies:
-            c.wait()
+        for sem in self.sems:
+            drain(self.buf.at[pl.ds(0, self.count - 1)], sem)
         parts = [self.buf[k] for k in range(self.count)]
         while len(parts) > 1:
             parts = [a + b for a, b in zip(parts[::2], parts[1::2])]
         return parts[0]
 
 
-def row_exchange(src, dst, send, got, own):
-    r = lax.axis_index("row")
-    local = pltpu.make_async_copy(src.at[r], dst.at[r], own)
-    copies = [local]
-    for d in range(1, FR):
-        peer = lax.rem(r + d, FR)
-        copies.append(
+class RowExchange:
+    def __init__(self, src, dst, send, got):
+        r = lax.axis_index("row")
+        self.src, self.dst, self.send, self.got = src, dst, send, got
+        self.copies = [pltpu.make_async_copy(src.at[r], dst.at[r], got)]
+        for d in range(1, FR):
+            peer = lax.rem(r + d, FR)
+            self.copies.append(
+                pltpu.make_async_remote_copy(
+                    src_ref=src.at[peer],
+                    dst_ref=dst.at[r],
+                    send_sem=send,
+                    recv_sem=got,
+                    device_id={"row": peer},
+                    device_id_type=MESH,
+                )
+            )
+
+    def start(self):
+        for c in self.copies:
+            c.start()
+
+    def wait(self):
+        drain(self.dst, self.got)
+        drain(self.src.at[pl.ds(0, FR - 1)], self.send)
+
+
+class EdgeExchange:
+    def __init__(self, src, dst, send, got):
+        r = lax.axis_index("row")
+        self.src, self.dst, self.send, self.got = src, dst, send, got
+        self.copies = [
             pltpu.make_async_remote_copy(
-                src_ref=src.at[peer],
-                dst_ref=dst.at[r],
-                send_sem=send.at[d],
-                recv_sem=got.at[d],
-                device_id={"row": peer},
+                src_ref=src.at[k],
+                dst_ref=dst.at[1 - k],
+                send_sem=send,
+                recv_sem=got,
+                device_id={"row": lax.rem(r + d, FR)},
                 device_id_type=MESH,
             )
-        )
-    return copies
-
-
-def edge_exchange(src, dst, send, got):
-    r = lax.axis_index("row")
-    return [
-        pltpu.make_async_remote_copy(
-            src_ref=src.at[k],
-            dst_ref=dst.at[1 - k],
-            send_sem=send.at[k],
-            recv_sem=got.at[k],
-            device_id={"row": lax.rem(r + d, FR)},
-            device_id_type=MESH,
-        )
-        for d, k in ((FR - 1, 0), (1, 1))
-    ]
+            for d, k in ((FR - 1, 0), (1, 1))
+        ]
+
+    def start(self):
+        for c in self.copies:
+            c.start()
+
+    def wait(self):
+        drain(self.dst, self.got)
+        drain(self.src, self.send)
 
 
 def start_all(copies):
@@ -434,10 +458,9 @@
     w_hbm, f_hbm, t_hbm, w1_hbm, w2_hbm, w3_hbm, w4_hbm, head_hbm,
     sums_ref, a_ref, b_ref, back_ref,
     fs, w_ref, t_ref, w1_ref, w2s, w3s, w4s, head_ref, wm, parts, edges, recv, nb, wide, want, rec, redges, ne, msg, gan,
-    gg, xsum, clip_buf, row_buf,
+    gg, gts, xsum, clip_buf, row_buf, w4t, t1t, hg,
     t1, pp, a1, s1, a2, s2, a3, s3, c4, c3, c2, c1,
-    fsem, wsem, own, send0, got0, send1, got1, esend0, egot0, esend1, egot1,
-    csend, cgot, rsend, rgot,
+    fsem, wsem, xsem,
 ):
     r = lax.axis_index("row")
     clip = lax.axis_index("clip")
@@ -450,7 +473,10 @@
         pl.semaphore_signal(
             barrier, inc=1, device_id={"clip": lax.rem(clip + d, clips)}, device_id_type=MESH
         )
-    loads = [pltpu.make_async_copy(f_hbm.at[f], fs.at[f], fsem.at[f]) for f in range(FR)]
+    loads = [
+        pltpu.make_async_copy(f_hbm.at[pl.ds(4 * k, 4)], fs.at[pl.ds(4 * k, 4)], fsem)
+        for k in range(4)
+    ]
     weights = [
         pltpu.make_async_copy(a, b, wsem.at[k])
         for k, (a, b) in enumerate(
@@ -461,10 +487,7 @@
         )
     ]
     weights[6].start()
-    for p in range(8):
-        loads[p].start()
-        loads[p + 8].start()
-    start_all(weights[3:6])
+    start_all(loads)
     weights[6].wait()
 
     wm[...] = jnp.zeros_like(wm)
@@ -482,12 +505,10 @@
     def pair_features(p):
         return jnp.concatenate([fs[p].reshape(768, 128), fs[p + 8].reshape(768, 128)], 1)
 
+    drain(fs, fsem)
+    start_all(weights[0:6])
     for p in range(8):
-        loads[p].wait()
-        loads[p + 8].wait()
-        if p == 5:
-            start_all(weights[0:3])
-        out = dot(wmb, pair_features(p), NT)
+        out = dot(pair_features(p), wmb, NT).T
         total = None
         for ab in range(9):
             a, b = ab // 3, ab % 3
@@ -503,10 +524,10 @@
                     for o in range(3):
                         edges[t // 6, o, f : f + 1, :] = tile[o : o + 1, :]
     pl.semaphore_wait(barrier, FR + clips - 2)
-    first = row_exchange(parts, recv, send0, got0, own.at[0])
-    ends = edge_exchange(edges, nb, esend0, egot0)
-    start_all(ends)
-    start_all(first)
+    first = RowExchange(parts, recv, xsem.at[0], xsem.at[1])
+    ends = EdgeExchange(edges, nb, xsem.at[2], xsem.at[3])
+    ends.start()
+    first.start()
 
     weights[4].wait()
     build_band(w1_ref, t1)
@@ -519,7 +540,7 @@
         for t in range(7):
             want[t, o] = tiles[t]
     flat = parts.reshape(FR * 24, 128)
-    wait_all(ends)
+    ends.wait()
     for o in range(3):
         for t in range(7):
             v = flat[pl.ds(3 * t + o, 16, stride=24), :]
@@ -535,21 +556,25 @@
             rec[t, o] = v
             if t in (0, 6):
                 redges[t // 6, o] = v
-    rends = edge_exchange(redges, ne, esend1, egot1)
-    start_all(rends)
-    wait_all(first)
-    weights[3].wait()
+    rends = EdgeExchange(redges, ne, xsem.at[4], xsem.at[5])
+    rends.start()
+    wait_all(weights[0:4])
+    head_term(head_ref, hg)
+    for k in range(16):
+        w4t[k] = w4s[k].T
+    for k in range(6):
+        t1t[:, k * 128 : k * 128 + 128] = t1[k * 128 : k * 128 + 128, :].T
+    first.wait()
 
     disc_stage(
-        recv.reshape(FR * 24, 128), w2s, w3s, w4s, head_ref, msg.reshape(FR * 24, 128),
-        weights[0].wait, weights[1].wait, weights[2].wait,
+        recv.reshape(FR * 24, 128), w2s, w3s, w4s, w4t, t1t, hg, msg.reshape(FR * 24, 128),
         t1, pp, a1, s1, a2, s2, a3, s3, c4, c3, c2, c1,
     )
-    second = row_exchange(msg, gan, send1, got1, own.at[1])
-    start_all(second)
+    second = RowExchange(msg, gan, xsem.at[6], xsem.at[7])
+    second.start()
 
     gg[...] = jnp.zeros_like(gg)
-    wait_all(rends)
+    rends.wait()
 
     def put(k, t, o, v):
         gg[k, pl.ds(t * 8 + o, 8, stride=56), :] = v[0:8]
@@ -564,36 +589,42 @@
                 v = v + jnp.where((lane >= W) & (lane < 2 * W) & (r < FR - 1), ne[1, o], 0.0)
             put(0, t, o, v)
 
-    def weight_part(k, p, acc, part_ref):
+    def weight_part(k, p, acc):
         g = jnp.concatenate([gg[k, p * 56 + t * 8 : p * 56 + t * 8 + 8, :] for t in range(7)], 1)
         gt = shifted(g, col)
-        out = dot(gt, wmb, TN)
-        part_ref[p] = out[:, 0:128]
-        part_ref[p + 8] = out[:, 128:256]
+        gts[p] = gt
         term = dot(gt, pair_features(p))
         return term if acc is None else acc + term
 
+    def feature_part(part_ref):
+        for p in range(8):
+            out = dot(gts[p], wmb, TN)
+            part_ref[p] = out[:, 0:128]
+            part_ref[p + 8] = out[:, 128:256]
+
     acc = None
     for p in range(8):
-        acc = weight_part(0, p, acc, a_ref)
+        acc = weight_part(0, p, acc)
     compact(xsum, acc)
-    rec_clip = Gather("clip", clips, clip_buf.at[0], csend.at[0], cgot.at[0])
-    rec_row = Gather("row", FR, row_buf.at[0], rsend.at[0], rgot.at[0])
-    gan_clip = Gather("clip", clips, clip_buf.at[1], csend.at[1], cgot.at[1])
-    gan_row = Gather("row", FR, row_buf.at[1], rsend.at[1], rgot.at[1])
+    rec_clip = Gather("clip", clips, clip_buf.at[0], xsem.at[8], xsem.at[9])
+    rec_row = Gather("row", FR, row_buf.at[0], xsem.at[10], xsem.at[11])
+    gan_clip = Gather("clip", clips, clip_buf.at[1], xsem.at[12], xsem.at[13])
+    gan_row = Gather("row", FR, row_buf.at[1], xsem.at[14], xsem.at[15])
     rec_clip.start(xsum[...])
-
-    wait_all(second)
+    feature_part(a_ref)
+
+    second.wait()
     flat = gan.reshape(FR * 24, 128)
     for o in range(3):
         for t in range(7):
             put(1, t, o, flat[pl.ds(3 * t + o, 16, stride=24), :])
     acc = None
     for p in range(8):
-        acc = weight_part(1, p, acc, b_ref)
+        acc = weight_part(1, p, acc)
     compact(xsum, acc)
     gan_clip.start(xsum[...])
     rec_row.start(rec_clip.finish())
+    feature_part(b_ref)
     for o in range(3):
         tiles = [flat[pl.ds(3 * t + o, 16, stride=24), :] for t in range(7)]
         for y in range(16):
@@ -639,9 +670,13 @@
             VM((FR, 24, 128), F32),
             VM((FR, 24, 128), F32),
             VM((2, 448, 128), F32),
+            VM((8, 80, 768), BF16),
             VM((32, 128), F32),
             VM((2, clips, 32, 128), F32),
             VM((2, FR, 32, 128), F32),
+            VM((16, 512, 256), BF16),
+            VM((1664, 768), BF16),
+            VM((160, 512), F32),
             VM((768, 1664), BF16),
             VM((9, 16, 384), BF16),
             VM((10, 13, 16, 128), BF16),
@@ -654,24 +689,12 @@
             VM((4, 8, 16, 256), BF16),
             VM((6, 14, 16, 128), BF16),
             VM((128, 1664), BF16),
-            dma((FR,)),
+            dma,
             dma((7,)),
-            dma((2,)),
-            dma((FR,)),
-            dma((FR,)),
-            dma((FR,)),
-            dma((FR,)),
-            dma((2,)),
-            dma((2,)),
-            dma((2,)),
-            dma((2,)),
-            dma((2, clips)),
-            dma((2, clips)),
-            dma((2, FR)),
-            dma((2, FR)),
+            dma((16,)),
         ],
         compiler_params=pltpu.CompilerParams(
-            collective_id=0, has_side_effects=True, vmem_limit_bytes=36 << 20
+            collective_id=0, has_side_effects=True, vmem_limit_bytes=44 << 20
         ),
         name="core",
     )(

time: 47.6 us -> 42.7 us (0.90)
  Pallas kernels: 46.4 us -> 41.7 us
    pallas_call x1, Pallas kernels: 43.7 us -> 39 us  [core(): pl.pallas_call(functools.partial(core_body, clips), out_shape=(VM((64, 12...]
where the time goes in v4:
time: 42.7 us; the launch traced here: 42.3 us
  Pallas kernels  41.7 us (98%)
  between operations  0.64 us (1%)
    pallas_call x1, Pallas kernels, core(): pl.pallas_call(functools.partial(core_body, clips), out_shape=(VM((64, 12...  39 us
    pallas_call x1, Pallas kernels, final(): pl.pallas_call(functools.partial(final_body, pixels), out_shape=(jax.Shap...  2.69 us

profile of v4, /device:TPU:1, one launch (start us, length us, event | category | flops | bytes accessed | tf_op | source)
XLA Modules:
  0.0 42.3 jit_solution(14516846986886059314)
XLA Ops:
  0.6 39.0 %core.1 = (f32[64,128]{1,0:T(8,128)S(1)}, f32[16,768,128]{2,1,0:T(8,128)S(1)}, f32[16,768,128]{2,1,0:T(8,128)S(1)}, bf16[768,48]{1,0:T(8,128)(2,1)S(1)}) custom-call(bf16[3,3,3,128]{3,2,1,0:T(4,128)(2,1)} %w_hbm.1, bf16[16,16,48,128]{3,2,1,0:T(8,128)(2,1)} %bitcast.17, bf16[768,48]{1,0:T(8,128)(2,1)} %bitcast.20, bf16[4,3,4,64]{3,2,1,0:T(4,128)(2,1)} %bitcast.22, ...), custom_call_target="tpu_custom_call" | custom-call | tf_op jit(solution)/shard_map/core/pallas_call | solution.py:641
  39.6 2.7 %final.1 = (bf16[16,16,48,128]{3,2,1,0:T(8,128)(2,1)}, f32[3,3,3,128]{3,2,1,0:T(4,128)}, f32[1,1]{1,0:T(1,128)}, bf16[768,48]{1,0:T(8,128)(2,1)}) custom-call(f32[64,128]{1,0:T(8,128)S(1)} %get-tuple-element.12.s_ref, f32[16,768,128]{2,1,0:T(8,128)S(1)} %get-tuple-element.13.a_ref, f32[16,768,128]{2,1,0:T(8,128)S(1)} %get-tuple-element.14.b_ref, ...), custom_call_target="tpu_custom_call" | custom-call | tf_op jit(solution)/shard_map/final/pallas_call | solution.py:730

commit v5 on v4

--- a/solution.py
+++ b/solution.py
@@ -125,8 +125,9 @@
     lane = iota((16, 128), 1)
     x = []
     for o in range(3):
-        tiles = [recv_ref[pl.ds(3 * t + o, 16, stride=24), :] for t in range(7)]
-        first, last = tiles[0], tiles[6]
+        tiles = [recv_ref[pl.ds(3 * t + o, 16, stride=32), :] for t in range(7)]
+        first = tiles[0] + recv_ref[pl.ds(21 + o, 16, stride=32), :]
+        last = tiles[6] + recv_ref[pl.ds(24 + o, 16, stride=32), :]
         tiles[0] = first + jnp.where((lane >= W) & (lane < 2 * W), down1(last), 0.0)
         tiles[6] = last + jnp.where(lane < W, up1(first), 0.0)
         x.append([rnd(v) for v in tiles])
@@ -329,9 +330,7 @@
         tiles[0] = first + jnp.where(lane < W, down1(last), 0.0)
         tiles[6] = last + jnp.where((lane >= W) & (lane < 2 * W), up1(first), 0.0)
         for t in range(7):
-            out_ref[pl.ds(3 * t + o, 16, stride=24), :] = tiles[t]
-    for k in range(21, 24):
-        out_ref[pl.ds(k, 16, stride=24), :] = jnp.zeros((16, 128), F32)
+            out_ref[pl.ds(4 * t + o, 16, stride=32), :] = tiles[t]
 
 def edge_mask(v, b, col):
     if b == 0:
@@ -361,61 +360,89 @@
     pltpu.make_async_copy(ref, ref, sem).wait()
 
 
-class Gather:
-    def __init__(self, axis, count, buf, send, got):
-        me = lax.axis_index(axis)
-        self.buf, self.me, self.count, self.sems = buf, me, count, (send, got)
-        self.copies = [
-            pltpu.make_async_remote_copy(
-                src_ref=buf.at[me],
-                dst_ref=buf.at[me],
-                send_sem=send,
-                recv_sem=got,
-                device_id={axis: lax.rem(me + d, count)},
-                device_id_type=MESH,
-            )
-            for d in range(1, count)
-        ]
-
-    def start(self, value):
-        self.buf[self.me] = value
-        for c in self.copies:
-            c.start()
-
-    def finish(self):
-        for sem in self.sems:
-            drain(self.buf.at[pl.ds(0, self.count - 1)], sem)
-        parts = [self.buf[k] for k in range(self.count)]
-        while len(parts) > 1:
-            parts = [a + b for a, b in zip(parts[::2], parts[1::2])]
-        return parts[0]
-
-
-class RowExchange:
-    def __init__(self, src, dst, send, got):
-        r = lax.axis_index("row")
-        self.src, self.dst, self.send, self.got = src, dst, send, got
-        self.copies = [pltpu.make_async_copy(src.at[r], dst.at[r], got)]
-        for d in range(1, FR):
-            peer = lax.rem(r + d, FR)
-            self.copies.append(
+def hops(d):
+    return min(d, 4 - d)
+
+
+ROW_OFFSETS = sorted(
+    ((dy, dz) for dy in range(4) for dz in range(4) if dy or dz),
+    key=lambda t: -(hops(t[0]) + hops(t[1])),
+)
+CLIP_OFFSETS = sorted(
+    ((dx, dc) for dx in range(4) for dc in range(2) if dx or dc), key=lambda t: -(2 * hops(t[0]) + t[1])
+)
+
+
+def row_peers():
+    r = lax.axis_index("row")
+    y, z = r // 4, lax.rem(r, 4)
+    return [lax.rem(y + dy, 4) * 4 + lax.rem(z + dz, 4) for dy, dz in ROW_OFFSETS]
+
+
+def tree(parts):
+    while len(parts) > 1:
+        parts = [a + b for a, b in zip(parts[::2], parts[1::2])]
+    return parts[0]
+
+
+class Total:
+    def __init__(self, src, clip_buf, row_buf, out, sems):
+        clip, row = lax.axis_index("clip"), lax.axis_index("row")
+        x, core = clip // 2, lax.rem(clip, 2)
+        self.src, self.clip_buf, self.row_buf, self.out, self.sems = src, clip_buf, row_buf, out, sems
+        self.clip, self.row = clip, row
+        self.half = pl.ds(pl.multiple_of(core * 16, 16), 16)
+        self.first = []
+        for dx, dc in CLIP_OFFSETS:
+            other = lax.rem(core + dc, 2)
+            self.first.append(
                 pltpu.make_async_remote_copy(
-                    src_ref=src.at[peer],
-                    dst_ref=dst.at[r],
-                    send_sem=send,
-                    recv_sem=got,
-                    device_id={"row": peer},
+                    src_ref=src.at[pl.ds(pl.multiple_of(other * 16, 16), 16)],
+                    dst_ref=clip_buf.at[clip],
+                    send_sem=sems.at[0],
+                    recv_sem=sems.at[1],
+                    device_id={"clip": lax.rem(x + dx, 4) * 2 + other},
                     device_id_type=MESH,
                 )
             )
+        self.second = [
+            pltpu.make_async_remote_copy(
+                src_ref=row_buf.at[row],
+                dst_ref=row_buf.at[row],
+                send_sem=sems.at[2],
+                recv_sem=sems.at[3],
+                device_id={"row": peer},
+                device_id_type=MESH,
+            )
+            for peer in row_peers()
+        ]
+        self.third = pltpu.make_async_remote_copy(
+            src_ref=out.at[self.half],
+            dst_ref=out.at[self.half],
+            send_sem=sems.at[4],
+            recv_sem=sems.at[5],
+            device_id={"clip": x * 2 + 1 - core},
+            device_id_type=MESH,
+        )
 
     def start(self):
-        for c in self.copies:
-            c.start()
-
-    def wait(self):
-        drain(self.dst, self.got)
-        drain(self.src.at[pl.ds(0, FR - 1)], self.send)
+        start_all(self.first)
+        self.clip_buf[self.clip] = self.src[self.half, :]
+
+    def middle(self):
+        for k in (1, 0):
+            drain(self.clip_buf.at[pl.ds(0, 7)], self.sems.at[k])
+        self.row_buf[self.row] = tree([self.clip_buf[k] for k in range(8)])
+        start_all(self.second)
+
+    def trade(self):
+        for k in (3, 2):
+            drain(self.row_buf.at[pl.ds(0, FR - 1)], self.sems.at[k])
+        self.out[self.half, :] = tree([self.row_buf[k] for k in range(FR)])
+        self.third.start()
+
+    def finish(self):
+        self.third.wait()
 
 
 class EdgeExchange:
@@ -454,28 +481,39 @@
 
 
 def core_body(
-    clips,
     w_hbm, f_hbm, t_hbm, w1_hbm, w2_hbm, w3_hbm, w4_hbm, head_hbm,
     sums_ref, a_ref, b_ref, back_ref,
-    fs, w_ref, t_ref, w1_ref, w2s, w3s, w4s, head_ref, wm, parts, edges, recv, nb, wide, want, rec, redges, ne, msg, gan,
+    fs, w_ref, t_ref, w1_ref, w2s, w3s, w4s, head_ref, wm, parts, parts16, edges, recv, recvf, nb, wide, want, rec,
+    redges, ne, msg, msgf, gan,
     gg, gts, xsum, clip_buf, row_buf, w4t, t1t, hg,
     t1, pp, a1, s1, a2, s2, a3, s3, c4, c3, c2, c1,
-    fsem, wsem, xsem,
+    fsem, wsem, xsem, gsem, tsem,
 ):
     r = lax.axis_index("row")
     clip = lax.axis_index("clip")
+    y, z = r // 4, lax.rem(r, 4)
     barrier = pltpu.get_barrier_semaphore()
     for d in range(1, FR):
         pl.semaphore_signal(
             barrier, inc=1, device_id={"row": lax.rem(r + d, FR)}, device_id_type=MESH
         )
+    clips = 8
     for d in range(1, clips):
         pl.semaphore_signal(
             barrier, inc=1, device_id={"clip": lax.rem(clip + d, clips)}, device_id_type=MESH
         )
+    pairs = [
+        [yy * 4 + lax.rem(z + dz, 4) for dz in dzs for yy in range(2)] for dzs in ((2,), (1, 3))
+    ]
+    ys = lax.rem(y, 2)
+    pairs.append([(1 - ys) * 4 + z, ys * 4 + z])
     loads = [
-        pltpu.make_async_copy(f_hbm.at[pl.ds(4 * k, 4)], fs.at[pl.ds(4 * k, 4)], fsem)
-        for k in range(4)
+        [
+            pltpu.make_async_copy(f_hbm.at[f], fs.at[f], fsem.at[k])
+            for p in group
+            for f in (p, p + 8)
+        ]
+        for k, group in enumerate(pairs)
     ]
     weights = [
         pltpu.make_async_copy(a, b, wsem.at[k])
@@ -487,7 +525,8 @@
         )
     ]
     weights[6].start()
-    start_all(loads)
+    for group in loads:
+        start_all(group)
     weights[6].wait()
 
     wm[...] = jnp.zeros_like(wm)
@@ -499,35 +538,57 @@
     col = iota((8, 768), 1) % W
     lane = iota((16, 128), 1)
     pad = jnp.zeros((8, 128), F32)
-    for k in range(21, 24):
+    for k in range(27, 32):
         parts[:, k, :] = jnp.zeros((FR, 128), F32)
 
     def pair_features(p):
         return jnp.concatenate([fs[p].reshape(768, 128), fs[p + 8].reshape(768, 128)], 1)
 
-    drain(fs, fsem)
-    start_all(weights[0:6])
-    for p in range(8):
-        out = dot(pair_features(p), wmb, NT).T
-        total = None
-        for ab in range(9):
-            a, b = ab // 3, ab % 3
-            g = edge_mask(out[ab * 8 : ab * 8 + 8, :], b, col)
-            g = lroll(jnp.concatenate([g, pad], 1), (2 - a) * W + 1 - b)
-            total = g if total is None else total + g
-        for h in range(2):
-            f = p + 8 * h
-            for t in range(7):
-                tile = total[4 * h : 4 * h + 3, t * 128 : t * 128 + 128]
-                parts[f, 3 * t : 3 * t + 3, :] = tile
-                if t in (0, 6):
-                    for o in range(3):
-                        edges[t // 6, o, f : f + 1, :] = tile[o : o + 1, :]
-    pl.semaphore_wait(barrier, FR + clips - 2)
-    first = RowExchange(parts, recv, xsem.at[0], xsem.at[1])
+    def send_images(f):
+        pltpu.make_async_remote_copy(
+            src_ref=parts16.at[f],
+            dst_ref=recv.at[r],
+            send_sem=xsem.at[0],
+            recv_sem=xsem.at[1],
+            device_id={"row": f},
+            device_id_type=MESH,
+        ).start()
+
+    for k, group in enumerate(pairs):
+        drain(fs.at[pl.ds(0, 2 * len(group))], fsem.at[k])
+        if k == 2:
+            start_all(weights[0:6])
+        for p in group:
+            out = dot(pair_features(p), wmb, NT).T
+            total = None
+            for ab in range(9):
+                a, b = ab // 3, ab % 3
+                g = edge_mask(out[ab * 8 : ab * 8 + 8, :], b, col)
+                g = lroll(jnp.concatenate([g, pad], 1), (2 - a) * W + 1 - b)
+                total = g if total is None else total + g
+            for h in range(2):
+                f = p + 8 * h
+                for t in range(7):
+                    tile = total[4 * h : 4 * h + 3, t * 128 : t * 128 + 128]
+                    parts[f, 3 * t : 3 * t + 3, :] = tile
+                    if t in (0, 6):
+                        parts[f, 21 + t // 2 : 24 + t // 2, :] = tile - rnd(tile)
+                parts16[f] = parts[f].astype(BF16)
+        if k == 0:
+            pl.semaphore_wait(barrier, FR + clips - 2)
+        for p in group:
+            if k < 2 or p is group[0]:
+                send_images(p)
+                send_images(p + 8)
+    send_images(lax.rem(r + 8, FR))
+    own = pltpu.make_async_copy(parts16.at[r], recv.at[r], xsem.at[1])
+    own.start()
+    flat = parts.reshape(FR * 32, 128)
+    for t in (0, 6):
+        for o in range(3):
+            edges[t // 6, o] = flat[pl.ds(3 * t + o, 16, stride=32), :]
     ends = EdgeExchange(edges, nb, xsem.at[2], xsem.at[3])
     ends.start()
-    first.start()
 
     weights[4].wait()
     build_band(w1_ref, t1)
@@ -539,11 +600,17 @@
             spread(tiles, lane, wide[pl.ds(o * 16 + y, 16, stride=48), :], 0, W * (y + 1))
         for t in range(7):
             want[t, o] = tiles[t]
-    flat = parts.reshape(FR * 24, 128)
+    msgf[...] = jnp.zeros_like(msgf)
+    wait_all(weights[0:4])
+    head_term(head_ref, hg)
+    for k in range(16):
+        w4t[k] = w4s[k].T
+    for k in range(6):
+        t1t[:, k * 128 : k * 128 + 128] = t1[k * 128 : k * 128 + 128, :].T
     ends.wait()
     for o in range(3):
         for t in range(7):
-            v = flat[pl.ds(3 * t + o, 16, stride=24), :]
+            v = flat[pl.ds(3 * t + o, 16, stride=32), :]
             if t == 0:
                 v = v + jnp.where((lane >= W) & (lane < 2 * W) & (r > 0), nb[0, o], 0.0)
             if t == 6:
@@ -558,27 +625,28 @@
                 redges[t // 6, o] = v
     rends = EdgeExchange(redges, ne, xsem.at[4], xsem.at[5])
     rends.start()
-    wait_all(weights[0:4])
-    head_term(head_ref, hg)
-    for k in range(16):
-        w4t[k] = w4s[k].T
-    for k in range(6):
-        t1t[:, k * 128 : k * 128 + 128] = t1[k * 128 : k * 128 + 128, :].T
-    first.wait()
+    drain(recv, xsem.at[1])
+    drain(parts16.at[pl.ds(0, FR - 1)], xsem.at[0])
+    recvf[...] = recv.reshape(FR * 32, 128)[...].astype(F32)
 
     disc_stage(
-        recv.reshape(FR * 24, 128), w2s, w3s, w4s, w4t, t1t, hg, msg.reshape(FR * 24, 128),
+        recvf, w2s, w3s, w4s, w4t, t1t, hg, msgf,
         t1, pp, a1, s1, a2, s2, a3, s3, c4, c3, c2, c1,
     )
-    second = RowExchange(msg, gan, xsem.at[6], xsem.at[7])
-    second.start()
+    msg.reshape(FR * 32, 128)[...] = msgf[...].astype(BF16)
+    for peer in row_peers():
+        pltpu.make_async_remote_copy(
+            src_ref=msg.at[peer],
+            dst_ref=gan.at[r],
+            send_sem=xsem.at[6],
+            recv_sem=gsem.at[r],
+            device_id={"row": peer},
+            device_id_type=MESH,
+        ).start()
+    pltpu.make_async_copy(msg.at[r], gan.at[r], gsem.at[r]).start()
 
     gg[...] = jnp.zeros_like(gg)
     rends.wait()
-
-    def put(k, t, o, v):
-        gg[k, pl.ds(t * 8 + o, 8, stride=56), :] = v[0:8]
-        gg[k, pl.ds(t * 8 + 4 + o, 8, stride=56), :] = v[8:16]
 
     for o in range(3):
         for t in range(7):
@@ -587,10 +655,10 @@
                 v = v + jnp.where((lane < W) & (r > 0), ne[0, o], 0.0)
             if t == 6:
                 v = v + jnp.where((lane >= W) & (lane < 2 * W) & (r < FR - 1), ne[1, o], 0.0)
-            put(0, t, o, v)
-
-    def weight_part(k, p, acc):
-        g = jnp.concatenate([gg[k, p * 56 + t * 8 : p * 56 + t * 8 + 8, :] for t in range(7)], 1)
+            gg[pl.ds(t * 8 + o, 8, stride=56), :] = v[0:8]
+            gg[pl.ds(t * 8 + 4 + o, 8, stride=56), :] = v[8:16]
+
+    def weight_part(g, p, acc):
         gt = shifted(g, col)
         gts[p] = gt
         term = dot(gt, pair_features(p))
@@ -602,44 +670,56 @@
             part_ref[p] = out[:, 0:128]
             part_ref[p + 8] = out[:, 128:256]
 
+    rec_total = Total(xsum.at[0], clip_buf.at[0], row_buf.at[0], sums_ref.at[pl.ds(0, 32)], tsem.at[0])
+    gan_total = Total(xsum.at[1], clip_buf.at[1], row_buf.at[1], sums_ref.at[pl.ds(32, 32)], tsem.at[1])
     acc = None
     for p in range(8):
-        acc = weight_part(0, p, acc)
-    compact(xsum, acc)
-    rec_clip = Gather("clip", clips, clip_buf.at[0], xsem.at[8], xsem.at[9])
-    rec_row = Gather("row", FR, row_buf.at[0], xsem.at[10], xsem.at[11])
-    gan_clip = Gather("clip", clips, clip_buf.at[1], xsem.at[12], xsem.at[13])
-    gan_row = Gather("row", FR, row_buf.at[1], xsem.at[14], xsem.at[15])
-    rec_clip.start(xsum[...])
+        g = jnp.concatenate([gg[p * 56 + t * 8 : p * 56 + t * 8 + 8, :] for t in range(7)], 1)
+        acc = weight_part(g, p, acc)
+    compact(xsum.at[0], acc)
+    rec_total.start()
     feature_part(a_ref)
 
-    second.wait()
-    flat = gan.reshape(FR * 24, 128)
+    low = iota((8, 128), 0) < 4
+    acc = None
+    for group in pairs[::-1]:
+        for p in group:
+            for f in (p, p + 8):
+                drain(gan.at[f], gsem.at[f])
+        for p in group:
+            va, vb = gan[p].astype(F32), gan[p + 8].astype(F32)
+            ua, ub = pltpu.roll(va, 28, 0), pltpu.roll(vb, 4, 0)
+            tiles = []
+            for t in range(7):
+                k = t // 2 * 8
+                if t % 2 == 0:
+                    tiles.append(jnp.where(low, va[k : k + 8], ub[k : k + 8]))
+                else:
+                    tiles.append(jnp.where(low, ua[k : k + 8], vb[k : k + 8]))
+            acc = weight_part(jnp.concatenate(tiles, 1), p, acc)
+    compact(xsum.at[1], acc)
+    gan_total.start()
+    rec_total.middle()
+    feature_part(b_ref)
+    drain(msg.at[pl.ds(0, FR - 1)], xsem.at[6])
+    msgf[...] = gan.reshape(FR * 32, 128)[...].astype(F32)
     for o in range(3):
-        for t in range(7):
-            put(1, t, o, flat[pl.ds(3 * t + o, 16, stride=24), :])
-    acc = None
-    for p in range(8):
-        acc = weight_part(1, p, acc)
-    compact(xsum, acc)
-    gan_clip.start(xsum[...])
-    rec_row.start(rec_clip.finish())
-    feature_part(b_ref)
-    for o in range(3):
-        tiles = [flat[pl.ds(3 * t + o, 16, stride=24), :] for t in range(7)]
+        tiles = [msgf[pl.ds(4 * t + o, 16, stride=32), :] for t in range(7)]
         for y in range(16):
             wide[pl.ds(o * 16 + y, 16, stride=48), :] = place(tiles, lane, W * (y + 1), 0)
     back_ref[...] = wide[:, 0:W].astype(BF16)
-    gan_row.start(gan_clip.finish())
-    sums_ref[0:32] = rec_row.finish()
-    sums_ref[32:64] = gan_row.finish()
-
-
-def core(clips, conv_weight, features, target, w1, w2, w3, w4, head):
+    gan_total.middle()
+    rec_total.trade()
+    rec_total.finish()
+    gan_total.trade()
+    gan_total.finish()
+
+
+def core(conv_weight, features, target, w1, w2, w3, w4, head):
     hbm = lambda: pl.BlockSpec(memory_space=pltpu.HBM)
     dma = pltpu.SemaphoreType.DMA
     return pl.pallas_call(
-        functools.partial(core_body, clips),
+        core_body,
         out_shape=(
             VM((64, 128), F32),
             VM((FR, 768, 128), F32),
@@ -658,22 +738,25 @@
             VM((16, 256, 512), BF16),
             VM((4, 4, 512), BF16),
             VM((80, 256), F32),
-            VM((FR, 24, 128), F32),
+            VM((FR, 32, 128), F32),
+            VM((FR, 32, 128), BF16),
             VM((2, 3, FR, 128), F32),
-            VM((FR, 24, 128), F32),
+            VM((FR, 32, 128), BF16),
+            VM((FR * 32, 128), F32),
             VM((2, 3, FR, 128), F32),
             VM((768, 128), F32),
             VM((7, 3, FR, 128), F32),
             VM((7, 3, FR, 128), F32),
             VM((2, 3, FR, 128), F32),
             VM((2, 3, FR, 128), F32),
-            VM((FR, 24, 128), F32),
-            VM((FR, 24, 128), F32),
-            VM((2, 448, 128), F32),
+            VM((FR, 32, 128), BF16),
+            VM((FR * 32, 128), F32),
+            VM((FR, 32, 128), BF16),
+            VM((448, 128), F32),
             VM((8, 80, 768), BF16),
-            VM((32, 128), F32),
-            VM((2, clips, 32, 128), F32),
-            VM((2, FR, 32, 128), F32),
+            VM((2, 32, 128), F32),
+            VM((2, 8, 16, 128), F32),
+            VM((2, FR, 16, 128), F32),
             VM((16, 512, 256), BF16),
             VM((1664, 768), BF16),
             VM((160, 512), F32),
@@ -689,9 +772,11 @@
             VM((4, 8, 16, 256), BF16),
             VM((6, 14, 16, 128), BF16),
             VM((128, 1664), BF16),
-            dma,
+            dma((3,)),
             dma((7,)),
-            dma((16,)),
+            dma((8,)),
+            dma((FR,)),
+            dma((2, 6)),
         ],
         compiler_params=pltpu.CompilerParams(
             collective_id=0, has_side_effects=True, vmem_limit_bytes=44 << 20
@@ -754,7 +839,7 @@
     w4 = disc_fourth.reshape(16, 256, 512)
     head = disc_head.reshape(4, 4, 512)
     pixels = float(clips * FR * 256 * W)
-    sums, a, b, back = core(clips, conv_weight, features[0], wanted, w1, w2, w3, w4, head)
+    sums, a, b, back = core(conv_weight, features[0], wanted, w1, w2, w3, w4, head)
     feature_grad, weight_grad, adaptive, back = final(sums, a, b, back, pixels)
     image_back = jnp.transpose(back.reshape(1, FR, 3, 16, W), (0, 1, 3, 2, 4))
     return (feature_grad[None], image_back, weight_grad, adaptive[0, 0])

time: 42.7 us -> 41.7 us (0.977)
  Pallas kernels: 41.7 us -> 40.7 us
    pallas_call x1, Pallas kernels: 39 us -> 38.1 us  [core(): pl.pallas_call(core_body, out_shape=(VM((64, 128), F32), VM((FR, 768, 128...]
where the time goes in v5:
time: 41.7 us; the launch traced here: 41.6 us
  Pallas kernels  40.7 us (98%)
  between operations  0.8 us (2%)
    pallas_call x1, Pallas kernels, core(): pl.pallas_call(core_body, out_shape=(VM((64, 128), F32), VM((FR, 768, 128...  38.1 us
    pallas_call x1, Pallas kernels, final(): pl.pallas_call(functools.partial(final_body, pixels), out_shape=(jax.Shap...  2.69 us

profile of v5, /device:TPU:1, one launch (start us, length us, event | category | flops | bytes accessed | tf_op | source)
XLA Modules:
  0.0 41.6 jit_solution(8575489434760226835)
XLA Ops:
  0.6 38.1 %core.1 = (f32[64,128]{1,0:T(8,128)S(1)}, f32[16,768,128]{2,1,0:T(8,128)S(1)}, f32[16,768,128]{2,1,0:T(8,128)S(1)}, bf16[768,48]{1,0:T(8,128)(2,1)S(1)}) custom-call(bf16[3,3,3,128]{3,2,1,0:T(4,128)(2,1)} %w_hbm.1, bf16[16,16,48,128]{3,2,1,0:T(8,128)(2,1)} %bitcast.17, bf16[768,48]{1,0:T(8,128)(2,1)} %bitcast.20, bf16[4,3,4,64]{3,2,1,0:T(4,128)(2,1)} %bitcast.22, ...), custom_call_target="tpu_custom_call" | custom-call | tf_op jit(solution)/shard_map/core/pallas_call | solution.py:721
  38.7 2.7 %final.1 = (bf16[16,16,48,128]{3,2,1,0:T(8,128)(2,1)}, f32[3,3,3,128]{3,2,1,0:T(4,128)}, f32[1,1]{1,0:T(1,128)}, bf16[768,48]{1,0:T(8,128)(2,1)}) custom-call(f32[64,128]{1,0:T(8,128)S(1)} %get-tuple-element.12.s_ref, f32[16,768,128]{2,1,0:T(8,128)S(1)} %get-tuple-element.13.a_ref, f32[16,768,128]{2,1,0:T(8,128)S(1)} %get-tuple-element.14.b_ref, ...), custom_call_target="tpu_custom_call" | custom-call | tf_op jit(solution)/shard_map/final/pallas_call | solution.py:815

commit v6 on v5

--- a/solution.py
+++ b/solution.py
@@ -119,7 +119,7 @@
 
 
 def disc_stage(
-    recv_ref, w2_ref, w3_ref, w4_ref, w4t, t1t, hg, out_ref,
+    recv_ref, w2x, w3_ref, w4_ref, w3t, w4t, t1t, hg, out_ref, w2_ref, between,
     t1, pp, a1, s1, a2, s2, a3, s3, c4, c3, c2, c1,
 ):
     lane = iota((16, 128), 1)
@@ -165,21 +165,26 @@
         a2[m, 1, 6] = zero
         c2[m, 0] = zero
         c2[m, 13] = zero
+    lhs = jnp.concatenate(
+        [
+            jnp.concatenate([a1[2 * m + a, 2 * u + k] for m in range(4) for u in range(6)], 0)
+            for a in range(4)
+            for k in range(3)
+        ],
+        1,
+    )
+    pre = dot(lhs, w2x[...])
     for m in range(4):
-        lhs = jnp.concatenate(
-            [a1[2 * m + a, k : k + 12].reshape(192, 128) for a in range(4) for k in range(2)], 1
-        )
-        pre = dot(lhs, w2_ref[...].reshape(1024, 128))
-        act, slope = silu_pair(pre)
-        s2[m] = slope.reshape(12, 16, 128)
         for c in range(12):
-            v = rows16(act, c)
+            k = (m * 6 + c // 2) * 16
+            act, slope = silu_pair(pre[k : k + 16, c % 2 * 128 : c % 2 * 128 + 128])
+            s2[m, c] = slope
             e, p = (c + 1) % 2, (c + 1) // 2
-            a2[m + 1, e, p] = v.astype(BF16)
+            a2[m + 1, e, p] = act.astype(BF16)
             if m == 3:
-                a2[0, e, p] = down1(v).astype(BF16)
+                a2[0, e, p] = down1(act).astype(BF16)
             if m == 0:
-                a2[5, e, p] = up1(v).astype(BF16)
+                a2[5, e, p] = up1(act).astype(BF16)
     zero = jnp.zeros((16, 256), BF16)
     for k in range(5):
         a3[k, 0] = zero
@@ -233,6 +238,7 @@
         c4[2, c + 2] = v0.astype(BF16)
         c4[3, c + 2] = v1.astype(BF16)
         c4[4, c + 2] = up1(v0).astype(BF16)
+    between()
     acc = None
     for a in range(4):
         lhs = jnp.concatenate(
@@ -255,27 +261,23 @@
         c3[3, c + 1] = up1(v0).astype(BF16)
     for first in (0, 1):
         rows = (1, 3) if first == 0 else (0, 2)
-        for e in range(2):
-            p0 = 1 - e
-            taps = [(a, b) for a in (first, first + 2) for b in (e, e + 2)]
-            lhs = jnp.concatenate(
-                [
-                    jnp.concatenate(
-                        [
-                            c3[(m + 1 - a) // 2 + 1, p0 + 1 - b // 2 : p0 + 7 - b // 2].reshape(96, 256)
-                            for m in rows
-                        ],
-                        0,
-                    )
-                    for a, b in taps
-                ],
-                1,
-            )
-            acc = dot(lhs, jnp.concatenate([w3_ref[a * 4 + b] for a, b in taps], 1), NT)
-            for n, m in enumerate(rows):
-                for p in range(6):
-                    c = 2 * (p0 + p) + e - 1
-                    v = rows16(acc, n * 6 + p) * s2[m, c]
+        lhs = jnp.concatenate(
+            [
+                jnp.concatenate(
+                    [c3[(m + 1 - a) // 2 + 1, off : off + 6].reshape(96, 256) for m in rows], 0
+                )
+                for a in (first, first + 2)
+                for off in range(3)
+            ],
+            1,
+        )
+        rhs = jnp.concatenate([w3t[a].reshape(768, 256) for a in (first, first + 2)], 0)
+        acc = dot(lhs, rhs)
+        for n, m in enumerate(rows):
+            for p in range(6):
+                for e in range(2):
+                    c = 2 * p + 1 - e
+                    v = rows16(acc, n * 6 + p)[:, e * 128 : e * 128 + 128] * s2[m, c]
                     c2[m + 1, c + 1] = v.astype(BF16)
                     if m == 3:
                         c2[0, c + 1] = down1(v).astype(BF16)
@@ -485,36 +487,13 @@
     sums_ref, a_ref, b_ref, back_ref,
     fs, w_ref, t_ref, w1_ref, w2s, w3s, w4s, head_ref, wm, parts, parts16, edges, recv, recvf, nb, wide, want, rec,
     redges, ne, msg, msgf, gan,
-    gg, gts, xsum, clip_buf, row_buf, w4t, t1t, hg,
+    gg, gts, xsum, clip_buf, row_buf, w2x, w3t, w4t, t1t, hg,
     t1, pp, a1, s1, a2, s2, a3, s3, c4, c3, c2, c1,
     fsem, wsem, xsem, gsem, tsem,
 ):
     r = lax.axis_index("row")
     clip = lax.axis_index("clip")
     y, z = r // 4, lax.rem(r, 4)
-    barrier = pltpu.get_barrier_semaphore()
-    for d in range(1, FR):
-        pl.semaphore_signal(
-            barrier, inc=1, device_id={"row": lax.rem(r + d, FR)}, device_id_type=MESH
-        )
-    clips = 8
-    for d in range(1, clips):
-        pl.semaphore_signal(
-            barrier, inc=1, device_id={"clip": lax.rem(clip + d, clips)}, device_id_type=MESH
-        )
-    pairs = [
-        [yy * 4 + lax.rem(z + dz, 4) for dz in dzs for yy in range(2)] for dzs in ((2,), (1, 3))
-    ]
-    ys = lax.rem(y, 2)
-    pairs.append([(1 - ys) * 4 + z, ys * 4 + z])
-    loads = [
-        [
-            pltpu.make_async_copy(f_hbm.at[f], fs.at[f], fsem.at[k])
-            for p in group
-            for f in (p, p + 8)
-        ]
-        for k, group in enumerate(pairs)
-    ]
     weights = [
         pltpu.make_async_copy(a, b, wsem.at[k])
         for k, (a, b) in enumerate(
@@ -525,6 +504,28 @@
         )
     ]
     weights[6].start()
+    start_all(weights[3:6])
+    barrier = pltpu.get_barrier_semaphore()
+    for d in range(1, FR):
+        pl.semaphore_signal(
+            barrier, inc=1, device_id={"row": lax.rem(r + d, FR)}, device_id_type=MESH
+        )
+    clips = 8
+    for d in range(1, clips):
+        pl.semaphore_signal(
+            barrier, inc=1, device_id={"clip": lax.rem(clip + d, clips)}, device_id_type=MESH
+        )
+    pairs = [
+        [yy * 4 + lax.rem(z + dz, 4) for dz in dzs for yy in range(2)] for dzs in ((2,), (1, 3), (0,))
+    ]
+    loads = [
+        [
+            pltpu.make_async_copy(f_hbm.at[f], fs.at[f], fsem.at[k])
+            for p in group
+            for f in (p, p + 8)
+        ]
+        for k, group in enumerate((pairs[0] + pairs[1][0:2], pairs[1][2:4] + pairs[2]))
+    ]
     for group in loads:
         start_all(group)
     weights[6].wait()
@@ -544,20 +545,11 @@
     def pair_features(p):
         return jnp.concatenate([fs[p].reshape(768, 128), fs[p + 8].reshape(768, 128)], 1)
 
-    def send_images(f):
-        pltpu.make_async_remote_copy(
-            src_ref=parts16.at[f],
-            dst_ref=recv.at[r],
-            send_sem=xsem.at[0],
-            recv_sem=xsem.at[1],
-            device_id={"row": f},
-            device_id_type=MESH,
-        ).start()
-
-    for k, group in enumerate(pairs):
-        drain(fs.at[pl.ds(0, 2 * len(group))], fsem.at[k])
-        if k == 2:
-            start_all(weights[0:6])
+    halves = (pairs[0] + pairs[1][0:2], pairs[1][2:4] + pairs[2])
+    for k, group in enumerate(halves):
+        drain(fs.at[pl.ds(0, 8)], fsem.at[k])
+        if k == 1:
+            start_all(weights[0:3])
         for p in group:
             out = dot(pair_features(p), wmb, NT).T
             total = None
@@ -574,15 +566,17 @@
                     if t in (0, 6):
                         parts[f, 21 + t // 2 : 24 + t // 2, :] = tile - rnd(tile)
                 parts16[f] = parts[f].astype(BF16)
-        if k == 0:
-            pl.semaphore_wait(barrier, FR + clips - 2)
-        for p in group:
-            if k < 2 or p is group[0]:
-                send_images(p)
-                send_images(p + 8)
-    send_images(lax.rem(r + 8, FR))
-    own = pltpu.make_async_copy(parts16.at[r], recv.at[r], xsem.at[1])
-    own.start()
+    pl.semaphore_wait(barrier, FR + clips - 2)
+    for peer in row_peers():
+        pltpu.make_async_remote_copy(
+            src_ref=parts16.at[peer],
+            dst_ref=recv.at[r],
+            send_sem=xsem.at[0],
+            recv_sem=xsem.at[1],
+            device_id={"row": peer},
+            device_id_type=MESH,
+        ).start()
+    pltpu.make_async_copy(parts16.at[r], recv.at[r], xsem.at[1]).start()
     flat = parts.reshape(FR * 32, 128)
     for t in (0, 6):
         for o in range(3):
@@ -603,34 +597,49 @@
     msgf[...] = jnp.zeros_like(msgf)
     wait_all(weights[0:4])
     head_term(head_ref, hg)
+    for k in range(4):
+        zero = jnp.zeros((128, 128), BF16)
+        for h in range(2):
+            w2x[k * 384 + h * 128 : k * 384 + h * 128 + 256, h * 128 : h * 128 + 128] = w2s[k]
+        w2x[k * 384 + 256 : k * 384 + 384, 0:128] = zero
+        w2x[k * 384 : k * 384 + 128, 128:256] = zero
+        w3t[k, 2, :, 0:128] = w3s[k * 4].T
+        w3t[k, 1, :, 0:128] = w3s[k * 4 + 2].T
+        w3t[k, 1, :, 128:256] = w3s[k * 4 + 1].T
+        w3t[k, 0, :, 128:256] = w3s[k * 4 + 3].T
+        w3t[k, 2, :, 128:256] = jnp.zeros((256, 128), BF16)
+        w3t[k, 0, :, 0:128] = jnp.zeros((256, 128), BF16)
     for k in range(16):
         w4t[k] = w4s[k].T
     for k in range(6):
         t1t[:, k * 128 : k * 128 + 128] = t1[k * 128 : k * 128 + 128, :].T
-    ends.wait()
-    for o in range(3):
-        for t in range(7):
-            v = flat[pl.ds(3 * t + o, 16, stride=32), :]
-            if t == 0:
-                v = v + jnp.where((lane >= W) & (lane < 2 * W) & (r > 0), nb[0, o], 0.0)
-            if t == 6:
-                v = v + jnp.where((lane < W) & (r < FR - 1), nb[1, o], 0.0)
-            v = SCALE * (v - want[t, o])
-            if t == 0:
-                v = jnp.where(lane >= W, v, 0.0)
-            if t == 6:
-                v = jnp.where(lane < W, v, 0.0)
-            rec[t, o] = v
-            if t in (0, 6):
-                redges[t // 6, o] = v
     rends = EdgeExchange(redges, ne, xsem.at[4], xsem.at[5])
-    rends.start()
+
+    def reconstruction():
+        ends.wait()
+        for o in range(3):
+            for t in range(7):
+                v = flat[pl.ds(3 * t + o, 16, stride=32), :]
+                if t == 0:
+                    v = v + jnp.where((lane >= W) & (lane < 2 * W) & (r > 0), nb[0, o], 0.0)
+                if t == 6:
+                    v = v + jnp.where((lane < W) & (r < FR - 1), nb[1, o], 0.0)
+                v = SCALE * (v - want[t, o])
+                if t == 0:
+                    v = jnp.where(lane >= W, v, 0.0)
+                if t == 6:
+                    v = jnp.where(lane < W, v, 0.0)
+                rec[t, o] = v
+                if t in (0, 6):
+                    redges[t // 6, o] = v
+        rends.start()
+
     drain(recv, xsem.at[1])
     drain(parts16.at[pl.ds(0, FR - 1)], xsem.at[0])
     recvf[...] = recv.reshape(FR * 32, 128)[...].astype(F32)
 
     disc_stage(
-        recvf, w2s, w3s, w4s, w4t, t1t, hg, msgf,
+        recvf, w2x, w3s, w4s, w3t, w4t, t1t, hg, msgf, w2s, reconstruction,
         t1, pp, a1, s1, a2, s2, a3, s3, c4, c3, c2, c1,
     )
     msg.reshape(FR * 32, 128)[...] = msgf[...].astype(BF16)
@@ -757,6 +766,8 @@
             VM((2, 32, 128), F32),
             VM((2, 8, 16, 128), F32),
             VM((2, FR, 16, 128), F32),
+            VM((1536, 256), BF16),
+            VM((4, 3, 256, 256), BF16),
             VM((16, 512, 256), BF16),
             VM((1664, 768), BF16),
             VM((160, 512), F32),
@@ -772,7 +783,7 @@
             VM((4, 8, 16, 256), BF16),
             VM((6, 14, 16, 128), BF16),
             VM((128, 1664), BF16),
-            dma((3,)),
+            dma((2,)),
             dma((7,)),
             dma((8,)),
             dma((FR,)),
@@ -790,28 +801,35 @@
     )
 
 
-def final_body(pixels, s_ref, a_ref, b_ref, g_ref, out_hbm, wg_ref, ad_ref, back_ref, buf, sem):
+def final_body(pixels, s_ref, a_ref, b_ref, g_ref, out_hbm, wg_hbm, ad_hbm, back_hbm, buf, wg, ad, sem, side):
+    sides = [
+        pltpu.make_async_copy(g_ref, back_hbm, side.at[0]),
+        pltpu.make_async_copy(wg, wg_hbm, side.at[1]),
+        pltpu.make_async_copy(ad, ad_hbm, side.at[2]),
+    ]
+    sides[0].start()
     rec, gan = s_ref[0:32], s_ref[32:64]
     adaptive = jnp.sqrt(jnp.sum(rec * rec, keepdims=True)) / (
         jnp.sqrt(jnp.sum(gan * gan, keepdims=True)) + EPS
     )
     scale = jnp.broadcast_to(adaptive, (8, 128))[None]
-    stores = []
-    for f in range(FR):
-        v = a_ref[f].reshape(96, 8, 128) + scale * b_ref[f].reshape(96, 8, 128)
-        buf[f] = v.reshape(16, W, 128).astype(BF16)
-        copy = pltpu.make_async_copy(buf.at[f], out_hbm.at[f], sem.at[f])
-        copy.start()
-        stores.append(copy)
-    ad_ref[...] = adaptive
+    ad[...] = adaptive
+    sides[2].start()
+    for k in range(4):
+        for f in range(4 * k, 4 * k + 4):
+            v = a_ref[f].reshape(96, 8, 128) + scale * b_ref[f].reshape(96, 8, 128)
+            buf[f] = v.reshape(16, W, 128).astype(BF16)
+        pltpu.make_async_copy(buf.at[pl.ds(4 * k, 4)], out_hbm.at[pl.ds(4 * k, 4)], sem).start()
     mixed = (rec + adaptive * gan) / pixels
     for ab in range(9):
-        wg_ref[ab // 3, ab % 3] = mixed[ab * 3 : ab * 3 + 3]
-    back_ref[...] = g_ref[...]
-    wait_all(stores)
+        wg[ab // 3, ab % 3] = mixed[ab * 3 : ab * 3 + 3]
+    sides[1].start()
+    drain(buf, sem)
+    wait_all(sides)
 
 
 def final(sums, a, b, back, pixels):
+    hbm = lambda: pl.BlockSpec(memory_space=pltpu.HBM)
     return pl.pallas_call(
         functools.partial(final_body, pixels),
         out_shape=(
@@ -821,8 +839,14 @@
             jax.ShapeDtypeStruct((768, W), BF16),
         ),
         in_specs=[vspec()] * 4,
-        out_specs=(pl.BlockSpec(memory_space=pltpu.HBM), vspec(), vspec(), vspec()),
-        scratch_shapes=[VM((FR, 16, W, 128), BF16), pltpu.SemaphoreType.DMA((FR,))],
+        out_specs=(hbm(), hbm(), hbm(), hbm()),
+        scratch_shapes=[
+            VM((FR, 16, W, 128), BF16),
+            VM((3, 3, 3, 128), F32),
+            VM((1, 1), F32),
+            pltpu.SemaphoreType.DMA,
+            pltpu.SemaphoreType.DMA((3,)),
+        ],
         compiler_params=pltpu.CompilerParams(vmem_limit_bytes=24 << 20),
         name="final",
     )(sums, a, b, back)

time: 41.7 us -> 40.9 us (0.981)
  Pallas kernels: 40.7 us -> 40 us
    pallas_call x1, Pallas kernels: 2.69 us -> 2.09 us  [final(): pl.pallas_call(functools.partial(final_body, pixels), out_shape=(jax.Shap...]
where the time goes in v6:
time: 40.9 us; the launch traced here: 40.8 us
  Pallas kernels  40 us (98%)
  between operations  0.8 us (2%)
    pallas_call x1, Pallas kernels, core(): pl.pallas_call(core_body, out_shape=(VM((64, 128), F32), VM((FR, 768, 128...  37.9 us
    pallas_call x1, Pallas kernels, final(): pl.pallas_call(functools.partial(final_body, pixels), out_shape=(jax.Shap...  2.09 us

profile of v6, /device:TPU:1, one launch (start us, length us, event | category | flops | bytes accessed | tf_op | source)
XLA Modules:
  0.0 40.8 jit_solution(11765472966682233180)
XLA Ops:
  0.6 37.9 %core.1 = (f32[64,128]{1,0:T(8,128)S(1)}, f32[16,768,128]{2,1,0:T(8,128)S(1)}, f32[16,768,128]{2,1,0:T(8,128)S(1)}, bf16[768,48]{1,0:T(8,128)(2,1)S(1)}) custom-call(bf16[3,3,3,128]{3,2,1,0:T(4,128)(2,1)} %w_hbm.1, bf16[16,16,48,128]{3,2,1,0:T(8,128)(2,1)} %bitcast.17, bf16[768,48]{1,0:T(8,128)(2,1)} %bitcast.20, bf16[4,3,4,64]{3,2,1,0:T(4,128)(2,1)} %bitcast.22, ...), custom_call_target="tpu_custom_call" | custom-call | tf_op jit(solution)/shard_map/core/pallas_call | solution.py:730
  38.5 2.1 %final.1 = (bf16[16,16,48,128]{3,2,1,0:T(8,128)(2,1)}, f32[3,3,3,128]{3,2,1,0:T(4,128)}, f32[1,1]{1,0:T(1,128)}, bf16[768,48]{1,0:T(8,128)(2,1)}) custom-call(f32[64,128]{1,0:T(8,128)S(1)} %get-tuple-element.12.s_ref, f32[16,768,128]{2,1,0:T(8,128)S(1)} %get-tuple-element.13.a_ref, f32[16,768,128]{2,1,0:T(8,128)S(1)} %get-tuple-element.14.b_ref, ...), custom_call_target="tpu_custom_call" | custom-call | tf_op jit(solution)/shard_map/final/pallas_call | solution.py:833

commit v7 on v6

--- a/solution.py
+++ b/solution.py
@@ -119,7 +119,7 @@
 
 
 def disc_stage(
-    recv_ref, w2x, w3_ref, w4_ref, w3t, w4t, t1t, hg, out_ref, w2_ref, between,
+    recv_ref, w2_ref, w3_ref, w4_ref, w3t, w4t, t1t, hg, out_ref, between,
     t1, pp, a1, s1, a2, s2, a3, s3, c4, c3, c2, c1,
 ):
     lane = iota((16, 128), 1)
@@ -165,26 +165,21 @@
         a2[m, 1, 6] = zero
         c2[m, 0] = zero
         c2[m, 13] = zero
-    lhs = jnp.concatenate(
-        [
-            jnp.concatenate([a1[2 * m + a, 2 * u + k] for m in range(4) for u in range(6)], 0)
-            for a in range(4)
-            for k in range(3)
-        ],
-        1,
-    )
-    pre = dot(lhs, w2x[...])
     for m in range(4):
+        lhs = jnp.concatenate(
+            [a1[2 * m + a, k : k + 12].reshape(192, 128) for a in range(4) for k in range(2)], 1
+        )
+        pre = dot(lhs, w2_ref[...].reshape(1024, 128))
+        act, slope = silu_pair(pre)
+        s2[m] = slope.reshape(12, 16, 128)
         for c in range(12):
-            k = (m * 6 + c // 2) * 16
-            act, slope = silu_pair(pre[k : k + 16, c % 2 * 128 : c % 2 * 128 + 128])
-            s2[m, c] = slope
+            v = rows16(act, c)
             e, p = (c + 1) % 2, (c + 1) // 2
-            a2[m + 1, e, p] = act.astype(BF16)
+            a2[m + 1, e, p] = v.astype(BF16)
             if m == 3:
-                a2[0, e, p] = down1(act).astype(BF16)
+                a2[0, e, p] = down1(v).astype(BF16)
             if m == 0:
-                a2[5, e, p] = up1(act).astype(BF16)
+                a2[5, e, p] = up1(v).astype(BF16)
     zero = jnp.zeros((16, 256), BF16)
     for k in range(5):
         a3[k, 0] = zero
@@ -487,7 +482,7 @@
     sums_ref, a_ref, b_ref, back_ref,
     fs, w_ref, t_ref, w1_ref, w2s, w3s, w4s, head_ref, wm, parts, parts16, edges, recv, recvf, nb, wide, want, rec,
     redges, ne, msg, msgf, gan,
-    gg, gts, xsum, clip_buf, row_buf, w2x, w3t, w4t, t1t, hg,
+    gg, gts, xsum, clip_buf, row_buf, w3t, w4t, t1t, hg,
     t1, pp, a1, s1, a2, s2, a3, s3, c4, c3, c2, c1,
     fsem, wsem, xsem, gsem, tsem,
 ):
@@ -548,10 +543,17 @@
     halves = (pairs[0] + pairs[1][0:2], pairs[1][2:4] + pairs[2])
     for k, group in enumerate(halves):
         drain(fs.at[pl.ds(0, 8)], fsem.at[k])
-        if k == 1:
-            start_all(weights[0:3])
-        for p in group:
-            out = dot(pair_features(p), wmb, NT).T
+        if k == 0:
+            weights[0].start()
+            for n in range(8):
+                part = pl.ds(2 * n, 2)
+                pltpu.make_async_copy(w3_hbm.at[part], w3s.at[part], wsem.at[1]).start()
+                pltpu.make_async_copy(w4_hbm.at[part], w4s.at[part], wsem.at[2]).start()
+        for n, p in enumerate(group):
+            if n % 2:
+                out = dot(pair_features(p), wmb, NT).T
+            else:
+                out = dot(wmb, pair_features(p), NT)
             total = None
             for ab in range(9):
                 a, b = ab // 3, ab % 3
@@ -598,11 +600,6 @@
     wait_all(weights[0:4])
     head_term(head_ref, hg)
     for k in range(4):
-        zero = jnp.zeros((128, 128), BF16)
-        for h in range(2):
-            w2x[k * 384 + h * 128 : k * 384 + h * 128 + 256, h * 128 : h * 128 + 128] = w2s[k]
-        w2x[k * 384 + 256 : k * 384 + 384, 0:128] = zero
-        w2x[k * 384 : k * 384 + 128, 128:256] = zero
         w3t[k, 2, :, 0:128] = w3s[k * 4].T
         w3t[k, 1, :, 0:128] = w3s[k * 4 + 2].T
         w3t[k, 1, :, 128:256] = w3s[k * 4 + 1].T
@@ -639,7 +636,7 @@
     recvf[...] = recv.reshape(FR * 32, 128)[...].astype(F32)
 
     disc_stage(
-        recvf, w2x, w3s, w4s, w3t, w4t, t1t, hg, msgf, w2s, reconstruction,
+        recvf, w2s, w3s, w4s, w3t, w4t, t1t, hg, msgf, reconstruction,
         t1, pp, a1, s1, a2, s2, a3, s3, c4, c3, c2, c1,
     )
     msg.reshape(FR * 32, 128)[...] = msgf[...].astype(BF16)
@@ -766,7 +763,6 @@
             VM((2, 32, 128), F32),
             VM((2, 8, 16, 128), F32),
             VM((2, FR, 16, 128), F32),
-            VM((1536, 256), BF16),
             VM((4, 3, 256, 256), BF16),
             VM((16, 512, 256), BF16),
             VM((1664, 768), BF16),

time: 40.9 us -> 40.5 us (level)
  Pallas kernels: 40 us -> 39.5 us
    pallas_call x1, Pallas kernels: 37.9 us -> 37.4 us  [core(): pl.pallas_call(core_body, out_shape=(VM((64, 128), F32), VM((FR, 768, 128...]
where the time goes in v7:
time: 40.5 us; the launch traced here: 40.3 us
  Pallas kernels  39.5 us (98%)
  between operations  0.8 us (2%)
    pallas_call x1, Pallas kernels, core(): pl.pallas_call(core_body, out_shape=(VM((64, 128), F32), VM((FR, 768, 128...  37.4 us
    pallas_call x1, Pallas kernels, final(): pl.pallas_call(functools.partial(final_body, pixels), out_shape=(jax.Shap...  2.09 us

profile of v7, /device:TPU:1, one launch (start us, length us, event | category | flops | bytes accessed | tf_op | source)
XLA Modules:
  0.0 40.3 jit_solution(7735885847721658407)
XLA Ops:
  0.6 37.4 %core.1 = (f32[64,128]{1,0:T(8,128)S(1)}, f32[16,768,128]{2,1,0:T(8,128)S(1)}, f32[16,768,128]{2,1,0:T(8,128)S(1)}, bf16[768,48]{1,0:T(8,128)(2,1)S(1)}) custom-call(bf16[3,3,3,128]{3,2,1,0:T(4,128)(2,1)} %w_hbm.1, bf16[16,16,48,128]{3,2,1,0:T(8,128)(2,1)} %bitcast.17, bf16[768,48]{1,0:T(8,128)(2,1)} %bitcast.20, bf16[4,3,4,64]{3,2,1,0:T(4,128)(2,1)} %bitcast.22, ...), custom_call_target="tpu_custom_call" | custom-call | tf_op jit(solution)/shard_map/core/pallas_call | solution.py:727
  38.1 2.1 %final.1 = (bf16[16,16,48,128]{3,2,1,0:T(8,128)(2,1)}, f32[3,3,3,128]{3,2,1,0:T(4,128)}, f32[1,1]{1,0:T(1,128)}, bf16[768,48]{1,0:T(8,128)(2,1)}) custom-call(f32[64,128]{1,0:T(8,128)S(1)} %get-tuple-element.12.s_ref, f32[16,768,128]{2,1,0:T(8,128)S(1)} %get-tuple-element.13.a_ref, f32[16,768,128]{2,1,0:T(8,128)S(1)} %get-tuple-element.14.b_ref, ...), custom_call_target="tpu_custom_call" | custom-call | tf_op jit(solution)/shard_map/final/pallas_call | solution.py:829

commit v8 on v7

--- a/solution.py
+++ b/solution.py
@@ -568,16 +568,18 @@
                     if t in (0, 6):
                         parts[f, 21 + t // 2 : 24 + t // 2, :] = tile - rnd(tile)
                 parts16[f] = parts[f].astype(BF16)
-    pl.semaphore_wait(barrier, FR + clips - 2)
-    for peer in row_peers():
-        pltpu.make_async_remote_copy(
-            src_ref=parts16.at[peer],
-            dst_ref=recv.at[r],
-            send_sem=xsem.at[0],
-            recv_sem=xsem.at[1],
-            device_id={"row": peer},
-            device_id_type=MESH,
-        ).start()
+        if k == 0:
+            pl.semaphore_wait(barrier, FR + clips - 2)
+        for peer, (_, dz) in zip(row_peers(), ROW_OFFSETS):
+            if (dz in (1, 2)) == (k == 0):
+                pltpu.make_async_remote_copy(
+                    src_ref=parts16.at[peer],
+                    dst_ref=recv.at[r],
+                    send_sem=xsem.at[0],
+                    recv_sem=xsem.at[1],
+                    device_id={"row": peer},
+                    device_id_type=MESH,
+                ).start()
     pltpu.make_async_copy(parts16.at[r], recv.at[r], xsem.at[1]).start()
     flat = parts.reshape(FR * 32, 128)
     for t in (0, 6):
@@ -640,16 +642,16 @@
         t1, pp, a1, s1, a2, s2, a3, s3, c4, c3, c2, c1,
     )
     msg.reshape(FR * 32, 128)[...] = msgf[...].astype(BF16)
-    for peer in row_peers():
+    for peer, (_, dz) in zip(row_peers(), ROW_OFFSETS):
         pltpu.make_async_remote_copy(
             src_ref=msg.at[peer],
             dst_ref=gan.at[r],
             send_sem=xsem.at[6],
-            recv_sem=gsem.at[r],
+            recv_sem=gsem.at[hops(dz)],
             device_id={"row": peer},
             device_id_type=MESH,
         ).start()
-    pltpu.make_async_copy(msg.at[r], gan.at[r], gsem.at[r]).start()
+    pltpu.make_async_copy(msg.at[r], gan.at[r], gsem.at[0]).start()
 
     gg[...] = jnp.zeros_like(gg)
     rends.wait()
@@ -688,10 +690,8 @@
 
     low = iota((8, 128), 0) < 4
     acc = None
-    for group in pairs[::-1]:
-        for p in group:
-            for f in (p, p + 8):
-                drain(gan.at[f], gsem.at[f])
+    for k, group in enumerate(pairs[::-1]):
+        drain(gan.at[pl.ds(0, 2 * len(group))], gsem.at[k])
         for p in group:
             va, vb = gan[p].astype(F32), gan[p + 8].astype(F32)
             ua, ub = pltpu.roll(va, 28, 0), pltpu.roll(vb, 4, 0)
@@ -782,7 +782,7 @@
             dma((2,)),
             dma((7,)),
             dma((8,)),
-            dma((FR,)),
+            dma((3,)),
             dma((2, 6)),
         ],
         compiler_params=pltpu.CompilerParams(
@@ -811,11 +811,10 @@
     scale = jnp.broadcast_to(adaptive, (8, 128))[None]
     ad[...] = adaptive
     sides[2].start()
-    for k in range(4):
-        for f in range(4 * k, 4 * k + 4):
-            v = a_ref[f].reshape(96, 8, 128) + scale * b_ref[f].reshape(96, 8, 128)
-            buf[f] = v.reshape(16, W, 128).astype(BF16)
-        pltpu.make_async_copy(buf.at[pl.ds(4 * k, 4)], out_hbm.at[pl.ds(4 * k, 4)], sem).start()
+    for f in range(FR):
+        v = a_ref[f].reshape(96, 8, 128) + scale * b_ref[f].reshape(96, 8, 128)
+        buf[f] = v.reshape(16, W, 128).astype(BF16)
+        pltpu.make_async_copy(buf.at[f], out_hbm.at[f], sem).start()
     mixed = (rec + adaptive * gan) / pixels
     for ab in range(9):
         wg[ab // 3, ab % 3] = mixed[ab * 3 : ab * 3 + 3]

time: 40.5 us -> 39.5 us (0.975)
  Pallas kernels: 39.5 us -> 38.5 us
    pallas_call x1, Pallas kernels: 37.4 us -> 36.6 us  [core(): pl.pallas_call(core_body, out_shape=(VM((64, 128), F32), VM((FR, 768, 128...]
where the time goes in v8:
time: 39.5 us; the launch traced here: 39.3 us
  Pallas kernels  38.5 us (97%)
  between operations  0.8 us (2%)
    pallas_call x1, Pallas kernels, core(): pl.pallas_call(core_body, out_shape=(VM((64, 128), F32), VM((FR, 768, 128...  36.6 us
    pallas_call x1, Pallas kernels, final(): pl.pallas_call(functools.partial(final_body, pixels), out_shape=(jax.Shap...  1.89 us

profile of v8, /device:TPU:1, one launch (start us, length us, event | category | flops | bytes accessed | tf_op | source)
XLA Modules:
  0.0 39.3 jit_solution(325976797336866469)
XLA Ops:
  0.6 36.6 %core.1 = (f32[64,128]{1,0:T(8,128)S(1)}, f32[16,768,128]{2,1,0:T(8,128)S(1)}, f32[16,768,128]{2,1,0:T(8,128)S(1)}, bf16[768,48]{1,0:T(8,128)(2,1)S(1)}) custom-call(bf16[3,3,3,128]{3,2,1,0:T(4,128)(2,1)} %w_hbm.1, bf16[16,16,48,128]{3,2,1,0:T(8,128)(2,1)} %bitcast.17, bf16[768,48]{1,0:T(8,128)(2,1)} %bitcast.20, bf16[4,3,4,64]{3,2,1,0:T(4,128)(2,1)} %bitcast.22, ...), custom_call_target="tpu_custom_call" | custom-call | tf_op jit(solution)/shard_map/core/pallas_call | solution.py:727
  37.3 1.9 %final.1 = (bf16[16,16,48,128]{3,2,1,0:T(8,128)(2,1)}, f32[3,3,3,128]{3,2,1,0:T(4,128)}, f32[1,1]{1,0:T(1,128)}, bf16[768,48]{1,0:T(8,128)(2,1)}) custom-call(f32[64,128]{1,0:T(8,128)S(1)} %get-tuple-element.12.s_ref, f32[16,768,128]{2,1,0:T(8,128)S(1)} %get-tuple-element.13.a_ref, f32[16,768,128]{2,1,0:T(8,128)S(1)} %get-tuple-element.14.b_ref, ...), custom_call_target="tpu_custom_call" | custom-call | tf_op jit(solution)/shard_map/final/pallas_call | solution.py:828

commit v9 on v8

--- a/solution.py
+++ b/solution.py
@@ -540,9 +540,10 @@
     def pair_features(p):
         return jnp.concatenate([fs[p].reshape(768, 128), fs[p + 8].reshape(768, 128)], 1)
 
-    halves = (pairs[0] + pairs[1][0:2], pairs[1][2:4] + pairs[2])
-    for k, group in enumerate(halves):
-        drain(fs.at[pl.ds(0, 8)], fsem.at[k])
+    steps = ((pairs[0] + pairs[1][0:2], (1, 2)), (pairs[1][2:4], (3,)), (pairs[2], (0,)))
+    for k, (group, sent) in enumerate(steps):
+        if k < 2:
+            drain(fs.at[pl.ds(0, 8)], fsem.at[k])
         if k == 0:
             weights[0].start()
             for n in range(8):
@@ -571,7 +572,7 @@
         if k == 0:
             pl.semaphore_wait(barrier, FR + clips - 2)
         for peer, (_, dz) in zip(row_peers(), ROW_OFFSETS):
-            if (dz in (1, 2)) == (k == 0):
+            if dz in sent:
                 pltpu.make_async_remote_copy(
                     src_ref=parts16.at[peer],
                     dst_ref=recv.at[r],

time: 39.5 us -> 39.4 us (level)
  no operation moved by 1% of the time
where the time goes in v9:
time: 39.4 us; the launch traced here: 39.2 us
  Pallas kernels  38.4 us (97%)
  between operations  0.8 us (2%)
    pallas_call x1, Pallas kernels, core(): pl.pallas_call(core_body, out_shape=(VM((64, 128), F32), VM((FR, 768, 128...  36.5 us
    pallas_call x1, Pallas kernels, final(): pl.pallas_call(functools.partial(final_body, pixels), out_shape=(jax.Shap...  1.89 us

profile of v9, /device:TPU:1, one launch (start us, length us, event | category | flops | bytes accessed | tf_op | source)
XLA Modules:
  0.0 39.2 jit_solution(13828526760410280735)
XLA Ops:
  0.6 36.5 %core.1 = (f32[64,128]{1,0:T(8,128)S(1)}, f32[16,768,128]{2,1,0:T(8,128)S(1)}, f32[16,768,128]{2,1,0:T(8,128)S(1)}, bf16[768,48]{1,0:T(8,128)(2,1)S(1)}) custom-call(bf16[3,3,3,128]{3,2,1,0:T(4,128)(2,1)} %w_hbm.1, bf16[16,16,48,128]{3,2,1,0:T(8,128)(2,1)} %bitcast.17, bf16[768,48]{1,0:T(8,128)(2,1)} %bitcast.20, bf16[4,3,4,64]{3,2,1,0:T(4,128)(2,1)} %bitcast.22, ...), custom_call_target="tpu_custom_call" | custom-call | tf_op jit(solution)/shard_map/core/pallas_call | solution.py:728
  37.2 1.9 %final.1 = (bf16[16,16,48,128]{3,2,1,0:T(8,128)(2,1)}, f32[3,3,3,128]{3,2,1,0:T(4,128)}, f32[1,1]{1,0:T(1,128)}, bf16[768,48]{1,0:T(8,128)(2,1)}) custom-call(f32[64,128]{1,0:T(8,128)S(1)} %get-tuple-element.12.s_ref, f32[16,768,128]{2,1,0:T(8,128)S(1)} %get-tuple-element.13.a_ref, f32[16,768,128]{2,1,0:T(8,128)S(1)} %get-tuple-element.14.b_ref, ...), custom_call_target="tpu_custom_call" | custom-call | tf_op jit(solution)/shard_map/final/pallas_call | solution.py:829
